TPU v7x, 32 devices: a whole 2x2x4 slice. The times are simulated.
32 devices in a mesh: grp: 16 (over z, y, core), half: 2 (over x).
Axes of the slice: x: 2, y: 2, z: 4, core: 2. Of those that a mesh axis runs over, the one named last changes fastest.
Arguments:
- field: bfloat16 [16, 2, 1024, 512], P('grp', 'half'), may hold values from -6 to 6
- source_one: bfloat16 [16, 2, 4, 256, 256], P('grp', 'half'), may hold values from -0.375 to 0.375
- sections_one: bfloat16 [16, 2, 3, 4, 256, 512], P('grp', 'half'), may hold values from -0.25 to 0.25
- target_one: bfloat16 [16, 2, 4, 256, 256], P('grp', 'half'), may hold values from -0.375 to 0.375
- source_two: bfloat16 [16, 2, 4, 256, 256], P('grp', 'half'), may hold values from -0.375 to 0.375
- sections_two: bfloat16 [16, 2, 3, 4, 256, 512], P('grp', 'half'), may hold values from -0.25 to 0.25
- target_two: bfloat16 [16, 2, 4, 256, 256], P('grp', 'half'), may hold values from -0.375 to 0.375
- pairing: int32 [2, 3, 16, 2, 4], P(None, None, 'grp', 'half'), may hold values from 0 to 3, each once within a row
Outputs:
- scattered: bfloat16 [16, 2, 1024, 512], P('grp', 'half')
Inputs may be any that keep to these rules, and one draw needn't show every extreme that they name: For every level l, section s, group index g and half h, pairing[l, s, g, h] is a permutation of the 4 nodes.
All inputs are finite; a program needn't handle non-finite values.
Results may differ from a plain program's by a relative error of at most 0.007.
Values may be sent and summed in bfloat16 or wider, within the bound.
No kernel may reach another device: no remote copies, remote signals or barrier semaphores. Data moves between devices by JAX's collectives and lax.ppermute only.
A program may use at most 64 MiB of HBM per device.

v0:
```python
import jax
import jax.numpy as jnp
from jax import lax
from jax.experimental import pallas as pl
from jax.experimental.pallas import tpu as pltpu
from jax.sharding import PartitionSpec as P


CHUNKS = 4
VMEM = pl.BlockSpec(memory_space=pltpu.VMEM)
SMEM = pl.BlockSpec(memory_space=pltpu.SMEM)
ORDER = (
    (2, 0, 2), (2, 0, 1), (1, 0, 3), (2, 0, 3), (1, 0, 1), (1, 1, 3),
    (1, 0, 2), (2, 0, 0), (1, 0, 0), (2, 1, 2), (1, 1, 1), (2, 1, 1),
    (2, 2, 2), (2, 1, 3), (1, 2, 3), (2, 3, 2), (2, 2, 1), (2, 2, 3),
    (2, 1, 0), (1, 1, 2), (1, 3, 3), (1, 1, 0), (2, 3, 3), (2, 2, 0),
    (2, 3, 1), (1, 2, 1), (2, 3, 0), (1, 2, 2), (1, 3, 1), (1, 2, 0),
    (1, 3, 2), (1, 3, 0), (0, 0, 3), (0, 0, 2), (0, 0, 1), (0, 0, 0),
)


def swapped(value, axis, bit):
    return lax.ppermute(value, axis, [(i, i ^ 1 << bit) for i in range(lax.axis_size(axis))])


def dot(a, b):
    return jnp.dot(a, b, preferred_element_type=jnp.float32)


def small(mib=12):
    return pltpu.CompilerParams(vmem_limit_bytes=mib * 1024 * 1024)


def cost(products, shape):
    nodes, leaf, width = shape
    return pl.CostEstimate(
        flops=2 * products * nodes * leaf * leaf * width,
        bytes_accessed=2 * nodes * leaf * (2 * width + products * leaf),
        transcendentals=0,
    )


def source(field, basis, chunk, width):
    nodes, leaf = basis.shape[2:4]

    def kernel(x_ref, s_ref, o_ref):
        for n in range(nodes):
            x = x_ref[0, 0, pl.ds(n * leaf, leaf), pl.ds(chunk * width, width)]
            o_ref[n] = dot(s_ref[0, 0, n], x).astype(o_ref.dtype)

    out = jax.ShapeDtypeStruct((nodes, leaf, width), jnp.bfloat16)
    return pl.pallas_call(
        kernel, out_shape=out, in_specs=[VMEM, VMEM], out_specs=VMEM,
        cost_estimate=cost(1, out.shape), compiler_params=small(),
    )(field, basis)


def advance(own, partner, weights, table, level, section):
    nodes, leaf, _ = own.shape

    def kernel(table_ref, own_ref, partner_ref, w_ref, o_ref):
        for n in range(nodes):
            w = w_ref[0, 0, section, n]
            other = partner_ref[table_ref[level, section, n]]
            total = dot(w[:, :leaf], own_ref[n]) + dot(w[:, leaf:], other)
            o_ref[n] = total.astype(o_ref.dtype)

    return pl.pallas_call(
        kernel, out_shape=jax.ShapeDtypeStruct(own.shape, own.dtype),
        in_specs=[SMEM, VMEM, VMEM, VMEM], out_specs=VMEM,
        cost_estimate=cost(2, own.shape), compiler_params=small(),
    )(table, own, partner, weights)


def target(sibling, distant, one, two, chunk, shape, held):
    nodes, leaf, width = sibling.shape

    def kernel(a_ref, b_ref, one_ref, two_ref, *refs):
        o_ref = refs[-1]
        for n in range(nodes):
            total = dot(one_ref[0, 0, n], a_ref[n]) + dot(two_ref[0, 0, n], b_ref[n])
            o_ref[0, 0, pl.ds(n * leaf, leaf), :] = total.astype(o_ref.dtype)

    args = (sibling, distant, one, two)
    specs = [VMEM] * 4
    alias = {}
    if held is not None:
        args += (held,)
        specs.append(pl.BlockSpec(memory_space=pl.ANY))
        alias = {4: 0}
    return pl.pallas_call(
        kernel, grid=(1,), out_shape=jax.ShapeDtypeStruct(shape, jnp.bfloat16),
        in_specs=specs,
        out_specs=pl.BlockSpec((1, 1, nodes * leaf, width), lambda i: (0, 0, 0, chunk)),
        input_output_aliases=alias,
        cost_estimate=cost(2, sibling.shape), compiler_params=small(),
    )(*args)


def on_device(
    field, source_one, sections_one, target_one, source_two, sections_two, target_two, pairing
):
    width = field.shape[3] // CHUNKS
    top = lax.axis_size("grp").bit_length() - 1
    table = pairing[:, :, 0, 0]
    sources = {1: source_one, 2: source_two}
    sections = {1: sections_one, 2: sections_two}
    last = sections_one.shape[2]
    value, moved = {}, {}
    out = None
    for step in ORDER:
        level, stage, k = step
        if level == 0:
            out = target(moved[1, k], moved[2, k], target_one, target_two, k, field.shape, out)
        elif stage == 0:
            value[level, k] = source(field, sources[level], k, width)
        else:
            value[level, k] = advance(
                value[level, k], moved[level, k], sections[level], table,
                level - 1, stage - 1,
            )
        if level:
            if stage < last:
                axis, bit = "grp", top - level - stage
            else:
                axis, bit = ("half", 0) if level == 1 else ("grp", top - 1)
            moved[level, k] = swapped(value[level, k], axis, bit)
    return out


def solution(mesh):
    placed = (
        P("grp", "half", None, None),
        P("grp", "half", None, None, None),
        P("grp", "half", None, None, None, None),
        P("grp", "half", None, None, None),
        P("grp", "half", None, None, None),
        P("grp", "half", None, None, None, None),
        P("grp", "half", None, None, None),
        P(None, None, "grp", "half", None),
    )
    return jax.shard_map(
        on_device,
        mesh=mesh,
        in_specs=placed,
        out_specs=P("grp", "half", None, None),
        check_vma=False,
    )
```

profile of v0, /device:TPU:0, one launch (start us, length us, event | category | flops | bytes accessed | tf_op | source)
XLA Modules:
  0.0 138.7 jit_solution(8995845713191224375)
XLA Ops:
  0.0 1.2 copy-done.2
  1.2 1.0 copy-done.4
  2.6 4.1 %collective-permute-start.24 = (bf16[4,256,128]{2,1,0:T(8,128)(2,1)S(1)}, bf16[4,256,128]{2,1,0:T(8,128)(2,1)S(1)}, u32[]{:S(2)}, u32[]{:S(2)}) collective-permute-start(bf16[4,256,128]{2,1,0:T(8,128)(2,1)S(1)} %shard_map.106.own_ref), channel_id=1, source_target_pairs={{0,16},{2,18},{4,20},{6,22},{8,24},{10,26},{12,28},{14,30},{16,0},... | collective-permute-start | bytes 786440 | tf_op jit(solution)/shard_map/ppermute | solution.py:23
  7.4 2.0 %collective-permute-start.28 = (bf16[4,256,128]{2,1,0:T(8,128)(2,1)S(1)}, bf16[4,256,128]{2,1,0:T(8,128)(2,1)S(1)}, u32[]{:S(2)}, u32[]{:S(2)}) collective-permute-start(bf16[4,256,128]{2,1,0:T(8,128)(2,1)S(1)} %shard_map.110.own_ref), channel_id=1, source_target_pairs={{0,8},{2,10},{4,12},{6,14},{8,0},{10,2},{12,4},{14,6},{16,24},{18,... | collective-permute-start | bytes 786440 | tf_op jit(solution)/shard_map/ppermute | solution.py:23
  10.1 3.0 %collective-permute-start.8 = (bf16[4,256,128]{2,1,0:T(8,128)(2,1)S(1)}, bf16[4,256,128]{2,1,0:T(8,128)(2,1)S(1)}, u32[]{:S(2)}, u32[]{:S(2)}) collective-permute-start(bf16[4,256,128]{2,1,0:T(8,128)(2,1)S(1)} %shard_map.90.own_ref), channel_id=1, source_target_pairs={{0,16},{2,18},{4,20},{6,22},{8,24},{10,26},{12,28},{14,30},{16,0},... | collective-permute-start | bytes 786440 | tf_op jit(solution)/shard_map/ppermute | solution.py:23
  13.7 11.5 %collective-permute-done.24.partner_ref = bf16[4,256,128]{2,1,0:T(8,128)(2,1)S(1)} collective-permute-done((bf16[4,256,128]{2,1,0:T(8,128)(2,1)S(1)}, bf16[4,256,128]{2,1,0:T(8,128)(2,1)S(1)}, u32[]{:S(2)}, u32[]{:S(2)}) %collective-permute-start.24) | collective-permute-done | bytes 262176 | tf_op jit(solution)/shard_map/ppermute | solution.py:23
  25.2 6.4 %collective-permute-done.16.partner_ref = bf16[4,256,128]{2,1,0:T(8,128)(2,1)S(1)} collective-permute-done((bf16[4,256,128]{2,1,0:T(8,128)(2,1)S(1)}, bf16[4,256,128]{2,1,0:T(8,128)(2,1)S(1)}, u32[]{:S(2)}, u32[]{:S(2)}) %collective-permute-start.16) | collective-permute-done | bytes 262176 | tf_op jit(solution)/shard_map/ppermute | solution.py:23
  32.0 1.0 shard_map.107.own_ref
  33.0 1.0 shard_map.99.own_ref
  34.0 3.7 %collective-permute-start = (bf16[4,256,128]{2,1,0:T(8,128)(2,1)S(1)}, bf16[4,256,128]{2,1,0:T(8,128)(2,1)S(1)}, u32[]{:S(2)}, u32[]{:S(2)}) collective-permute-start(bf16[4,256,128]{2,1,0:T(8,128)(2,1)S(1)} %shard_map.82.own_ref), channel_id=1, source_target_pairs={{0,16},{2,18},{4,20},{6,22},{8,24},{10,26},{12,28},{14,30},{16,0},... | collective-permute-start | bytes 786440 | tf_op jit(solution)/shard_map/ppermute | solution.py:23
  37.7 1.0 shard_map.111.own_ref
  38.8 3.3 %collective-permute-done.8.partner_ref = bf16[4,256,128]{2,1,0:T(8,128)(2,1)S(1)} collective-permute-done((bf16[4,256,128]{2,1,0:T(8,128)(2,1)S(1)}, bf16[4,256,128]{2,1,0:T(8,128)(2,1)S(1)}, u32[]{:S(2)}, u32[]{:S(2)}) %collective-permute-start.8) | collective-permute-done | bytes 262176 | tf_op jit(solution)/shard_map/ppermute | solution.py:23
  42.1 1.8 %collective-permute-start.29 = (bf16[4,256,128]{2,1,0:T(8,128)(2,1)S(1)}, bf16[4,256,128]{2,1,0:T(8,128)(2,1)S(1)}, u32[]{:S(2)}, u32[]{:S(2)}) collective-permute-start(bf16[4,256,128]{2,1,0:T(8,128)(2,1)S(1)} %shard_map.111.own_ref), channel_id=1, source_target_pairs={{0,4},{2,6},{4,0},{6,2},{8,12},{10,14},{12,8},{14,10},{16,20},{18,... | collective-permute-start | bytes 786440 | tf_op jit(solution)/shard_map/ppermute | solution.py:23
  43.9 1.0 shard_map.103.own_ref
  44.9 3.7 %collective-permute-done.12.partner_ref = bf16[4,256,128]{2,1,0:T(8,128)(2,1)S(1)} collective-permute-done((bf16[4,256,128]{2,1,0:T(8,128)(2,1)S(1)}, bf16[4,256,128]{2,1,0:T(8,128)(2,1)S(1)}, u32[]{:S(2)}, u32[]{:S(2)}) %collective-permute-start.12) | collective-permute-done | bytes 262176 | tf_op jit(solution)/shard_map/ppermute | solution.py:23
  48.7 5.6 %collective-permute-done.4.partner_ref = bf16[4,256,128]{2,1,0:T(8,128)(2,1)S(1)} collective-permute-done((bf16[4,256,128]{2,1,0:T(8,128)(2,1)S(1)}, bf16[4,256,128]{2,1,0:T(8,128)(2,1)S(1)}, u32[]{:S(2)}, u32[]{:S(2)}) %collective-permute-start.4) | collective-permute-done | bytes 262176 | tf_op jit(solution)/shard_map/ppermute | solution.py:23
  54.3 1.6 %collective-permute-start.21 = (bf16[4,256,128]{2,1,0:T(8,128)(2,1)S(1)}, bf16[4,256,128]{2,1,0:T(8,128)(2,1)S(1)}, u32[]{:S(2)}, u32[]{:S(2)}) collective-permute-start(bf16[4,256,128]{2,1,0:T(8,128)(2,1)S(1)} %shard_map.103.own_ref), channel_id=1, source_target_pairs={{0,4},{2,6},{4,0},{6,2},{8,12},{10,14},{12,8},{14,10},{16,20},{18,... | collective-permute-start | bytes 786440 | tf_op jit(solution)/shard_map/ppermute | solution.py:23
  55.9 1.0 shard_map.91.own_ref
  58.0 1.0 shard_map.87.own_ref
  59.1 1.0 shard_map.83.own_ref
  60.1 1.4 %collective-permute-start.13 = (bf16[4,256,128]{2,1,0:T(8,128)(2,1)S(1)}, bf16[4,256,128]{2,1,0:T(8,128)(2,1)S(1)}, u32[]{:S(2)}, u32[]{:S(2)}) collective-permute-start(bf16[4,256,128]{2,1,0:T(8,128)(2,1)S(1)} %shard_map.95.own_ref), channel_id=1, source_target_pairs={{0,4},{2,6},{4,0},{6,2},{8,12},{10,14},{12,8},{14,10},{16,20},{18,... | collective-permute-start | bytes 786440 | tf_op jit(solution)/shard_map/ppermute | solution.py:23
  62.2 1.0 shard_map.108.own_ref
  63.2 2.3 %collective-permute-done.17.partner_ref = bf16[4,256,128]{2,1,0:T(8,128)(2,1)S(1)} collective-permute-done((bf16[4,256,128]{2,1,0:T(8,128)(2,1)S(1)}, bf16[4,256,128]{2,1,0:T(8,128)(2,1)S(1)}, u32[]{:S(2)}, u32[]{:S(2)}) %collective-permute-start.17) | collective-permute-done | bytes 262176 | tf_op jit(solution)/shard_map/ppermute | solution.py:23
  66.5 1.5 %collective-permute-start.26 = (bf16[4,256,128]{2,1,0:T(8,128)(2,1)S(1)}, bf16[4,256,128]{2,1,0:T(8,128)(2,1)S(1)}, u32[]{:S(2)}, u32[]{:S(2)}) collective-permute-start(bf16[4,256,128]{2,1,0:T(8,128)(2,1)S(1)} %shard_map.108.own_ref), channel_id=1, source_target_pairs={{0,4},{2,6},{4,0},{6,2},{8,12},{10,14},{12,8},{14,10},{16,20},{18,... | collective-permute-start | bytes 786440 | tf_op jit(solution)/shard_map/ppermute | solution.py:23
  68.0 1.0 shard_map.112.own_ref
  69.1 1.0 shard_map.100.own_ref
  70.1 1.0 shard_map.104.own_ref
  72.2 1.6 %collective-permute-start.18 = (bf16[4,256,128]{2,1,0:T(8,128)(2,1)S(1)}, bf16[4,256,128]{2,1,0:T(8,128)(2,1)S(1)}, u32[]{:S(2)}, u32[]{:S(2)}) collective-permute-start(bf16[4,256,128]{2,1,0:T(8,128)(2,1)S(1)} %shard_map.100.own_ref), channel_id=1, source_target_pairs={{0,4},{2,6},{4,0},{6,2},{8,12},{10,14},{12,8},{14,10},{16,20},{18,... | collective-permute-start | bytes 786440 | tf_op jit(solution)/shard_map/ppermute | solution.py:23
  75.8 1.6 %collective-permute-start.10 = (bf16[4,256,128]{2,1,0:T(8,128)(2,1)S(1)}, bf16[4,256,128]{2,1,0:T(8,128)(2,1)S(1)}, u32[]{:S(2)}, u32[]{:S(2)}) collective-permute-start(bf16[4,256,128]{2,1,0:T(8,128)(2,1)S(1)} %shard_map.92.own_ref), channel_id=1, source_target_pairs={{0,4},{2,6},{4,0},{6,2},{8,12},{10,14},{12,8},{14,10},{16,20},{18,... | collective-permute-start | bytes 786440 | tf_op jit(solution)/shard_map/ppermute | solution.py:23
  77.4 2.4 %collective-permute-done.26.partner_ref = bf16[4,256,128]{2,1,0:T(8,128)(2,1)S(1)} collective-permute-done((bf16[4,256,128]{2,1,0:T(8,128)(2,1)S(1)}, bf16[4,256,128]{2,1,0:T(8,128)(2,1)S(1)}, u32[]{:S(2)}, u32[]{:S(2)}) %collective-permute-start.26) | collective-permute-done | bytes 262176 | tf_op jit(solution)/shard_map/ppermute | solution.py:23
  80.8 1.0 shard_map.84.own_ref
  81.8 1.0 shard_map.109
  85.4 1.6 %collective-permute-start.2 = (bf16[4,256,128]{2,1,0:T(8,128)(2,1)S(1)}, bf16[4,256,128]{2,1,0:T(8,128)(2,1)S(1)}, u32[]{:S(2)}, u32[]{:S(2)}) collective-permute-start(bf16[4,256,128]{2,1,0:T(8,128)(2,1)S(1)} %shard_map.84.own_ref), channel_id=1, source_target_pairs={{0,4},{2,6},{4,0},{6,2},{8,12},{10,14},{12,8},{14,10},{16,20},{18,... | collective-permute-start | bytes 786440 | tf_op jit(solution)/shard_map/ppermute | solution.py:23
  87.0 1.5 %collective-permute-start.27 = (bf16[4,256,128]{2,1,0:T(8,128)(2,1)S(1)}, bf16[4,256,128]{2,1,0:T(8,128)(2,1)S(1)}, u32[]{:S(2)}, u32[]{:S(2)}) collective-permute-start(bf16[4,256,128]{2,1,0:T(8,128)(2,1)S(1)} %shard_map.109), channel_id=1, source_target_pairs={{0,1},{1,0},{2,3},{3,2},{4,5},{5,4},{6,7},{7,6},{8,9},{9,8},{10,11... | collective-permute-start | bytes 786440 | tf_op jit(solution)/shard_map/ppermute | solution.py:23
  88.5 1.0 shard_map.101
  90.5 3.7 %collective-permute-start.31 = (bf16[4,256,128]{2,1,0:T(8,128)(2,1)S(1)}, bf16[4,256,128]{2,1,0:T(8,128)(2,1)S(1)}, u32[]{:S(2)}, u32[]{:S(2)}) collective-permute-start(bf16[4,256,128]{2,1,0:T(8,128)(2,1)S(1)} %shard_map.113), channel_id=1, source_target_pairs={{0,16},{2,18},{4,20},{6,22},{8,24},{10,26},{12,28},{14,30},{16,0},... | collective-permute-start | bytes 786440 | tf_op jit(solution)/shard_map/ppermute | solution.py:23
  94.2 1.5 %collective-permute-start.19 = (bf16[4,256,128]{2,1,0:T(8,128)(2,1)S(1)}, bf16[4,256,128]{2,1,0:T(8,128)(2,1)S(1)}, u32[]{:S(2)}, u32[]{:S(2)}) collective-permute-start(bf16[4,256,128]{2,1,0:T(8,128)(2,1)S(1)} %shard_map.101), channel_id=1, source_target_pairs={{0,1},{1,0},{2,3},{3,2},{4,5},{5,4},{6,7},{7,6},{8,9},{9,8},{10,11... | collective-permute-start | bytes 786440 | tf_op jit(solution)/shard_map/ppermute | solution.py:23
  96.7 1.0 shard_map.93
  97.7 1.0 shard_map.97
  100.5 2.9 %collective-permute-start.15 = (bf16[4,256,128]{2,1,0:T(8,128)(2,1)S(1)}, bf16[4,256,128]{2,1,0:T(8,128)(2,1)S(1)}, u32[]{:S(2)}, u32[]{:S(2)}) collective-permute-start(bf16[4,256,128]{2,1,0:T(8,128)(2,1)S(1)} %shard_map.97), channel_id=1, source_target_pairs={{0,16},{2,18},{4,20},{6,22},{8,24},{10,26},{12,28},{14,30},{16,0},... | collective-permute-start | bytes 786440 | tf_op jit(solution)/shard_map/ppermute | solution.py:23
  104.4 12.5 %collective-permute-done.31.b_ref = bf16[4,256,128]{2,1,0:T(8,128)(2,1)S(1)} collective-permute-done((bf16[4,256,128]{2,1,0:T(8,128)(2,1)S(1)}, bf16[4,256,128]{2,1,0:T(8,128)(2,1)S(1)}, u32[]{:S(2)}, u32[]{:S(2)}) %collective-permute-start.31) | collective-permute-done | bytes 262176 | tf_op jit(solution)/shard_map/ppermute | solution.py:23
  117.4 1.1 shard_map.114.refs_0_
  118.6 9.5 %collective-permute-done.23.b_ref = bf16[4,256,128]{2,1,0:T(8,128)(2,1)S(1)} collective-permute-done((bf16[4,256,128]{2,1,0:T(8,128)(2,1)S(1)}, bf16[4,256,128]{2,1,0:T(8,128)(2,1)S(1)}, u32[]{:S(2)}, u32[]{:S(2)}) %collective-permute-start.23) | collective-permute-done | bytes 262176 | tf_op jit(solution)/shard_map/ppermute | solution.py:23
  128.1 1.1 shard_map.115.refs_0_
  129.3 4.5 %collective-permute-done.15.b_ref = bf16[4,256,128]{2,1,0:T(8,128)(2,1)S(1)} collective-permute-done((bf16[4,256,128]{2,1,0:T(8,128)(2,1)S(1)}, bf16[4,256,128]{2,1,0:T(8,128)(2,1)S(1)}, u32[]{:S(2)}, u32[]{:S(2)}) %collective-permute-start.15) | collective-permute-done | bytes 262176 | tf_op jit(solution)/shard_map/ppermute | solution.py:23
  133.7 1.1 shard_map.116.refs_0_
  134.9 2.7 %collective-permute-done.7.b_ref = bf16[4,256,128]{2,1,0:T(8,128)(2,1)S(1)} collective-permute-done((bf16[4,256,128]{2,1,0:T(8,128)(2,1)S(1)}, bf16[4,256,128]{2,1,0:T(8,128)(2,1)S(1)}, u32[]{:S(2)}, u32[]{:S(2)}) %collective-permute-start.7) | collective-permute-done | bytes 262176 | tf_op jit(solution)/shard_map/ppermute | solution.py:23
  137.6 1.1 shard_map.117
  (70 shorter events, 17.3 us)
Async XLA Ops:
  0.0 1.2 copy-start.2
  1.2 1.0 copy-start.4
  2.3 4.8 %copy-start.3 = (bf16[1,1,4,256,256]{4,3,2,1,0:T(8,128)(2,1)S(1)}, bf16[1,1,4,256,256]{4,3,2,1,0:T(8,128)(2,1)}, u32[]{:S(2)}) copy-start(bf16[1,1,4,256,256]{4,3,2,1,0:T(8,128)(2,1)} %s_ref.15) | copy-start | bytes 1572868
  2.6 22.6 %collective-permute-start.24 = (bf16[4,256,128]{2,1,0:T(8,128)(2,1)S(1)}, bf16[4,256,128]{2,1,0:T(8,128)(2,1)S(1)}, u32[]{:S(2)}, u32[]{:S(2)}) collective-permute-start(bf16[4,256,128]{2,1,0:T(8,128)(2,1)S(1)} %shard_map.106.own_ref), channel_id=1, source_target_pairs={{0,16},{2,18},{4,20},{6,22},{8,24},{10,26},{12,28},{14,30},{16,0},... | collective-permute-start | bytes 786440 | tf_op jit(solution)/shard_map/ppermute | solution.py:23
  7.0 24.6 %collective-permute-start.16 = (bf16[4,256,128]{2,1,0:T(8,128)(2,1)S(1)}, bf16[4,256,128]{2,1,0:T(8,128)(2,1)S(1)}, u32[]{:S(2)}, u32[]{:S(2)}) collective-permute-start(bf16[4,256,128]{2,1,0:T(8,128)(2,1)S(1)} %shard_map.98.own_ref), channel_id=1, source_target_pairs={{0,16},{2,18},{4,20},{6,22},{8,24},{10,26},{12,28},{14,30},{16,0},... | collective-permute-start | bytes 786440 | tf_op jit(solution)/shard_map/ppermute | solution.py:23
  7.4 26.7 %collective-permute-start.28 = (bf16[4,256,128]{2,1,0:T(8,128)(2,1)S(1)}, bf16[4,256,128]{2,1,0:T(8,128)(2,1)S(1)}, u32[]{:S(2)}, u32[]{:S(2)}) collective-permute-start(bf16[4,256,128]{2,1,0:T(8,128)(2,1)S(1)} %shard_map.110.own_ref), channel_id=1, source_target_pairs={{0,8},{2,10},{4,12},{6,14},{8,0},{10,2},{12,4},{14,6},{16,24},{18,... | collective-permute-start | bytes 786440 | tf_op jit(solution)/shard_map/ppermute | solution.py:23
  9.6 22.0 %copy-start.7 = (s32[2,3,1,1,4]{4,3,2,1,0:T(1,128)S(1)}, s32[2,3,1,1,4]{4,3,2,1,0:T(1,128)}, u32[]{:S(2)}) copy-start(s32[2,3,1,1,4]{4,3,2,1,0:T(1,128)} %param.15) | copy-start | bytes 292
  9.6 29.1 %collective-permute-start.20 = (bf16[4,256,128]{2,1,0:T(8,128)(2,1)S(1)}, bf16[4,256,128]{2,1,0:T(8,128)(2,1)S(1)}, u32[]{:S(2)}, u32[]{:S(2)}) collective-permute-start(bf16[4,256,128]{2,1,0:T(8,128)(2,1)S(1)} %shard_map.102.own_ref), channel_id=1, source_target_pairs={{0,8},{2,10},{4,12},{6,14},{8,0},{10,2},{12,4},{14,6},{16,24},{18,... | collective-permute-start | bytes 786440 | tf_op jit(solution)/shard_map/ppermute | solution.py:23
  10.1 21.8 %copy-start.1 = (bf16[1,1,3,4,256,512]{5,4,3,2,1,0:T(8,128)(2,1)S(1)}, bf16[1,1,3,4,256,512]{5,4,3,2,1,0:T(8,128)(2,1)}, u32[]{:S(2)}) copy-start(bf16[1,1,3,4,256,512]{5,4,3,2,1,0:T(8,128)(2,1)} %w_ref.44) | copy-start | bytes 9437188
  10.1 32.0 %collective-permute-start.8 = (bf16[4,256,128]{2,1,0:T(8,128)(2,1)S(1)}, bf16[4,256,128]{2,1,0:T(8,128)(2,1)S(1)}, u32[]{:S(2)}, u32[]{:S(2)}) collective-permute-start(bf16[4,256,128]{2,1,0:T(8,128)(2,1)S(1)} %shard_map.90.own_ref), channel_id=1, source_target_pairs={{0,16},{2,18},{4,20},{6,22},{8,24},{10,26},{12,28},{14,30},{16,0},... | collective-permute-start | bytes 786440 | tf_op jit(solution)/shard_map/ppermute | solution.py:23
  25.2 23.5 %collective-permute-start.12 = (bf16[4,256,128]{2,1,0:T(8,128)(2,1)S(1)}, bf16[4,256,128]{2,1,0:T(8,128)(2,1)S(1)}, u32[]{:S(2)}, u32[]{:S(2)}) collective-permute-start(bf16[4,256,128]{2,1,0:T(8,128)(2,1)S(1)} %shard_map.94.own_ref), channel_id=1, source_target_pairs={{0,8},{2,10},{4,12},{6,14},{8,0},{10,2},{12,4},{14,6},{16,24},{18,... | collective-permute-start | bytes 786440 | tf_op jit(solution)/shard_map/ppermute | solution.py:23
  31.6 22.6 %collective-permute-start.4 = (bf16[4,256,128]{2,1,0:T(8,128)(2,1)S(1)}, bf16[4,256,128]{2,1,0:T(8,128)(2,1)S(1)}, u32[]{:S(2)}, u32[]{:S(2)}) collective-permute-start(bf16[4,256,128]{2,1,0:T(8,128)(2,1)S(1)} %shard_map.86.own_ref), channel_id=1, source_target_pairs={{0,8},{2,10},{4,12},{6,14},{8,0},{10,2},{12,4},{14,6},{16,24},{18,... | collective-permute-start | bytes 786440 | tf_op jit(solution)/shard_map/ppermute | solution.py:23
  31.9 5.7 %copy-start = (bf16[1,1,3,4,256,512]{5,4,3,2,1,0:T(8,128)(2,1)S(1)}, bf16[1,1,3,4,256,512]{5,4,3,2,1,0:T(8,128)(2,1)}, u32[]{:S(2)}) copy-start(bf16[1,1,3,4,256,512]{5,4,3,2,1,0:T(8,128)(2,1)} %w_ref.47) | copy-start | bytes 9437188
  34.0 25.0 %collective-permute-start = (bf16[4,256,128]{2,1,0:T(8,128)(2,1)S(1)}, bf16[4,256,128]{2,1,0:T(8,128)(2,1)S(1)}, u32[]{:S(2)}, u32[]{:S(2)}) collective-permute-start(bf16[4,256,128]{2,1,0:T(8,128)(2,1)S(1)} %shard_map.82.own_ref), channel_id=1, source_target_pairs={{0,16},{2,18},{4,20},{6,22},{8,24},{10,26},{12,28},{14,30},{16,0},... | collective-permute-start | bytes 786440 | tf_op jit(solution)/shard_map/ppermute | solution.py:23
  38.7 21.4 %collective-permute-start.25 = (bf16[4,256,128]{2,1,0:T(8,128)(2,1)S(1)}, bf16[4,256,128]{2,1,0:T(8,128)(2,1)S(1)}, u32[]{:S(2)}, u32[]{:S(2)}) collective-permute-start(bf16[4,256,128]{2,1,0:T(8,128)(2,1)S(1)} %shard_map.107.own_ref), channel_id=1, source_target_pairs={{0,8},{2,10},{4,12},{6,14},{8,0},{10,2},{12,4},{14,6},{16,24},{18,... | collective-permute-start | bytes 786440 | tf_op jit(solution)/shard_map/ppermute | solution.py:23
  42.1 19.4 %collective-permute-start.29 = (bf16[4,256,128]{2,1,0:T(8,128)(2,1)S(1)}, bf16[4,256,128]{2,1,0:T(8,128)(2,1)S(1)}, u32[]{:S(2)}, u32[]{:S(2)}) collective-permute-start(bf16[4,256,128]{2,1,0:T(8,128)(2,1)S(1)} %shard_map.111.own_ref), channel_id=1, source_target_pairs={{0,4},{2,6},{4,0},{6,2},{8,12},{10,14},{12,8},{14,10},{16,20},{18,... | collective-permute-start | bytes 786440 | tf_op jit(solution)/shard_map/ppermute | solution.py:23
  48.6 16.9 %collective-permute-start.17 = (bf16[4,256,128]{2,1,0:T(8,128)(2,1)S(1)}, bf16[4,256,128]{2,1,0:T(8,128)(2,1)S(1)}, u32[]{:S(2)}, u32[]{:S(2)}) collective-permute-start(bf16[4,256,128]{2,1,0:T(8,128)(2,1)S(1)} %shard_map.99.own_ref), channel_id=1, source_target_pairs={{0,8},{2,10},{4,12},{6,14},{8,0},{10,2},{12,4},{14,6},{16,24},{18,... | collective-permute-start | bytes 786440 | tf_op jit(solution)/shard_map/ppermute | solution.py:23
  54.3 12.3 %collective-permute-start.21 = (bf16[4,256,128]{2,1,0:T(8,128)(2,1)S(1)}, bf16[4,256,128]{2,1,0:T(8,128)(2,1)S(1)}, u32[]{:S(2)}, u32[]{:S(2)}) collective-permute-start(bf16[4,256,128]{2,1,0:T(8,128)(2,1)S(1)} %shard_map.103.own_ref), channel_id=1, source_target_pairs={{0,4},{2,6},{4,0},{6,2},{8,12},{10,14},{12,8},{14,10},{16,20},{18,... | collective-permute-start | bytes 786440 | tf_op jit(solution)/shard_map/ppermute | solution.py:23
  59.0 12.1 %collective-permute-start.9 = (bf16[4,256,128]{2,1,0:T(8,128)(2,1)S(1)}, bf16[4,256,128]{2,1,0:T(8,128)(2,1)S(1)}, u32[]{:S(2)}, u32[]{:S(2)}) collective-permute-start(bf16[4,256,128]{2,1,0:T(8,128)(2,1)S(1)} %shard_map.91.own_ref), channel_id=1, source_target_pairs={{0,8},{2,10},{4,12},{6,14},{8,0},{10,2},{12,4},{14,6},{16,24},{18,... | collective-permute-start | bytes 786440 | tf_op jit(solution)/shard_map/ppermute | solution.py:23
  60.1 12.1 %collective-permute-start.13 = (bf16[4,256,128]{2,1,0:T(8,128)(2,1)S(1)}, bf16[4,256,128]{2,1,0:T(8,128)(2,1)S(1)}, u32[]{:S(2)}, u32[]{:S(2)}) collective-permute-start(bf16[4,256,128]{2,1,0:T(8,128)(2,1)S(1)} %shard_map.95.own_ref), channel_id=1, source_target_pairs={{0,4},{2,6},{4,0},{6,2},{8,12},{10,14},{12,8},{14,10},{16,20},{18,... | collective-permute-start | bytes 786440 | tf_op jit(solution)/shard_map/ppermute | solution.py:23
  61.5 13.3 %collective-permute-start.5 = (bf16[4,256,128]{2,1,0:T(8,128)(2,1)S(1)}, bf16[4,256,128]{2,1,0:T(8,128)(2,1)S(1)}, u32[]{:S(2)}, u32[]{:S(2)}) collective-permute-start(bf16[4,256,128]{2,1,0:T(8,128)(2,1)S(1)} %shard_map.87.own_ref), channel_id=1, source_target_pairs={{0,4},{2,6},{4,0},{6,2},{8,12},{10,14},{12,8},{14,10},{16,20},{18,... | collective-permute-start | bytes 786440 | tf_op jit(solution)/shard_map/ppermute | solution.py:23
  65.5 10.3 %collective-permute-start.1 = (bf16[4,256,128]{2,1,0:T(8,128)(2,1)S(1)}, bf16[4,256,128]{2,1,0:T(8,128)(2,1)S(1)}, u32[]{:S(2)}, u32[]{:S(2)}) collective-permute-start(bf16[4,256,128]{2,1,0:T(8,128)(2,1)S(1)} %shard_map.83.own_ref), channel_id=1, source_target_pairs={{0,8},{2,10},{4,12},{6,14},{8,0},{10,2},{12,4},{14,6},{16,24},{18,... | collective-permute-start | bytes 786440 | tf_op jit(solution)/shard_map/ppermute | solution.py:23
  66.5 13.3 %collective-permute-start.26 = (bf16[4,256,128]{2,1,0:T(8,128)(2,1)S(1)}, bf16[4,256,128]{2,1,0:T(8,128)(2,1)S(1)}, u32[]{:S(2)}, u32[]{:S(2)}) collective-permute-start(bf16[4,256,128]{2,1,0:T(8,128)(2,1)S(1)} %shard_map.108.own_ref), channel_id=1, source_target_pairs={{0,4},{2,6},{4,0},{6,2},{8,12},{10,14},{12,8},{14,10},{16,20},{18,... | collective-permute-start | bytes 786440 | tf_op jit(solution)/shard_map/ppermute | solution.py:23
  71.1 11.7 %collective-permute-start.30 = (bf16[4,256,128]{2,1,0:T(8,128)(2,1)S(1)}, bf16[4,256,128]{2,1,0:T(8,128)(2,1)S(1)}, u32[]{:S(2)}, u32[]{:S(2)}) collective-permute-start(bf16[4,256,128]{2,1,0:T(8,128)(2,1)S(1)} %shard_map.112.own_ref), channel_id=1, source_target_pairs={{0,2},{2,0},{4,6},{6,4},{8,10},{10,8},{12,14},{14,12},{16,18},{18,... | collective-permute-start | bytes 786440 | tf_op jit(solution)/shard_map/ppermute | solution.py:23
  72.2 13.2 %collective-permute-start.18 = (bf16[4,256,128]{2,1,0:T(8,128)(2,1)S(1)}, bf16[4,256,128]{2,1,0:T(8,128)(2,1)S(1)}, u32[]{:S(2)}, u32[]{:S(2)}) collective-permute-start(bf16[4,256,128]{2,1,0:T(8,128)(2,1)S(1)} %shard_map.100.own_ref), channel_id=1, source_target_pairs={{0,4},{2,6},{4,0},{6,2},{8,12},{10,14},{12,8},{14,10},{16,20},{18,... | collective-permute-start | bytes 786440 | tf_op jit(solution)/shard_map/ppermute | solution.py:23
  74.8 12.2 %collective-permute-start.22 = (bf16[4,256,128]{2,1,0:T(8,128)(2,1)S(1)}, bf16[4,256,128]{2,1,0:T(8,128)(2,1)S(1)}, u32[]{:S(2)}, u32[]{:S(2)}) collective-permute-start(bf16[4,256,128]{2,1,0:T(8,128)(2,1)S(1)} %shard_map.104.own_ref), channel_id=1, source_target_pairs={{0,2},{2,0},{4,6},{6,4},{8,10},{10,8},{12,14},{14,12},{16,18},{18,... | collective-permute-start | bytes 786440 | tf_op jit(solution)/shard_map/ppermute | solution.py:23
  75.8 14.7 %collective-permute-start.10 = (bf16[4,256,128]{2,1,0:T(8,128)(2,1)S(1)}, bf16[4,256,128]{2,1,0:T(8,128)(2,1)S(1)}, u32[]{:S(2)}, u32[]{:S(2)}) collective-permute-start(bf16[4,256,128]{2,1,0:T(8,128)(2,1)S(1)} %shard_map.92.own_ref), channel_id=1, source_target_pairs={{0,4},{2,6},{4,0},{6,2},{8,12},{10,14},{12,8},{14,10},{16,20},{18,... | collective-permute-start | bytes 786440 | tf_op jit(solution)/shard_map/ppermute | solution.py:23
  79.8 14.4 %collective-permute-start.14 = (bf16[4,256,128]{2,1,0:T(8,128)(2,1)S(1)}, bf16[4,256,128]{2,1,0:T(8,128)(2,1)S(1)}, u32[]{:S(2)}, u32[]{:S(2)}) collective-permute-start(bf16[4,256,128]{2,1,0:T(8,128)(2,1)S(1)} %shard_map.96.own_ref), channel_id=1, source_target_pairs={{0,2},{2,0},{4,6},{6,4},{8,10},{10,8},{12,14},{14,12},{16,18},{18,... | collective-permute-start | bytes 786440 | tf_op jit(solution)/shard_map/ppermute | solution.py:23
  82.9 15.9 %collective-permute-start.6 = (bf16[4,256,128]{2,1,0:T(8,128)(2,1)S(1)}, bf16[4,256,128]{2,1,0:T(8,128)(2,1)S(1)}, u32[]{:S(2)}, u32[]{:S(2)}) collective-permute-start(bf16[4,256,128]{2,1,0:T(8,128)(2,1)S(1)} %shard_map.88.own_ref), channel_id=1, source_target_pairs={{0,2},{2,0},{4,6},{6,4},{8,10},{10,8},{12,14},{14,12},{16,18},{18,... | collective-permute-start | bytes 786440 | tf_op jit(solution)/shard_map/ppermute | solution.py:23
  85.4 14.5 %collective-permute-start.2 = (bf16[4,256,128]{2,1,0:T(8,128)(2,1)S(1)}, bf16[4,256,128]{2,1,0:T(8,128)(2,1)S(1)}, u32[]{:S(2)}, u32[]{:S(2)}) collective-permute-start(bf16[4,256,128]{2,1,0:T(8,128)(2,1)S(1)} %shard_map.84.own_ref), channel_id=1, source_target_pairs={{0,4},{2,6},{4,0},{6,2},{8,12},{10,14},{12,8},{14,10},{16,20},{18,... | collective-permute-start | bytes 786440 | tf_op jit(solution)/shard_map/ppermute | solution.py:23
  87.0 13.5 %collective-permute-start.27 = (bf16[4,256,128]{2,1,0:T(8,128)(2,1)S(1)}, bf16[4,256,128]{2,1,0:T(8,128)(2,1)S(1)}, u32[]{:S(2)}, u32[]{:S(2)}) collective-permute-start(bf16[4,256,128]{2,1,0:T(8,128)(2,1)S(1)} %shard_map.109), channel_id=1, source_target_pairs={{0,1},{1,0},{2,3},{3,2},{4,5},{5,4},{6,7},{7,6},{8,9},{9,8},{10,11... | collective-permute-start | bytes 786440 | tf_op jit(solution)/shard_map/ppermute | solution.py:23
  90.5 26.4 %collective-permute-start.31 = (bf16[4,256,128]{2,1,0:T(8,128)(2,1)S(1)}, bf16[4,256,128]{2,1,0:T(8,128)(2,1)S(1)}, u32[]{:S(2)}, u32[]{:S(2)}) collective-permute-start(bf16[4,256,128]{2,1,0:T(8,128)(2,1)S(1)} %shard_map.113), channel_id=1, source_target_pairs={{0,16},{2,18},{4,20},{6,22},{8,24},{10,26},{12,28},{14,30},{16,0},... | collective-permute-start | bytes 786440 | tf_op jit(solution)/shard_map/ppermute | solution.py:23
  94.2 22.7 %collective-permute-start.19 = (bf16[4,256,128]{2,1,0:T(8,128)(2,1)S(1)}, bf16[4,256,128]{2,1,0:T(8,128)(2,1)S(1)}, u32[]{:S(2)}, u32[]{:S(2)}) collective-permute-start(bf16[4,256,128]{2,1,0:T(8,128)(2,1)S(1)} %shard_map.101), channel_id=1, source_target_pairs={{0,1},{1,0},{2,3},{3,2},{4,5},{5,4},{6,7},{7,6},{8,9},{9,8},{10,11... | collective-permute-start | bytes 786440 | tf_op jit(solution)/shard_map/ppermute | solution.py:23
  98.8 18.7 %copy-start.5 = (bf16[1,1,4,256,256]{4,3,2,1,0:T(8,128)(2,1)S(1)}, bf16[1,1,4,256,256]{4,3,2,1,0:T(8,128)(2,1)}, u32[]{:S(2)}) copy-start(bf16[1,1,4,256,256]{4,3,2,1,0:T(8,128)(2,1)} %one_ref.7) | copy-start | bytes 1572868
  98.8 18.7 %copy-start.6 = (bf16[1,1,4,256,256]{4,3,2,1,0:T(8,128)(2,1)S(1)}, bf16[1,1,4,256,256]{4,3,2,1,0:T(8,128)(2,1)}, u32[]{:S(2)}) copy-start(bf16[1,1,4,256,256]{4,3,2,1,0:T(8,128)(2,1)} %two_ref.7) | copy-start | bytes 1572868
  98.8 29.3 %collective-permute-start.23 = (bf16[4,256,128]{2,1,0:T(8,128)(2,1)S(1)}, bf16[4,256,128]{2,1,0:T(8,128)(2,1)S(1)}, u32[]{:S(2)}, u32[]{:S(2)}) collective-permute-start(bf16[4,256,128]{2,1,0:T(8,128)(2,1)S(1)} %shard_map.105), channel_id=1, source_target_pairs={{0,16},{2,18},{4,20},{6,22},{8,24},{10,26},{12,28},{14,30},{16,0},... | collective-permute-start | bytes 786440 | tf_op jit(solution)/shard_map/ppermute | solution.py:23
  99.9 29.4 %collective-permute-start.11 = (bf16[4,256,128]{2,1,0:T(8,128)(2,1)S(1)}, bf16[4,256,128]{2,1,0:T(8,128)(2,1)S(1)}, u32[]{:S(2)}, u32[]{:S(2)}) collective-permute-start(bf16[4,256,128]{2,1,0:T(8,128)(2,1)S(1)} %shard_map.93), channel_id=1, source_target_pairs={{0,1},{1,0},{2,3},{3,2},{4,5},{5,4},{6,7},{7,6},{8,9},{9,8},{10,11... | collective-permute-start | bytes 786440 | tf_op jit(solution)/shard_map/ppermute | solution.py:23
  100.5 33.2 %collective-permute-start.15 = (bf16[4,256,128]{2,1,0:T(8,128)(2,1)S(1)}, bf16[4,256,128]{2,1,0:T(8,128)(2,1)S(1)}, u32[]{:S(2)}, u32[]{:S(2)}) collective-permute-start(bf16[4,256,128]{2,1,0:T(8,128)(2,1)S(1)} %shard_map.97), channel_id=1, source_target_pairs={{0,16},{2,18},{4,20},{6,22},{8,24},{10,26},{12,28},{14,30},{16,0},... | collective-permute-start | bytes 786440 | tf_op jit(solution)/shard_map/ppermute | solution.py:23
  116.9 20.7 %collective-permute-start.7 = (bf16[4,256,128]{2,1,0:T(8,128)(2,1)S(1)}, bf16[4,256,128]{2,1,0:T(8,128)(2,1)S(1)}, u32[]{:S(2)}, u32[]{:S(2)}) collective-permute-start(bf16[4,256,128]{2,1,0:T(8,128)(2,1)S(1)} %shard_map.89), channel_id=1, source_target_pairs={{0,16},{2,18},{4,20},{6,22},{8,24},{10,26},{12,28},{14,30},{16,0},... | collective-permute-start | bytes 786440 | tf_op jit(solution)/shard_map/ppermute | solution.py:23
  116.9 20.7 %collective-permute-start.3 = (bf16[4,256,128]{2,1,0:T(8,128)(2,1)S(1)}, bf16[4,256,128]{2,1,0:T(8,128)(2,1)S(1)}, u32[]{:S(2)}, u32[]{:S(2)}) collective-permute-start(bf16[4,256,128]{2,1,0:T(8,128)(2,1)S(1)} %shard_map.85), channel_id=1, source_target_pairs={{0,1},{1,0},{2,3},{3,2},{4,5},{5,4},{6,7},{7,6},{8,9},{9,8},{10,11... | collective-permute-start | bytes 786440 | tf_op jit(solution)/shard_map/ppermute | solution.py:23
where the time goes:
time: 139 us
  waiting for transfers between devices  67.3 us (48%)
  starting transfers between devices  37.5 us (27%)
  Pallas kernels  31.3 us (23%)
  local copies, waits for them, and re-layouts  2.31 us (2%)
    ppermute x32, waiting for transfers between devices, swapped(): lax.ppermute(value, axis, [(i, i ^ 1 << bit) for i in range(lax.axis_size...  67.3 us
    ppermute x32, starting transfers between devices, swapped(): lax.ppermute(value, axis, [(i, i ^ 1 << bit) for i in range(lax.axis_size...  37.5 us
    pallas_call x24, Pallas kernels, advance(): pl.pallas_call(kernel, out_shape=jax.ShapeDtypeStruct(own.shape, own.dtyp...  24.5 us
    pallas_call x4, Pallas kernels, target(): pl.pallas_call(kernel, grid=(1,), out_shape=jax.ShapeDtypeStruct(shape, j...  4.54 us
  transfers between devices with their start and end apart: 32, of which 14 were waited for; matrix products, arithmetic and copies ran while one was open for 0% of the time, Pallas kernels for 22%

commit v1 on v0

--- a/solution.py
+++ b/solution.py
@@ -9,13 +9,16 @@
 CHUNKS = 4
 VMEM = pl.BlockSpec(memory_space=pltpu.VMEM)
 SMEM = pl.BlockSpec(memory_space=pltpu.SMEM)
+HBM = pl.BlockSpec(memory_space=pltpu.HBM)
 ORDER = (
-    (2, 0, 2), (2, 0, 1), (1, 0, 3), (2, 0, 3), (1, 0, 1), (1, 1, 3),
-    (1, 0, 2), (2, 0, 0), (1, 0, 0), (2, 1, 2), (1, 1, 1), (2, 1, 1),
-    (2, 2, 2), (2, 1, 3), (1, 2, 3), (2, 3, 2), (2, 2, 1), (2, 2, 3),
-    (2, 1, 0), (1, 1, 2), (1, 3, 3), (1, 1, 0), (2, 3, 3), (2, 2, 0),
-    (2, 3, 1), (1, 2, 1), (2, 3, 0), (1, 2, 2), (1, 3, 1), (1, 2, 0),
-    (1, 3, 2), (1, 3, 0), (0, 0, 3), (0, 0, 2), (0, 0, 1), (0, 0, 0),
+    (2, 0, 2), (1, 0, 3), (3, 0, 0), (2, 0, 1), (2, 1, 2), (1, 0, 0),
+    (1, 1, 3), (2, 0, 3), (1, 0, 1), (2, 1, 1), (2, 0, 0), (3, 2, 0),
+    (1, 0, 2), (1, 1, 0), (2, 1, 3), (1, 2, 3), (1, 1, 1), (3, 1, 0),
+    (2, 2, 1), (2, 2, 3), (2, 1, 0), (2, 3, 1), (1, 2, 1), (1, 1, 2),
+    (2, 2, 0), (1, 3, 3), (2, 3, 3), (2, 2, 2), (1, 2, 0), (1, 3, 1),
+    (2, 3, 0), (1, 4, 3), (1, 4, 1), (1, 2, 2), (1, 3, 0), (0, 0, 1),
+    (2, 3, 2), (1, 4, 0), (1, 3, 2), (0, 0, 0), (0, 0, 3), (1, 4, 2),
+    (0, 0, 2),
 )
 
 
@@ -40,6 +43,38 @@
     )
 
 
+def first_source(field, one, two, level, chunk, width):
+    nodes, leaf = one.shape[2:4]
+
+    def kernel(x_ref, one_ref, two_ref, o_ref, x_held, one_held, two_held, sem):
+        rows = field.shape[2] // nodes
+        pieces = []
+        for n in range(nodes):
+            at = pl.ds(n * rows, rows)
+            pieces.append((x_ref.at[0, 0, at], x_held.at[0, 0, at]))
+        pieces.append((one_ref, one_held))
+        pieces.append((two_ref, two_held))
+        copies = [
+            pltpu.make_async_copy(*piece, sem.at[i]) for i, piece in enumerate(pieces)
+        ]
+        for copy in copies:
+            copy.start()
+        for copy in copies:
+            copy.wait()
+        held = one_held if level == 1 else two_held
+        for n in range(nodes):
+            x = x_held[0, 0, pl.ds(n * leaf, leaf), pl.ds(chunk * width, width)]
+            o_ref[n] = dot(held[0, 0, n], x).astype(o_ref.dtype)
+
+    out = jax.ShapeDtypeStruct((nodes, leaf, width), jnp.bfloat16)
+    like = [jax.ShapeDtypeStruct(a.shape, a.dtype) for a in (field, one, two)]
+    return pl.pallas_call(
+        kernel, out_shape=[out, *like], in_specs=[HBM] * 3, out_specs=[VMEM] * 4,
+        scratch_shapes=[pltpu.SemaphoreType.DMA((nodes + 2,))],
+        cost_estimate=cost(1, out.shape), compiler_params=small(),
+    )(*[pltpu.with_memory_space_constraint(a, pltpu.HBM) for a in (field, one, two)])
+
+
 def source(field, basis, chunk, width):
     nodes, leaf = basis.shape[2:4]
 
@@ -55,12 +90,12 @@
     )(field, basis)
 
 
-def advance(own, partner, weights, table, level, section):
+def advance(own, partner, weights, at, table, level, section):
     nodes, leaf, _ = own.shape
 
     def kernel(table_ref, own_ref, partner_ref, w_ref, o_ref):
         for n in range(nodes):
-            w = w_ref[0, 0, section, n]
+            w = w_ref[0, 0, at, n]
             other = partner_ref[table_ref[level, section, n]]
             total = dot(w[:, :leaf], own_ref[n]) + dot(w[:, leaf:], other)
             o_ref[n] = total.astype(o_ref.dtype)
@@ -100,31 +135,55 @@
 def on_device(
     field, source_one, sections_one, target_one, source_two, sections_two, target_two, pairing
 ):
-    width = field.shape[3] // CHUNKS
+    shape = field.shape
+    width = shape[3] // CHUNKS
     top = lax.axis_size("grp").bit_length() - 1
-    table = pairing[:, :, 0, 0]
+    tables = pairing[:, :, 0, 0]
     sources = {1: source_one, 2: source_two}
-    sections = {1: sections_one, 2: sections_two}
-    last = sections_one.shape[2]
     value, moved = {}, {}
     out = None
     for step in ORDER:
         level, stage, k = step
+        axis, bit = "half", 0
+        sent = None
         if level == 0:
-            out = target(moved[1, k], moved[2, k], target_one, target_two, k, field.shape, out)
+            out = target(
+                value[1, k], moved[2, k], target_one, target_two, k, shape, out
+            )
+        elif level == 3:
+            sent = pairing if stage == 2 else sections_one[:, :, stage + 1 : stage + 2]
         elif stage == 0:
-            value[level, k] = source(field, sources[level], k, width)
+            if value:
+                sent = source(field, sources[level], k, width)
+            else:
+                sent, field, sources[1], sources[2] = first_source(
+                    field, source_one, source_two, level, k, width
+                )
+            value[level, k] = sent
+            axis, bit = "grp", top - level
+        elif level == 2:
+            sent = value[2, k] = advance(
+                value[2, k], moved[2, k], sections_two, stage - 1, tables, 1, stage - 1
+            )
+            axis, bit = "grp", top - 2 - stage if stage < 3 else top - 1
+        elif stage == 1:
+            sent = value[1, k] = advance(
+                value[1, k], moved[1, k], sections_one, 0, tables, 0, 0
+            )
+        elif stage == 2:
+            sent = value[1, k] = moved[1, k]
+            axis, bit = "grp", top - 2
         else:
-            value[level, k] = advance(
-                value[level, k], moved[level, k], sections[level], table,
-                level - 1, stage - 1,
-            )
-        if level:
-            if stage < last:
-                axis, bit = "grp", top - level - stage
-            else:
-                axis, bit = ("half", 0) if level == 1 else ("grp", top - 1)
-            moved[level, k] = swapped(value[level, k], axis, bit)
+            value[1, k] = advance(
+                value[1, k], moved[1, k], moved[3, stage - 3], 0,
+                moved[3, 2][:, :, 0, 0], 0, stage - 2,
+            )
+            if stage == 3:
+                sent = value[1, k]
+                axis, bit = "grp", top - 3
+        if sent is not None:
+            result = swapped(sent, axis, bit)
+            moved[(level, stage) if level == 3 else (level, k)] = result
     return out
 
 

time: 139 us -> 186 us (1.34)
  waiting for transfers between devices: 67.3 us -> 107 us
  starting transfers between devices: 37.5 us -> 45.6 us
  local copies, waits for them, and re-layouts: 2.31 us -> 0.18 us
    ppermute x32 -> x35, waiting for transfers between devices: 67.3 us -> 107 us  [swapped(): lax.ppermute(value, axis, [(i, i ^ 1 << bit) for i in range(lax.axis_size...]
    ppermute x32 -> x35, starting transfers between devices: 37.5 us -> 45.6 us  [swapped(): lax.ppermute(value, axis, [(i, i ^ 1 << bit) for i in range(lax.axis_size...]
    unnamed x17 -> x11, local copies, waits for them, and re-layouts: 2.3 us -> 0.03 us
  transfers between devices with their start and end apart: 32 -> 35, of which waited for: 14 -> 20; matrix products, arithmetic and copies ran while one was open for 0% -> 0% of each run, Pallas kernels for 22% -> 16%
where the time goes in v1:
time: 186 us
  waiting for transfers between devices  107 us (58%)
  starting transfers between devices  45.6 us (25%)
  Pallas kernels  32.9 us (18%)
    ppermute x35, waiting for transfers between devices, swapped(): lax.ppermute(value, axis, [(i, i ^ 1 << bit) for i in range(lax.axis_size...  107 us
    ppermute x35, starting transfers between devices, swapped(): lax.ppermute(value, axis, [(i, i ^ 1 << bit) for i in range(lax.axis_size...  45.6 us
    pallas_call x24, Pallas kernels, advance(): pl.pallas_call(kernel, out_shape=jax.ShapeDtypeStruct(own.shape, own.dtyp...  24.5 us
    pallas_call x4, Pallas kernels, target(): pl.pallas_call(kernel, grid=(1,), out_shape=jax.ShapeDtypeStruct(shape, j...  4.51 us
  transfers between devices with their start and end apart: 35, of which 20 were waited for; matrix products, arithmetic and copies ran while one was open for 0% of the time, Pallas kernels for 16%

profile of v1, /device:TPU:0, one launch (start us, length us, event | category | flops | bytes accessed | tf_op | source)
XLA Modules:
  0.0 185.8 jit_solution(12206771645221624550)
XLA Ops:
  0.0 1.9 shard_map.82
  2.2 4.1 %collective-permute-start.1 = (bf16[4,256,128]{2,1,0:T(8,128)(2,1)S(1)}, bf16[4,256,128]{2,1,0:T(8,128)(2,1)S(1)}, u32[]{:S(2)}, u32[]{:S(2)}) collective-permute-start(bf16[4,256,128]{2,1,0:T(8,128)(2,1)S(1)} %shard_map.83.own_ref), channel_id=1, source_target_pairs={{0,16},{2,18},{4,20},{6,22},{8,24},{10,26},{12,28},{14,30},{16,0},... | collective-permute-start | bytes 786440 | tf_op jit(solution)/shard_map/ppermute | solution.py:26
  7.0 3.0 %collective-permute-start.19 = (bf16[4,256,128]{2,1,0:T(8,128)(2,1)S(1)}, bf16[4,256,128]{2,1,0:T(8,128)(2,1)S(1)}, u32[]{:S(2)}, u32[]{:S(2)}) collective-permute-start(bf16[4,256,128]{2,1,0:T(8,128)(2,1)S(1)} %shard_map.98.own_ref), channel_id=1, source_target_pairs={{0,16},{2,18},{4,20},{6,22},{8,24},{10,26},{12,28},{14,30},{16,0},... | collective-permute-start | bytes 786440 | tf_op jit(solution)/shard_map/ppermute | solution.py:26
  10.6 2.0 %collective-permute-start.15 = (bf16[4,256,128]{2,1,0:T(8,128)(2,1)S(1)}, bf16[4,256,128]{2,1,0:T(8,128)(2,1)S(1)}, u32[]{:S(2)}, u32[]{:S(2)}) collective-permute-start(bf16[4,256,128]{2,1,0:T(8,128)(2,1)S(1)} %shard_map.94.own_ref), channel_id=1, source_target_pairs={{0,8},{2,10},{4,12},{6,14},{8,0},{10,2},{12,4},{14,6},{16,24},{18,... | collective-permute-start | bytes 786440 | tf_op jit(solution)/shard_map/ppermute | solution.py:26
  13.2 22.8 %collective-permute-done.1.partner_ref = bf16[4,256,128]{2,1,0:T(8,128)(2,1)S(1)} collective-permute-done((bf16[4,256,128]{2,1,0:T(8,128)(2,1)S(1)}, bf16[4,256,128]{2,1,0:T(8,128)(2,1)S(1)}, u32[]{:S(2)}, u32[]{:S(2)}) %collective-permute-start.1) | collective-permute-done | bytes 262176 | tf_op jit(solution)/shard_map/ppermute | solution.py:26
  35.9 1.8 collective-permute-start
  37.7 1.0 shard_map.84
  38.7 2.8 %collective-permute-done.11.partner_ref = bf16[4,256,128]{2,1,0:T(8,128)(2,1)S(1)} collective-permute-done((bf16[4,256,128]{2,1,0:T(8,128)(2,1)S(1)}, bf16[4,256,128]{2,1,0:T(8,128)(2,1)S(1)}, u32[]{:S(2)}, u32[]{:S(2)}) %collective-permute-start.11) | collective-permute-done | bytes 262176 | tf_op jit(solution)/shard_map/ppermute | solution.py:26
  42.6 2.1 %collective-permute-start.31 = (bf16[4,256,128]{2,1,0:T(8,128)(2,1)S(1)}, bf16[4,256,128]{2,1,0:T(8,128)(2,1)S(1)}, u32[]{:S(2)}, u32[]{:S(2)}) collective-permute-start(bf16[4,256,128]{2,1,0:T(8,128)(2,1)S(1)} %shard_map.110.own_ref), channel_id=1, source_target_pairs={{0,8},{2,10},{4,12},{6,14},{8,0},{10,2},{12,4},{14,6},{16,24},{18,... | collective-permute-start | bytes 786440 | tf_op jit(solution)/shard_map/ppermute | solution.py:26
  44.7 2.6 %collective-permute-done.19.partner_ref = bf16[4,256,128]{2,1,0:T(8,128)(2,1)S(1)} collective-permute-done((bf16[4,256,128]{2,1,0:T(8,128)(2,1)S(1)}, bf16[4,256,128]{2,1,0:T(8,128)(2,1)S(1)}, u32[]{:S(2)}, u32[]{:S(2)}) %collective-permute-start.19) | collective-permute-done | bytes 262176 | tf_op jit(solution)/shard_map/ppermute | solution.py:26
  47.2 4.8 %collective-permute-done.27.partner_ref = bf16[4,256,128]{2,1,0:T(8,128)(2,1)S(1)} collective-permute-done((bf16[4,256,128]{2,1,0:T(8,128)(2,1)S(1)}, bf16[4,256,128]{2,1,0:T(8,128)(2,1)S(1)}, u32[]{:S(2)}, u32[]{:S(2)}) %collective-permute-start.27) | collective-permute-done | bytes 262176 | tf_op jit(solution)/shard_map/ppermute | solution.py:26
  52.0 1.5 collective-permute-start.2
  54.2 3.4 %collective-permute-done.23.partner_ref = bf16[4,256,128]{2,1,0:T(8,128)(2,1)S(1)} collective-permute-done((bf16[4,256,128]{2,1,0:T(8,128)(2,1)S(1)}, bf16[4,256,128]{2,1,0:T(8,128)(2,1)S(1)}, u32[]{:S(2)}, u32[]{:S(2)}) %collective-permute-start.23) | collective-permute-done | bytes 262176 | tf_op jit(solution)/shard_map/ppermute | solution.py:26
  57.6 1.5 collective-permute-start.4
  59.2 1.0 shard_map.99
  60.2 3.0 %collective-permute-done.31.partner_ref = bf16[4,256,128]{2,1,0:T(8,128)(2,1)S(1)} collective-permute-done((bf16[4,256,128]{2,1,0:T(8,128)(2,1)S(1)}, bf16[4,256,128]{2,1,0:T(8,128)(2,1)S(1)}, u32[]{:S(2)}, u32[]{:S(2)}) %collective-permute-start.31) | collective-permute-done | bytes 262176 | tf_op jit(solution)/shard_map/ppermute | solution.py:26
  63.2 1.5 collective-permute-start.20
  64.8 1.0 shard_map.107
  65.8 2.9 %collective-permute-done.7.partner_ref = bf16[4,256,128]{2,1,0:T(8,128)(2,1)S(1)} collective-permute-done((bf16[4,256,128]{2,1,0:T(8,128)(2,1)S(1)}, bf16[4,256,128]{2,1,0:T(8,128)(2,1)S(1)}, u32[]{:S(2)}, u32[]{:S(2)}) %collective-permute-start.7) | collective-permute-done | bytes 262176 | tf_op jit(solution)/shard_map/ppermute | solution.py:26
  68.8 1.5 collective-permute-start.28
  71.3 1.6 collective-permute-start.16
  74.5 20.4 %collective-permute-done.20.own_ref = bf16[4,256,128]{2,1,0:T(8,128)(2,1)S(1)} collective-permute-done((bf16[4,256,128]{2,1,0:T(8,128)(2,1)S(1)}, bf16[4,256,128]{2,1,0:T(8,128)(2,1)S(1)}, u32[]{:S(2)}, u32[]{:S(2)}) %collective-permute-start.20) | collective-permute-done | bytes 262176 | tf_op jit(solution)/shard_map/ppermute | solution.py:26
  94.9 1.5 collective-permute-start.6
  97.5 3.1 %collective-permute-done.28.own_ref = bf16[4,256,128]{2,1,0:T(8,128)(2,1)S(1)} collective-permute-done((bf16[4,256,128]{2,1,0:T(8,128)(2,1)S(1)}, bf16[4,256,128]{2,1,0:T(8,128)(2,1)S(1)}, u32[]{:S(2)}, u32[]{:S(2)}) %collective-permute-start.28) | collective-permute-done | bytes 262176 | tf_op jit(solution)/shard_map/ppermute | solution.py:26
  100.5 1.6 collective-permute-start.32
  104.3 3.8 %collective-permute-done.32.partner_ref = bf16[4,256,128]{2,1,0:T(8,128)(2,1)S(1)} collective-permute-done((bf16[4,256,128]{2,1,0:T(8,128)(2,1)S(1)}, bf16[4,256,128]{2,1,0:T(8,128)(2,1)S(1)}, u32[]{:S(2)}, u32[]{:S(2)}) %collective-permute-start.32) | collective-permute-done | bytes 262176 | tf_op jit(solution)/shard_map/ppermute | solution.py:26
  108.1 2.2 %collective-permute-start.13 = (bf16[4,256,128]{2,1,0:T(8,128)(2,1)S(1)}, bf16[4,256,128]{2,1,0:T(8,128)(2,1)S(1)}, u32[]{:S(2)}, u32[]{:S(2)}) collective-permute-start(bf16[4,256,128]{2,1,0:T(8,128)(2,1)S(1)} %collective-permute-done.12.own_ref), channel_id=1, source_target_pairs={{0,8},{2,10},{4,12},{6,14},{8,0},{10,2},{12,4},{14,6},{16,24},{18,... | collective-permute-start | bytes 786440 | tf_op jit(solution)/shard_map/ppermute | solution.py:26
  110.9 2.3 %collective-permute-start.21 = (bf16[4,256,128]{2,1,0:T(8,128)(2,1)S(1)}, bf16[4,256,128]{2,1,0:T(8,128)(2,1)S(1)}, u32[]{:S(2)}, u32[]{:S(2)}) collective-permute-start(bf16[4,256,128]{2,1,0:T(8,128)(2,1)S(1)} %collective-permute-done.20.own_ref), channel_id=1, source_target_pairs={{0,8},{2,10},{4,12},{6,14},{8,0},{10,2},{12,4},{14,6},{16,24},{18,... | collective-permute-start | bytes 786440 | tf_op jit(solution)/shard_map/ppermute | solution.py:26
  114.3 3.2 %collective-permute-done.13.partner_ref = bf16[4,256,128]{2,1,0:T(8,128)(2,1)S(1)} collective-permute-done((bf16[4,256,128]{2,1,0:T(8,128)(2,1)S(1)}, bf16[4,256,128]{2,1,0:T(8,128)(2,1)S(1)}, u32[]{:S(2)}, u32[]{:S(2)}) %collective-permute-start.13) | collective-permute-done | bytes 262176 | tf_op jit(solution)/shard_map/ppermute | solution.py:26
  118.5 4.1 %collective-permute-done.21.partner_ref = bf16[4,256,128]{2,1,0:T(8,128)(2,1)S(1)} collective-permute-done((bf16[4,256,128]{2,1,0:T(8,128)(2,1)S(1)}, bf16[4,256,128]{2,1,0:T(8,128)(2,1)S(1)}, u32[]{:S(2)}, u32[]{:S(2)}) %collective-permute-start.21) | collective-permute-done | bytes 262176 | tf_op jit(solution)/shard_map/ppermute | solution.py:26
  123.7 1.8 collective-permute-done.29.partner_ref
  128.1 1.6 collective-permute-start.5
  129.7 1.0 shard_map.92.own_ref
  131.3 1.0 shard_map.100.own_ref
  132.4 1.6 collective-permute-start.22
  134.0 1.0 shard_map.108.own_ref
  136.6 3.3 %collective-permute-start.34 = (bf16[4,256,128]{2,1,0:T(8,128)(2,1)S(1)}, bf16[4,256,128]{2,1,0:T(8,128)(2,1)S(1)}, u32[]{:S(2)}, u32[]{:S(2)}) collective-permute-start(bf16[4,256,128]{2,1,0:T(8,128)(2,1)S(1)} %shard_map.113), channel_id=1, source_target_pairs={{0,16},{2,18},{4,20},{6,22},{8,24},{10,26},{12,28},{14,30},{16,0},... | collective-permute-start | bytes 786440 | tf_op jit(solution)/shard_map/ppermute | solution.py:26
  143.0 3.3 %collective-permute-start.18 = (bf16[4,256,128]{2,1,0:T(8,128)(2,1)S(1)}, bf16[4,256,128]{2,1,0:T(8,128)(2,1)S(1)}, u32[]{:S(2)}, u32[]{:S(2)}) collective-permute-start(bf16[4,256,128]{2,1,0:T(8,128)(2,1)S(1)} %shard_map.97), channel_id=1, source_target_pairs={{0,16},{2,18},{4,20},{6,22},{8,24},{10,26},{12,28},{14,30},{16,0},... | collective-permute-start | bytes 786440 | tf_op jit(solution)/shard_map/ppermute | solution.py:26
  147.3 1.3 collective-permute-done.22.partner_ref
  148.6 3.3 %collective-permute-start.10 = (bf16[4,256,128]{2,1,0:T(8,128)(2,1)S(1)}, bf16[4,256,128]{2,1,0:T(8,128)(2,1)S(1)}, u32[]{:S(2)}, u32[]{:S(2)}) collective-permute-start(bf16[4,256,128]{2,1,0:T(8,128)(2,1)S(1)} %shard_map.89), channel_id=1, source_target_pairs={{0,16},{2,18},{4,20},{6,22},{8,24},{10,26},{12,28},{14,30},{16,0},... | collective-permute-start | bytes 786440 | tf_op jit(solution)/shard_map/ppermute | solution.py:26
  156.0 13.1 %collective-permute-done.34.b_ref = bf16[4,256,128]{2,1,0:T(8,128)(2,1)S(1)} collective-permute-done((bf16[4,256,128]{2,1,0:T(8,128)(2,1)S(1)}, bf16[4,256,128]{2,1,0:T(8,128)(2,1)S(1)}, u32[]{:S(2)}, u32[]{:S(2)}) %collective-permute-start.34) | collective-permute-done | bytes 262176 | tf_op jit(solution)/shard_map/ppermute | solution.py:26
  169.1 1.1 shard_map.114.refs_0_
  170.2 4.5 %collective-permute-done.26.b_ref = bf16[4,256,128]{2,1,0:T(8,128)(2,1)S(1)} collective-permute-done((bf16[4,256,128]{2,1,0:T(8,128)(2,1)S(1)}, bf16[4,256,128]{2,1,0:T(8,128)(2,1)S(1)}, u32[]{:S(2)}, u32[]{:S(2)}) %collective-permute-start.26) | collective-permute-done | bytes 262176 | tf_op jit(solution)/shard_map/ppermute | solution.py:26
  174.7 1.1 shard_map.115.refs_0_
  175.8 4.5 %collective-permute-done.18.b_ref = bf16[4,256,128]{2,1,0:T(8,128)(2,1)S(1)} collective-permute-done((bf16[4,256,128]{2,1,0:T(8,128)(2,1)S(1)}, bf16[4,256,128]{2,1,0:T(8,128)(2,1)S(1)}, u32[]{:S(2)}, u32[]{:S(2)}) %collective-permute-start.18) | collective-permute-done | bytes 262176 | tf_op jit(solution)/shard_map/ppermute | solution.py:26
  180.3 1.1 shard_map.116.refs_0_
  181.4 3.2 %collective-permute-done.10.b_ref = bf16[4,256,128]{2,1,0:T(8,128)(2,1)S(1)} collective-permute-done((bf16[4,256,128]{2,1,0:T(8,128)(2,1)S(1)}, bf16[4,256,128]{2,1,0:T(8,128)(2,1)S(1)}, u32[]{:S(2)}, u32[]{:S(2)}) %collective-permute-start.10) | collective-permute-done | bytes 262176 | tf_op jit(solution)/shard_map/ppermute | solution.py:26
  184.7 1.1 shard_map.117
  (73 shorter events, 26.3 us)
Async XLA Ops:
  2.2 33.8 %collective-permute-start.1 = (bf16[4,256,128]{2,1,0:T(8,128)(2,1)S(1)}, bf16[4,256,128]{2,1,0:T(8,128)(2,1)S(1)}, u32[]{:S(2)}, u32[]{:S(2)}) collective-permute-start(bf16[4,256,128]{2,1,0:T(8,128)(2,1)S(1)} %shard_map.83.own_ref), channel_id=1, source_target_pairs={{0,16},{2,18},{4,20},{6,22},{8,24},{10,26},{12,28},{14,30},{16,0},... | collective-permute-start | bytes 786440 | tf_op jit(solution)/shard_map/ppermute | solution.py:26
  6.6 6.0 %copy-start.4 = (s32[2,3,1,1,4]{4,3,2,1,0:T(1,128)S(1)}, s32[2,3,1,1,4]{4,3,2,1,0:T(1,128)}, u32[]{:S(2)}) copy-start(s32[2,3,1,1,4]{4,3,2,1,0:T(1,128)} %param.15) | copy-start | bytes 292
  6.6 34.9 %collective-permute-start.11 = (bf16[4,256,128]{2,1,0:T(8,128)(2,1)S(1)}, bf16[4,256,128]{2,1,0:T(8,128)(2,1)S(1)}, u32[]{:S(2)}, u32[]{:S(2)}) collective-permute-start(bf16[4,256,128]{2,1,0:T(8,128)(2,1)S(1)} %shard_map.90.own_ref), channel_id=1, source_target_pairs={{0,16},{2,18},{4,20},{6,22},{8,24},{10,26},{12,28},{14,30},{16,0},... | collective-permute-start | bytes 786440 | tf_op jit(solution)/shard_map/ppermute | solution.py:26
  7.0 40.3 %collective-permute-start.19 = (bf16[4,256,128]{2,1,0:T(8,128)(2,1)S(1)}, bf16[4,256,128]{2,1,0:T(8,128)(2,1)S(1)}, u32[]{:S(2)}, u32[]{:S(2)}) collective-permute-start(bf16[4,256,128]{2,1,0:T(8,128)(2,1)S(1)} %shard_map.98.own_ref), channel_id=1, source_target_pairs={{0,16},{2,18},{4,20},{6,22},{8,24},{10,26},{12,28},{14,30},{16,0},... | collective-permute-start | bytes 786440 | tf_op jit(solution)/shard_map/ppermute | solution.py:26
  10.2 27.5 %copy-start.1 = (bf16[1,1,3,4,256,512]{5,4,3,2,1,0:T(8,128)(2,1)S(1)}, bf16[1,1,3,4,256,512]{5,4,3,2,1,0:T(8,128)(2,1)}, u32[]{:S(2)}) copy-start(bf16[1,1,3,4,256,512]{5,4,3,2,1,0:T(8,128)(2,1)} %w_ref.28) | copy-start | bytes 9437188
  10.2 41.8 %collective-permute-start.27 = (bf16[4,256,128]{2,1,0:T(8,128)(2,1)S(1)}, bf16[4,256,128]{2,1,0:T(8,128)(2,1)S(1)}, u32[]{:S(2)}, u32[]{:S(2)}) collective-permute-start(bf16[4,256,128]{2,1,0:T(8,128)(2,1)S(1)} %shard_map.106.own_ref), channel_id=1, source_target_pairs={{0,16},{2,18},{4,20},{6,22},{8,24},{10,26},{12,28},{14,30},{16,0},... | collective-permute-start | bytes 786440 | tf_op jit(solution)/shard_map/ppermute | solution.py:26
  10.6 43.0 %collective-permute-start.15 = (bf16[4,256,128]{2,1,0:T(8,128)(2,1)S(1)}, bf16[4,256,128]{2,1,0:T(8,128)(2,1)S(1)}, u32[]{:S(2)}, u32[]{:S(2)}) collective-permute-start(bf16[4,256,128]{2,1,0:T(8,128)(2,1)S(1)} %shard_map.94.own_ref), channel_id=1, source_target_pairs={{0,8},{2,10},{4,12},{6,14},{8,0},{10,2},{12,4},{14,6},{16,24},{18,... | collective-permute-start | bytes 786440 | tf_op jit(solution)/shard_map/ppermute | solution.py:26
  35.9 6.7 %collective-permute-start = (s32[2,3,1,1,4]{4,3,2,1,0:T(1,128)S(1)}, s32[2,3,1,1,4]{4,3,2,1,0:T(1,128)S(1)}, u32[]{:S(2)}, u32[]{:S(2)}) collective-permute-start(s32[2,3,1,1,4]{4,3,2,1,0:T(1,128)S(1)} %copy-done.4), channel_id=1, source_target_pairs={{0,1},{1,0},{2,3},{3,2},{4,5},{5,4},{6,7},{7,6},{8,9},{9,8},{10,11... | collective-permute-start | bytes 296 | tf_op jit(solution)/shard_map/ppermute | solution.py:26
  41.5 16.1 %collective-permute-start.23 = (bf16[4,256,128]{2,1,0:T(8,128)(2,1)S(1)}, bf16[4,256,128]{2,1,0:T(8,128)(2,1)S(1)}, u32[]{:S(2)}, u32[]{:S(2)}) collective-permute-start(bf16[4,256,128]{2,1,0:T(8,128)(2,1)S(1)} %shard_map.102.own_ref), channel_id=1, source_target_pairs={{0,8},{2,10},{4,12},{6,14},{8,0},{10,2},{12,4},{14,6},{16,24},{18,... | collective-permute-start | bytes 786440 | tf_op jit(solution)/shard_map/ppermute | solution.py:26
  42.6 20.7 %collective-permute-start.31 = (bf16[4,256,128]{2,1,0:T(8,128)(2,1)S(1)}, bf16[4,256,128]{2,1,0:T(8,128)(2,1)S(1)}, u32[]{:S(2)}, u32[]{:S(2)}) collective-permute-start(bf16[4,256,128]{2,1,0:T(8,128)(2,1)S(1)} %shard_map.110.own_ref), channel_id=1, source_target_pairs={{0,8},{2,10},{4,12},{6,14},{8,0},{10,2},{12,4},{14,6},{16,24},{18,... | collective-permute-start | bytes 786440 | tf_op jit(solution)/shard_map/ppermute | solution.py:26
  47.2 21.5 %collective-permute-start.7 = (bf16[4,256,128]{2,1,0:T(8,128)(2,1)S(1)}, bf16[4,256,128]{2,1,0:T(8,128)(2,1)S(1)}, u32[]{:S(2)}, u32[]{:S(2)}) collective-permute-start(bf16[4,256,128]{2,1,0:T(8,128)(2,1)S(1)} %get-tuple-element.11.own_ref), channel_id=1, source_target_pairs={{0,8},{2,10},{4,12},{6,14},{8,0},{10,2},{12,4},{14,6},{16,24},{18,... | collective-permute-start | bytes 786440 | tf_op jit(solution)/shard_map/ppermute | solution.py:26
  52.0 19.3 %collective-permute-start.2 = (bf16[4,256,128]{2,1,0:T(8,128)(2,1)S(1)}, bf16[4,256,128]{2,1,0:T(8,128)(2,1)S(1)}, u32[]{:S(2)}, u32[]{:S(2)}) collective-permute-start(bf16[4,256,128]{2,1,0:T(8,128)(2,1)S(1)} %shard_map.84), channel_id=1, source_target_pairs={{0,1},{1,0},{2,3},{3,2},{4,5},{5,4},{6,7},{7,6},{8,9},{9,8},{10,11... | collective-permute-start | bytes 786440 | tf_op jit(solution)/shard_map/ppermute | solution.py:26
  53.6 20.4 %collective-permute-start.12 = (bf16[4,256,128]{2,1,0:T(8,128)(2,1)S(1)}, bf16[4,256,128]{2,1,0:T(8,128)(2,1)S(1)}, u32[]{:S(2)}, u32[]{:S(2)}) collective-permute-start(bf16[4,256,128]{2,1,0:T(8,128)(2,1)S(1)} %shard_map.91), channel_id=1, source_target_pairs={{0,1},{1,0},{2,3},{3,2},{4,5},{5,4},{6,7},{7,6},{8,9},{9,8},{10,11... | collective-permute-start | bytes 786440 | tf_op jit(solution)/shard_map/ppermute | solution.py:26
  57.6 12.7 %copy-start = (bf16[1,1,3,4,256,512]{5,4,3,2,1,0:T(8,128)(2,1)S(1)}, bf16[1,1,3,4,256,512]{5,4,3,2,1,0:T(8,128)(2,1)}, u32[]{:S(2)}) copy-start(bf16[1,1,3,4,256,512]{5,4,3,2,1,0:T(8,128)(2,1)} %w_ref.31) | copy-start | bytes 9437188
  57.6 68.9 %collective-permute-start.4 = (bf16[1,1,1,4,256,512]{5,4,3,2,1,0:T(8,128)(2,1)S(1)}, bf16[1,1,1,4,256,512]{5,4,3,2,1,0:T(8,128)(2,1)S(1)}, u32[]{:S(2)}, u32[]{:S(2)}) collective-permute-start(bf16[1,1,1,4,256,512]{5,4,3,2,1,0:T(8,128)(2,1)S(1)} %get-tuple-element.14), channel_id=1, source_target_pairs={{0,1},{1,0},{2,3},{3,2},{4,5},{5,4},{6,7},{7,6},{8,9},{9,8},{10,11... | collective-permute-start | bytes 3145736 | tf_op jit(solution)/shard_map/ppermute | solution.py:26
  63.2 31.7 %collective-permute-start.20 = (bf16[4,256,128]{2,1,0:T(8,128)(2,1)S(1)}, bf16[4,256,128]{2,1,0:T(8,128)(2,1)S(1)}, u32[]{:S(2)}, u32[]{:S(2)}) collective-permute-start(bf16[4,256,128]{2,1,0:T(8,128)(2,1)S(1)} %shard_map.99), channel_id=1, source_target_pairs={{0,1},{1,0},{2,3},{3,2},{4,5},{5,4},{6,7},{7,6},{8,9},{9,8},{10,11... | collective-permute-start | bytes 786440 | tf_op jit(solution)/shard_map/ppermute | solution.py:26
  68.8 31.7 %collective-permute-start.28 = (bf16[4,256,128]{2,1,0:T(8,128)(2,1)S(1)}, bf16[4,256,128]{2,1,0:T(8,128)(2,1)S(1)}, u32[]{:S(2)}, u32[]{:S(2)}) collective-permute-start(bf16[4,256,128]{2,1,0:T(8,128)(2,1)S(1)} %shard_map.107), channel_id=1, source_target_pairs={{0,1},{1,0},{2,3},{3,2},{4,5},{5,4},{6,7},{7,6},{8,9},{9,8},{10,11... | collective-permute-start | bytes 786440 | tf_op jit(solution)/shard_map/ppermute | solution.py:26
  71.3 31.8 %collective-permute-start.16 = (bf16[4,256,128]{2,1,0:T(8,128)(2,1)S(1)}, bf16[4,256,128]{2,1,0:T(8,128)(2,1)S(1)}, u32[]{:S(2)}, u32[]{:S(2)}) collective-permute-start(bf16[4,256,128]{2,1,0:T(8,128)(2,1)S(1)} %shard_map.95.own_ref), channel_id=1, source_target_pairs={{0,4},{2,6},{4,0},{6,2},{8,12},{10,14},{12,8},{14,10},{16,20},{18,... | collective-permute-start | bytes 786440 | tf_op jit(solution)/shard_map/ppermute | solution.py:26
  74.0 29.7 %collective-permute-start.24 = (bf16[4,256,128]{2,1,0:T(8,128)(2,1)S(1)}, bf16[4,256,128]{2,1,0:T(8,128)(2,1)S(1)}, u32[]{:S(2)}, u32[]{:S(2)}) collective-permute-start(bf16[4,256,128]{2,1,0:T(8,128)(2,1)S(1)} %shard_map.103.own_ref), channel_id=1, source_target_pairs={{0,4},{2,6},{4,0},{6,2},{8,12},{10,14},{12,8},{14,10},{16,20},{18,... | collective-permute-start | bytes 786440 | tf_op jit(solution)/shard_map/ppermute | solution.py:26
  94.9 41.7 %collective-permute-start.6 = (bf16[1,1,1,4,256,512]{5,4,3,2,1,0:T(8,128)(2,1)S(1)}, bf16[1,1,1,4,256,512]{5,4,3,2,1,0:T(8,128)(2,1)S(1)}, u32[]{:S(2)}, u32[]{:S(2)}) collective-permute-start(bf16[1,1,1,4,256,512]{5,4,3,2,1,0:T(8,128)(2,1)S(1)} %get-tuple-element.13), channel_id=1, source_target_pairs={{0,1},{1,0},{2,3},{3,2},{4,5},{5,4},{6,7},{7,6},{8,9},{9,8},{10,11... | collective-permute-start | bytes 3145736 | tf_op jit(solution)/shard_map/ppermute | solution.py:26
  100.5 7.6 %collective-permute-start.32 = (bf16[4,256,128]{2,1,0:T(8,128)(2,1)S(1)}, bf16[4,256,128]{2,1,0:T(8,128)(2,1)S(1)}, u32[]{:S(2)}, u32[]{:S(2)}) collective-permute-start(bf16[4,256,128]{2,1,0:T(8,128)(2,1)S(1)} %shard_map.111.own_ref), channel_id=1, source_target_pairs={{0,4},{2,6},{4,0},{6,2},{8,12},{10,14},{12,8},{14,10},{16,20},{18,... | collective-permute-start | bytes 786440 | tf_op jit(solution)/shard_map/ppermute | solution.py:26
  103.1 7.8 %collective-permute-start.8 = (bf16[4,256,128]{2,1,0:T(8,128)(2,1)S(1)}, bf16[4,256,128]{2,1,0:T(8,128)(2,1)S(1)}, u32[]{:S(2)}, u32[]{:S(2)}) collective-permute-start(bf16[4,256,128]{2,1,0:T(8,128)(2,1)S(1)} %shard_map.87.own_ref), channel_id=1, source_target_pairs={{0,4},{2,6},{4,0},{6,2},{8,12},{10,14},{12,8},{14,10},{16,20},{18,... | collective-permute-start | bytes 786440 | tf_op jit(solution)/shard_map/ppermute | solution.py:26
  103.6 9.6 %collective-permute-start.3 = (bf16[4,256,128]{2,1,0:T(8,128)(2,1)S(1)}, bf16[4,256,128]{2,1,0:T(8,128)(2,1)S(1)}, u32[]{:S(2)}, u32[]{:S(2)}) collective-permute-start(bf16[4,256,128]{2,1,0:T(8,128)(2,1)S(1)} %collective-permute-done.2.own_ref), channel_id=1, source_target_pairs={{0,8},{2,10},{4,12},{6,14},{8,0},{10,2},{12,4},{14,6},{16,24},{18,... | collective-permute-start | bytes 786440 | tf_op jit(solution)/shard_map/ppermute | solution.py:26
  108.1 9.4 %collective-permute-start.13 = (bf16[4,256,128]{2,1,0:T(8,128)(2,1)S(1)}, bf16[4,256,128]{2,1,0:T(8,128)(2,1)S(1)}, u32[]{:S(2)}, u32[]{:S(2)}) collective-permute-start(bf16[4,256,128]{2,1,0:T(8,128)(2,1)S(1)} %collective-permute-done.12.own_ref), channel_id=1, source_target_pairs={{0,8},{2,10},{4,12},{6,14},{8,0},{10,2},{12,4},{14,6},{16,24},{18,... | collective-permute-start | bytes 786440 | tf_op jit(solution)/shard_map/ppermute | solution.py:26
  110.9 11.7 %collective-permute-start.21 = (bf16[4,256,128]{2,1,0:T(8,128)(2,1)S(1)}, bf16[4,256,128]{2,1,0:T(8,128)(2,1)S(1)}, u32[]{:S(2)}, u32[]{:S(2)}) collective-permute-start(bf16[4,256,128]{2,1,0:T(8,128)(2,1)S(1)} %collective-permute-done.20.own_ref), channel_id=1, source_target_pairs={{0,8},{2,10},{4,12},{6,14},{8,0},{10,2},{12,4},{14,6},{16,24},{18,... | collective-permute-start | bytes 786440 | tf_op jit(solution)/shard_map/ppermute | solution.py:26
  113.2 12.2 %collective-permute-start.29 = (bf16[4,256,128]{2,1,0:T(8,128)(2,1)S(1)}, bf16[4,256,128]{2,1,0:T(8,128)(2,1)S(1)}, u32[]{:S(2)}, u32[]{:S(2)}) collective-permute-start(bf16[4,256,128]{2,1,0:T(8,128)(2,1)S(1)} %collective-permute-done.28.own_ref), channel_id=1, source_target_pairs={{0,8},{2,10},{4,12},{6,14},{8,0},{10,2},{12,4},{14,6},{16,24},{18,... | collective-permute-start | bytes 786440 | tf_op jit(solution)/shard_map/ppermute | solution.py:26
  117.5 10.6 %collective-permute-start.17 = (bf16[4,256,128]{2,1,0:T(8,128)(2,1)S(1)}, bf16[4,256,128]{2,1,0:T(8,128)(2,1)S(1)}, u32[]{:S(2)}, u32[]{:S(2)}) collective-permute-start(bf16[4,256,128]{2,1,0:T(8,128)(2,1)S(1)} %shard_map.96.own_ref), channel_id=1, source_target_pairs={{0,2},{2,0},{4,6},{6,4},{8,10},{10,8},{12,14},{14,12},{16,18},{18,... | collective-permute-start | bytes 786440 | tf_op jit(solution)/shard_map/ppermute | solution.py:26
  122.7 8.1 %collective-permute-start.25 = (bf16[4,256,128]{2,1,0:T(8,128)(2,1)S(1)}, bf16[4,256,128]{2,1,0:T(8,128)(2,1)S(1)}, u32[]{:S(2)}, u32[]{:S(2)}) collective-permute-start(bf16[4,256,128]{2,1,0:T(8,128)(2,1)S(1)} %shard_map.104.own_ref), channel_id=1, source_target_pairs={{0,2},{2,0},{4,6},{6,4},{8,10},{10,8},{12,14},{14,12},{16,18},{18,... | collective-permute-start | bytes 786440 | tf_op jit(solution)/shard_map/ppermute | solution.py:26
  125.5 6.9 %collective-permute-start.33 = (bf16[4,256,128]{2,1,0:T(8,128)(2,1)S(1)}, bf16[4,256,128]{2,1,0:T(8,128)(2,1)S(1)}, u32[]{:S(2)}, u32[]{:S(2)}) collective-permute-start(bf16[4,256,128]{2,1,0:T(8,128)(2,1)S(1)} %shard_map.112.own_ref), channel_id=1, source_target_pairs={{0,2},{2,0},{4,6},{6,4},{8,10},{10,8},{12,14},{14,12},{16,18},{18,... | collective-permute-start | bytes 786440 | tf_op jit(solution)/shard_map/ppermute | solution.py:26
  126.5 8.5 %collective-permute-start.9 = (bf16[4,256,128]{2,1,0:T(8,128)(2,1)S(1)}, bf16[4,256,128]{2,1,0:T(8,128)(2,1)S(1)}, u32[]{:S(2)}, u32[]{:S(2)}) collective-permute-start(bf16[4,256,128]{2,1,0:T(8,128)(2,1)S(1)} %shard_map.88.own_ref), channel_id=1, source_target_pairs={{0,2},{2,0},{4,6},{6,4},{8,10},{10,8},{12,14},{14,12},{16,18},{18,... | collective-permute-start | bytes 786440 | tf_op jit(solution)/shard_map/ppermute | solution.py:26
  128.1 12.8 %collective-permute-start.5 = (bf16[4,256,128]{2,1,0:T(8,128)(2,1)S(1)}, bf16[4,256,128]{2,1,0:T(8,128)(2,1)S(1)}, u32[]{:S(2)}, u32[]{:S(2)}) collective-permute-start(bf16[4,256,128]{2,1,0:T(8,128)(2,1)S(1)} %shard_map.85.own_ref), channel_id=1, source_target_pairs={{0,4},{2,6},{4,0},{6,2},{8,12},{10,14},{12,8},{14,10},{16,20},{18,... | collective-permute-start | bytes 786440 | tf_op jit(solution)/shard_map/ppermute | solution.py:26
  130.8 12.2 %collective-permute-start.14 = (bf16[4,256,128]{2,1,0:T(8,128)(2,1)S(1)}, bf16[4,256,128]{2,1,0:T(8,128)(2,1)S(1)}, u32[]{:S(2)}, u32[]{:S(2)}) collective-permute-start(bf16[4,256,128]{2,1,0:T(8,128)(2,1)S(1)} %shard_map.92.own_ref), channel_id=1, source_target_pairs={{0,4},{2,6},{4,0},{6,2},{8,12},{10,14},{12,8},{14,10},{16,20},{18,... | collective-permute-start | bytes 786440 | tf_op jit(solution)/shard_map/ppermute | solution.py:26
  132.4 16.2 %collective-permute-start.22 = (bf16[4,256,128]{2,1,0:T(8,128)(2,1)S(1)}, bf16[4,256,128]{2,1,0:T(8,128)(2,1)S(1)}, u32[]{:S(2)}, u32[]{:S(2)}) collective-permute-start(bf16[4,256,128]{2,1,0:T(8,128)(2,1)S(1)} %shard_map.100.own_ref), channel_id=1, source_target_pairs={{0,4},{2,6},{4,0},{6,2},{8,12},{10,14},{12,8},{14,10},{16,20},{18,... | collective-permute-start | bytes 786440 | tf_op jit(solution)/shard_map/ppermute | solution.py:26
  135.0 20.0 %collective-permute-start.30 = (bf16[4,256,128]{2,1,0:T(8,128)(2,1)S(1)}, bf16[4,256,128]{2,1,0:T(8,128)(2,1)S(1)}, u32[]{:S(2)}, u32[]{:S(2)}) collective-permute-start(bf16[4,256,128]{2,1,0:T(8,128)(2,1)S(1)} %shard_map.108.own_ref), channel_id=1, source_target_pairs={{0,4},{2,6},{4,0},{6,2},{8,12},{10,14},{12,8},{14,10},{16,20},{18,... | collective-permute-start | bytes 786440 | tf_op jit(solution)/shard_map/ppermute | solution.py:26
  136.6 32.5 %collective-permute-start.34 = (bf16[4,256,128]{2,1,0:T(8,128)(2,1)S(1)}, bf16[4,256,128]{2,1,0:T(8,128)(2,1)S(1)}, u32[]{:S(2)}, u32[]{:S(2)}) collective-permute-start(bf16[4,256,128]{2,1,0:T(8,128)(2,1)S(1)} %shard_map.113), channel_id=1, source_target_pairs={{0,16},{2,18},{4,20},{6,22},{8,24},{10,26},{12,28},{14,30},{16,0},... | collective-permute-start | bytes 786440 | tf_op jit(solution)/shard_map/ppermute | solution.py:26
  141.0 33.7 %collective-permute-start.26 = (bf16[4,256,128]{2,1,0:T(8,128)(2,1)S(1)}, bf16[4,256,128]{2,1,0:T(8,128)(2,1)S(1)}, u32[]{:S(2)}, u32[]{:S(2)}) collective-permute-start(bf16[4,256,128]{2,1,0:T(8,128)(2,1)S(1)} %shard_map.105), channel_id=1, source_target_pairs={{0,16},{2,18},{4,20},{6,22},{8,24},{10,26},{12,28},{14,30},{16,0},... | collective-permute-start | bytes 786440 | tf_op jit(solution)/shard_map/ppermute | solution.py:26
  143.0 37.3 %collective-permute-start.18 = (bf16[4,256,128]{2,1,0:T(8,128)(2,1)S(1)}, bf16[4,256,128]{2,1,0:T(8,128)(2,1)S(1)}, u32[]{:S(2)}, u32[]{:S(2)}) collective-permute-start(bf16[4,256,128]{2,1,0:T(8,128)(2,1)S(1)} %shard_map.97), channel_id=1, source_target_pairs={{0,16},{2,18},{4,20},{6,22},{8,24},{10,26},{12,28},{14,30},{16,0},... | collective-permute-start | bytes 786440 | tf_op jit(solution)/shard_map/ppermute | solution.py:26
  148.6 36.1 %collective-permute-start.10 = (bf16[4,256,128]{2,1,0:T(8,128)(2,1)S(1)}, bf16[4,256,128]{2,1,0:T(8,128)(2,1)S(1)}, u32[]{:S(2)}, u32[]{:S(2)}) collective-permute-start(bf16[4,256,128]{2,1,0:T(8,128)(2,1)S(1)} %shard_map.89), channel_id=1, source_target_pairs={{0,16},{2,18},{4,20},{6,22},{8,24},{10,26},{12,28},{14,30},{16,0},... | collective-permute-start | bytes 786440 | tf_op jit(solution)/shard_map/ppermute | solution.py:26
  152.9 16.2 %copy-start.2 = (bf16[1,1,4,256,256]{4,3,2,1,0:T(8,128)(2,1)S(1)}, bf16[1,1,4,256,256]{4,3,2,1,0:T(8,128)(2,1)}, u32[]{:S(2)}) copy-start(bf16[1,1,4,256,256]{4,3,2,1,0:T(8,128)(2,1)} %one_ref.9) | copy-start | bytes 1572868
  152.9 16.2 %copy-start.3 = (bf16[1,1,4,256,256]{4,3,2,1,0:T(8,128)(2,1)S(1)}, bf16[1,1,4,256,256]{4,3,2,1,0:T(8,128)(2,1)}, u32[]{:S(2)}) copy-start(bf16[1,1,4,256,256]{4,3,2,1,0:T(8,128)(2,1)} %two_ref.9) | copy-start | bytes 1572868

commit v2 on v1

--- a/solution.py
+++ b/solution.py
@@ -8,17 +8,16 @@
 
 CHUNKS = 4
 VMEM = pl.BlockSpec(memory_space=pltpu.VMEM)
-SMEM = pl.BlockSpec(memory_space=pltpu.SMEM)
 HBM = pl.BlockSpec(memory_space=pltpu.HBM)
 ORDER = (
-    (2, 0, 2), (1, 0, 3), (3, 0, 0), (2, 0, 1), (2, 1, 2), (1, 0, 0),
-    (1, 1, 3), (2, 0, 3), (1, 0, 1), (2, 1, 1), (2, 0, 0), (3, 2, 0),
-    (1, 0, 2), (1, 1, 0), (2, 1, 3), (1, 2, 3), (1, 1, 1), (3, 1, 0),
-    (2, 2, 1), (2, 2, 3), (2, 1, 0), (2, 3, 1), (1, 2, 1), (1, 1, 2),
-    (2, 2, 0), (1, 3, 3), (2, 3, 3), (2, 2, 2), (1, 2, 0), (1, 3, 1),
-    (2, 3, 0), (1, 4, 3), (1, 4, 1), (1, 2, 2), (1, 3, 0), (0, 0, 1),
-    (2, 3, 2), (1, 4, 0), (1, 3, 2), (0, 0, 0), (0, 0, 3), (1, 4, 2),
-    (0, 0, 2),
+    (2, 0, 0), (1, 0, 0), (2, 0, 2), (3, 0, 0), (1, 0, 2), (2, 0, 3),
+    (3, 2, 0), (1, 0, 3), (2, 0, 1), (2, 1, 0), (2, 2, 0), (1, 1, 2),
+    (1, 1, 0), (2, 1, 2), (1, 0, 1), (1, 2, 2), (2, 1, 3), (1, 1, 3),
+    (2, 2, 2), (1, 2, 0), (2, 1, 1), (2, 3, 0), (2, 3, 2), (1, 1, 1),
+    (3, 1, 0), (2, 2, 3), (1, 2, 3), (1, 3, 0), (1, 3, 2), (2, 3, 3),
+    (1, 2, 1), (2, 2, 1), (1, 3, 3), (2, 3, 1), (1, 4, 2), (1, 3, 1),
+    (1, 4, 3), (0, 0, 2), (1, 4, 0), (0, 0, 3), (0, 0, 0), (1, 4, 1),
+    (0, 0, 1),
 )
 
 
@@ -48,23 +47,25 @@
 
     def kernel(x_ref, one_ref, two_ref, o_ref, x_held, one_held, two_held, sem):
         rows = field.shape[2] // nodes
-        pieces = []
+        held = one_held if level == 1 else two_held
+        needed = (one_ref if level == 1 else two_ref, held)
+        later = (two_ref, two_held) if level == 1 else (one_ref, one_held)
+        pieces = [needed]
         for n in range(nodes):
             at = pl.ds(n * rows, rows)
             pieces.append((x_ref.at[0, 0, at], x_held.at[0, 0, at]))
-        pieces.append((one_ref, one_held))
-        pieces.append((two_ref, two_held))
+        pieces.append(later)
         copies = [
             pltpu.make_async_copy(*piece, sem.at[i]) for i, piece in enumerate(pieces)
         ]
         for copy in copies:
             copy.start()
-        for copy in copies:
-            copy.wait()
-        held = one_held if level == 1 else two_held
-        for n in range(nodes):
+        copies[0].wait()
+        for n in range(nodes):
+            copies[n + 1].wait()
             x = x_held[0, 0, pl.ds(n * leaf, leaf), pl.ds(chunk * width, width)]
             o_ref[n] = dot(held[0, 0, n], x).astype(o_ref.dtype)
+        copies[-1].wait()
 
     out = jax.ShapeDtypeStruct((nodes, leaf, width), jnp.bfloat16)
     like = [jax.ShapeDtypeStruct(a.shape, a.dtype) for a in (field, one, two)]
@@ -96,13 +97,13 @@
     def kernel(table_ref, own_ref, partner_ref, w_ref, o_ref):
         for n in range(nodes):
             w = w_ref[0, 0, at, n]
-            other = partner_ref[table_ref[level, section, n]]
+            other = partner_ref[table_ref[level, section, 0, 0, n]]
             total = dot(w[:, :leaf], own_ref[n]) + dot(w[:, leaf:], other)
             o_ref[n] = total.astype(o_ref.dtype)
 
     return pl.pallas_call(
         kernel, out_shape=jax.ShapeDtypeStruct(own.shape, own.dtype),
-        in_specs=[SMEM, VMEM, VMEM, VMEM], out_specs=VMEM,
+        in_specs=[VMEM] * 4, out_specs=VMEM,
         cost_estimate=cost(2, own.shape), compiler_params=small(),
     )(table, own, partner, weights)
 
@@ -111,23 +112,31 @@
     nodes, leaf, width = sibling.shape
 
     def kernel(a_ref, b_ref, one_ref, two_ref, *refs):
-        o_ref = refs[-1]
+        o_ref, z_ref, sem = refs[-3:]
+        copies = []
         for n in range(nodes):
             total = dot(one_ref[0, 0, n], a_ref[n]) + dot(two_ref[0, 0, n], b_ref[n])
-            o_ref[0, 0, pl.ds(n * leaf, leaf), :] = total.astype(o_ref.dtype)
+            z_ref[n] = total.astype(z_ref.dtype)
+            piece = o_ref.at[0, 0, pl.ds(n * leaf, leaf), pl.ds(chunk * width, width)]
+            copies.append(pltpu.make_async_copy(z_ref.at[n], piece, sem.at[n]))
+            copies[n].start()
+        for copy in copies:
+            copy.wait()
 
     args = (sibling, distant, one, two)
     specs = [VMEM] * 4
     alias = {}
     if held is not None:
         args += (held,)
-        specs.append(pl.BlockSpec(memory_space=pl.ANY))
+        specs.append(HBM)
         alias = {4: 0}
     return pl.pallas_call(
-        kernel, grid=(1,), out_shape=jax.ShapeDtypeStruct(shape, jnp.bfloat16),
-        in_specs=specs,
-        out_specs=pl.BlockSpec((1, 1, nodes * leaf, width), lambda i: (0, 0, 0, chunk)),
-        input_output_aliases=alias,
+        kernel, out_shape=jax.ShapeDtypeStruct(shape, jnp.bfloat16),
+        in_specs=specs, out_specs=HBM, input_output_aliases=alias,
+        scratch_shapes=[
+            pltpu.VMEM((nodes, leaf, width), jnp.bfloat16),
+            pltpu.SemaphoreType.DMA((nodes,)),
+        ],
         cost_estimate=cost(2, sibling.shape), compiler_params=small(),
     )(*args)
 
@@ -138,7 +147,6 @@
     shape = field.shape
     width = shape[3] // CHUNKS
     top = lax.axis_size("grp").bit_length() - 1
-    tables = pairing[:, :, 0, 0]
     sources = {1: source_one, 2: source_two}
     value, moved = {}, {}
     out = None
@@ -163,12 +171,12 @@
             axis, bit = "grp", top - level
         elif level == 2:
             sent = value[2, k] = advance(
-                value[2, k], moved[2, k], sections_two, stage - 1, tables, 1, stage - 1
+                value[2, k], moved[2, k], sections_two, stage - 1, pairing, 1, stage - 1
             )
             axis, bit = "grp", top - 2 - stage if stage < 3 else top - 1
         elif stage == 1:
             sent = value[1, k] = advance(
-                value[1, k], moved[1, k], sections_one, 0, tables, 0, 0
+                value[1, k], moved[1, k], sections_one, 0, pairing, 0, 0
             )
         elif stage == 2:
             sent = value[1, k] = moved[1, k]
@@ -176,7 +184,7 @@
         else:
             value[1, k] = advance(
                 value[1, k], moved[1, k], moved[3, stage - 3], 0,
-                moved[3, 2][:, :, 0, 0], 0, stage - 2,
+                moved[3, 2], 0, stage - 2,
             )
             if stage == 3:
                 sent = value[1, k]

time: 186 us -> 183 us (0.984)
  Pallas kernels: 32.9 us -> 19.2 us
  waiting for transfers between devices: 107 us -> 115 us
  starting transfers between devices: 45.6 us -> 47.7 us
    pallas_call x24, Pallas kernels: 24.5 us -> 10.9 us  [advance(): pl.pallas_call(kernel, out_shape=jax.ShapeDtypeStruct(own.shape, own.dtyp...]
    ppermute x35, waiting for transfers between devices: 107 us -> 115 us  [swapped(): lax.ppermute(value, axis, [(i, i ^ 1 << bit) for i in range(lax.axis_size...]
    ppermute x35, starting transfers between devices: 45.6 us -> 47.7 us  [swapped(): lax.ppermute(value, axis, [(i, i ^ 1 << bit) for i in range(lax.axis_size...]
  transfers between devices with their start and end apart: 35 -> 35, of which waited for: 20 -> 21; matrix products, arithmetic and copies ran while one was open for 0% -> 0% of each run, Pallas kernels for 16% -> 9%
where the time goes in v2:
time: 183 us; the launch traced here: 182 us
  waiting for transfers between devices  115 us (63%)
  starting transfers between devices  47.7 us (26%)
  Pallas kernels  19.2 us (10%)
    ppermute x35, waiting for transfers between devices, swapped(): lax.ppermute(value, axis, [(i, i ^ 1 << bit) for i in range(lax.axis_size...  115 us
    ppermute x35, starting transfers between devices, swapped(): lax.ppermute(value, axis, [(i, i ^ 1 << bit) for i in range(lax.axis_size...  47.7 us
    pallas_call x24, Pallas kernels, advance(): pl.pallas_call(kernel, out_shape=jax.ShapeDtypeStruct(own.shape, own.dtyp...  10.9 us
    pallas_call x4, Pallas kernels, target(): pl.pallas_call(kernel, out_shape=jax.ShapeDtypeStruct(shape, jnp.bfloat16...  4.35 us
  transfers between devices with their start and end apart: 35, of which 21 were waited for; matrix products, arithmetic and copies ran while one was open for 0% of the time, Pallas kernels for 9%

profile of v2, /device:TPU:0, one launch (start us, length us, event | category | flops | bytes accessed | tf_op | source)
XLA Modules:
  0.0 182.5 jit_solution(13772439575854722385)
XLA Ops:
  0.0 2.0 %shard_map.82 = (bf16[4,256,128]{2,1,0:T(8,128)(2,1)S(1)}, bf16[1,1,1024,512]{3,2,1,0:T(8,128)(2,1)S(1)}, bf16[1,1,4,256,256]{4,3,2,1,0:T(8,128)(2,1)S(1)}, bf16[1,1,4,256,256]{4,3,2,1,0:T(8,128)(2,1)S(1)}) custom-call(bf16[1,1,1024,512]{3,2,1,0:T(8,128)(2,1)} %x_ref.1, bf16[1,1,4,256,256]{4,3,2,1,0:T(8,128)(2,1)} %one_ref.5, ...), custom_call_target="tpu_custom_call" | custom-call | flops 67108864 | bytes 1048576 | tf_op jit(solution)/shard_map/pallas_call | solution.py:72
  2.3 4.1 %collective-permute-start.1 = (bf16[4,256,128]{2,1,0:T(8,128)(2,1)S(1)}, bf16[4,256,128]{2,1,0:T(8,128)(2,1)S(1)}, u32[]{:S(2)}, u32[]{:S(2)}) collective-permute-start(bf16[4,256,128]{2,1,0:T(8,128)(2,1)S(1)} %shard_map.83.own_ref), channel_id=1, source_target_pairs={{0,16},{2,18},{4,20},{6,22},{8,24},{10,26},{12,28},{14,30},{16,0},... | collective-permute-start | bytes 786440 | tf_op jit(solution)/shard_map/ppermute | solution.py:25
  7.1 3.0 %collective-permute-start.19 = (bf16[4,256,128]{2,1,0:T(8,128)(2,1)S(1)}, bf16[4,256,128]{2,1,0:T(8,128)(2,1)S(1)}, u32[]{:S(2)}, u32[]{:S(2)}) collective-permute-start(bf16[4,256,128]{2,1,0:T(8,128)(2,1)S(1)} %shard_map.98.own_ref), channel_id=1, source_target_pairs={{0,16},{2,18},{4,20},{6,22},{8,24},{10,26},{12,28},{14,30},{16,0},... | collective-permute-start | bytes 786440 | tf_op jit(solution)/shard_map/ppermute | solution.py:25
  10.7 2.0 %collective-permute-start.7 = (bf16[4,256,128]{2,1,0:T(8,128)(2,1)S(1)}, bf16[4,256,128]{2,1,0:T(8,128)(2,1)S(1)}, u32[]{:S(2)}, u32[]{:S(2)}) collective-permute-start(bf16[4,256,128]{2,1,0:T(8,128)(2,1)S(1)} %shard_map.87.own_ref), channel_id=1, source_target_pairs={{0,8},{2,10},{4,12},{6,14},{8,0},{10,2},{12,4},{14,6},{16,24},{18,... | collective-permute-start | bytes 786440 | tf_op jit(solution)/shard_map/ppermute | solution.py:25
  13.2 22.8 %collective-permute-done.1.partner_ref = bf16[4,256,128]{2,1,0:T(8,128)(2,1)S(1)} collective-permute-done((bf16[4,256,128]{2,1,0:T(8,128)(2,1)S(1)}, bf16[4,256,128]{2,1,0:T(8,128)(2,1)S(1)}, u32[]{:S(2)}, u32[]{:S(2)}) %collective-permute-start.1) | collective-permute-done | bytes 262176 | tf_op jit(solution)/shard_map/ppermute | solution.py:25
  36.0 1.8 collective-permute-start
  38.3 3.4 %collective-permute-done.11.partner_ref = bf16[4,256,128]{2,1,0:T(8,128)(2,1)S(1)} collective-permute-done((bf16[4,256,128]{2,1,0:T(8,128)(2,1)S(1)}, bf16[4,256,128]{2,1,0:T(8,128)(2,1)S(1)}, u32[]{:S(2)}, u32[]{:S(2)}) %collective-permute-start.11) | collective-permute-done | bytes 262176 | tf_op jit(solution)/shard_map/ppermute | solution.py:25
  42.1 2.1 %collective-permute-start.31 = (bf16[4,256,128]{2,1,0:T(8,128)(2,1)S(1)}, bf16[4,256,128]{2,1,0:T(8,128)(2,1)S(1)}, u32[]{:S(2)}, u32[]{:S(2)}) collective-permute-start(bf16[4,256,128]{2,1,0:T(8,128)(2,1)S(1)} %shard_map.110.own_ref), channel_id=1, source_target_pairs={{0,8},{2,10},{4,12},{6,14},{8,0},{10,2},{12,4},{14,6},{16,24},{18,... | collective-permute-start | bytes 786440 | tf_op jit(solution)/shard_map/ppermute | solution.py:25
  44.2 3.2 %collective-permute-done.19.partner_ref = bf16[4,256,128]{2,1,0:T(8,128)(2,1)S(1)} collective-permute-done((bf16[4,256,128]{2,1,0:T(8,128)(2,1)S(1)}, bf16[4,256,128]{2,1,0:T(8,128)(2,1)S(1)}, u32[]{:S(2)}, u32[]{:S(2)}) %collective-permute-start.19) | collective-permute-done | bytes 262176 | tf_op jit(solution)/shard_map/ppermute | solution.py:25
  47.4 4.8 %collective-permute-done.27.partner_ref = bf16[4,256,128]{2,1,0:T(8,128)(2,1)S(1)} collective-permute-done((bf16[4,256,128]{2,1,0:T(8,128)(2,1)S(1)}, bf16[4,256,128]{2,1,0:T(8,128)(2,1)S(1)}, u32[]{:S(2)}, u32[]{:S(2)}) %collective-permute-start.27) | collective-permute-done | bytes 262176 | tf_op jit(solution)/shard_map/ppermute | solution.py:25
  52.1 1.5 collective-permute-start.2
  54.4 3.4 %collective-permute-done.23.partner_ref = bf16[4,256,128]{2,1,0:T(8,128)(2,1)S(1)} collective-permute-done((bf16[4,256,128]{2,1,0:T(8,128)(2,1)S(1)}, bf16[4,256,128]{2,1,0:T(8,128)(2,1)S(1)}, u32[]{:S(2)}, u32[]{:S(2)}) %collective-permute-start.23) | collective-permute-done | bytes 262176 | tf_op jit(solution)/shard_map/ppermute | solution.py:25
  57.7 1.5 collective-permute-start.4
  59.7 3.6 %collective-permute-done.31.partner_ref = bf16[4,256,128]{2,1,0:T(8,128)(2,1)S(1)} collective-permute-done((bf16[4,256,128]{2,1,0:T(8,128)(2,1)S(1)}, bf16[4,256,128]{2,1,0:T(8,128)(2,1)S(1)}, u32[]{:S(2)}, u32[]{:S(2)}) %collective-permute-start.31) | collective-permute-done | bytes 262176 | tf_op jit(solution)/shard_map/ppermute | solution.py:25
  63.4 1.5 collective-permute-start.20
  65.3 3.5 %collective-permute-done.15.partner_ref = bf16[4,256,128]{2,1,0:T(8,128)(2,1)S(1)} collective-permute-done((bf16[4,256,128]{2,1,0:T(8,128)(2,1)S(1)}, bf16[4,256,128]{2,1,0:T(8,128)(2,1)S(1)}, u32[]{:S(2)}, u32[]{:S(2)}) %collective-permute-start.15) | collective-permute-done | bytes 262176 | tf_op jit(solution)/shard_map/ppermute | solution.py:25
  68.9 1.5 collective-permute-start.28
  70.9 1.6 collective-permute-start.8
  73.5 21.5 %collective-permute-done.20.own_ref = bf16[4,256,128]{2,1,0:T(8,128)(2,1)S(1)} collective-permute-done((bf16[4,256,128]{2,1,0:T(8,128)(2,1)S(1)}, bf16[4,256,128]{2,1,0:T(8,128)(2,1)S(1)}, u32[]{:S(2)}, u32[]{:S(2)}) %collective-permute-start.20) | collective-permute-done | bytes 262176 | tf_op jit(solution)/shard_map/ppermute | solution.py:25
  95.0 1.5 collective-permute-start.6
  97.0 3.6 %collective-permute-done.28.own_ref = bf16[4,256,128]{2,1,0:T(8,128)(2,1)S(1)} collective-permute-done((bf16[4,256,128]{2,1,0:T(8,128)(2,1)S(1)}, bf16[4,256,128]{2,1,0:T(8,128)(2,1)S(1)}, u32[]{:S(2)}, u32[]{:S(2)}) %collective-permute-start.28) | collective-permute-done | bytes 262176 | tf_op jit(solution)/shard_map/ppermute | solution.py:25
  100.6 1.6 collective-permute-start.32
  103.2 0.7 collective-permute-start.3
  103.8 4.4 %collective-permute-done.32.partner_ref = bf16[4,256,128]{2,1,0:T(8,128)(2,1)S(1)} collective-permute-done((bf16[4,256,128]{2,1,0:T(8,128)(2,1)S(1)}, bf16[4,256,128]{2,1,0:T(8,128)(2,1)S(1)}, u32[]{:S(2)}, u32[]{:S(2)}) %collective-permute-start.32) | collective-permute-done | bytes 262176 | tf_op jit(solution)/shard_map/ppermute | solution.py:25
  108.2 2.2 %collective-permute-start.13 = (bf16[4,256,128]{2,1,0:T(8,128)(2,1)S(1)}, bf16[4,256,128]{2,1,0:T(8,128)(2,1)S(1)}, u32[]{:S(2)}, u32[]{:S(2)}) collective-permute-start(bf16[4,256,128]{2,1,0:T(8,128)(2,1)S(1)} %collective-permute-done.12.own_ref), channel_id=1, source_target_pairs={{0,8},{2,10},{4,12},{6,14},{8,0},{10,2},{12,4},{14,6},{16,24},{18,... | collective-permute-start | bytes 786440 | tf_op jit(solution)/shard_map/ppermute | solution.py:25
  111.0 2.3 %collective-permute-start.21 = (bf16[4,256,128]{2,1,0:T(8,128)(2,1)S(1)}, bf16[4,256,128]{2,1,0:T(8,128)(2,1)S(1)}, u32[]{:S(2)}, u32[]{:S(2)}) collective-permute-start(bf16[4,256,128]{2,1,0:T(8,128)(2,1)S(1)} %collective-permute-done.20.own_ref), channel_id=1, source_target_pairs={{0,8},{2,10},{4,12},{6,14},{8,0},{10,2},{12,4},{14,6},{16,24},{18,... | collective-permute-start | bytes 786440 | tf_op jit(solution)/shard_map/ppermute | solution.py:25
  113.8 3.8 %collective-permute-done.13.partner_ref = bf16[4,256,128]{2,1,0:T(8,128)(2,1)S(1)} collective-permute-done((bf16[4,256,128]{2,1,0:T(8,128)(2,1)S(1)}, bf16[4,256,128]{2,1,0:T(8,128)(2,1)S(1)}, u32[]{:S(2)}, u32[]{:S(2)}) %collective-permute-start.13) | collective-permute-done | bytes 262176 | tf_op jit(solution)/shard_map/ppermute | solution.py:25
  118.1 4.7 %collective-permute-done.21.partner_ref = bf16[4,256,128]{2,1,0:T(8,128)(2,1)S(1)} collective-permute-done((bf16[4,256,128]{2,1,0:T(8,128)(2,1)S(1)}, bf16[4,256,128]{2,1,0:T(8,128)(2,1)S(1)}, u32[]{:S(2)}, u32[]{:S(2)}) %collective-permute-start.21) | collective-permute-done | bytes 262176 | tf_op jit(solution)/shard_map/ppermute | solution.py:25
  123.2 2.4 %collective-permute-done.29.partner_ref = bf16[4,256,128]{2,1,0:T(8,128)(2,1)S(1)} collective-permute-done((bf16[4,256,128]{2,1,0:T(8,128)(2,1)S(1)}, bf16[4,256,128]{2,1,0:T(8,128)(2,1)S(1)}, u32[]{:S(2)}, u32[]{:S(2)}) %collective-permute-start.29) | collective-permute-done | bytes 262176 | tf_op jit(solution)/shard_map/ppermute | solution.py:25
  127.1 1.6 collective-permute-start.5
  129.1 0.6 collective-permute-start.14
  130.2 1.6 collective-permute-start.22
  132.2 0.6 collective-permute-start.30
  133.3 3.3 %collective-permute-start.34 = (bf16[4,256,128]{2,1,0:T(8,128)(2,1)S(1)}, bf16[4,256,128]{2,1,0:T(8,128)(2,1)S(1)}, u32[]{:S(2)}, u32[]{:S(2)}) collective-permute-start(bf16[4,256,128]{2,1,0:T(8,128)(2,1)S(1)} %shard_map.113), channel_id=1, source_target_pairs={{0,16},{2,18},{4,20},{6,22},{8,24},{10,26},{12,28},{14,30},{16,0},... | collective-permute-start | bytes 786440 | tf_op jit(solution)/shard_map/ppermute | solution.py:25
  136.5 0.6 shard_map.105
  137.2 2.4 %collective-permute-start.26 = (bf16[4,256,128]{2,1,0:T(8,128)(2,1)S(1)}, bf16[4,256,128]{2,1,0:T(8,128)(2,1)S(1)}, u32[]{:S(2)}, u32[]{:S(2)}) collective-permute-start(bf16[4,256,128]{2,1,0:T(8,128)(2,1)S(1)} %shard_map.105), channel_id=1, source_target_pairs={{0,16},{2,18},{4,20},{6,22},{8,24},{10,26},{12,28},{14,30},{16,0},... | collective-permute-start | bytes 786440 | tf_op jit(solution)/shard_map/ppermute | solution.py:25
  140.0 1.9 %collective-permute-done.14.partner_ref = bf16[4,256,128]{2,1,0:T(8,128)(2,1)S(1)} collective-permute-done((bf16[4,256,128]{2,1,0:T(8,128)(2,1)S(1)}, bf16[4,256,128]{2,1,0:T(8,128)(2,1)S(1)}, u32[]{:S(2)}, u32[]{:S(2)}) %collective-permute-start.14) | collective-permute-done | bytes 262176 | tf_op jit(solution)/shard_map/ppermute | solution.py:25
  141.9 3.2 %collective-permute-start.18 = (bf16[4,256,128]{2,1,0:T(8,128)(2,1)S(1)}, bf16[4,256,128]{2,1,0:T(8,128)(2,1)S(1)}, u32[]{:S(2)}, u32[]{:S(2)}) collective-permute-start(bf16[4,256,128]{2,1,0:T(8,128)(2,1)S(1)} %shard_map.97), channel_id=1, source_target_pairs={{0,16},{2,18},{4,20},{6,22},{8,24},{10,26},{12,28},{14,30},{16,0},... | collective-permute-start | bytes 786440 | tf_op jit(solution)/shard_map/ppermute | solution.py:25
  145.6 2.0 %collective-permute-done.22.partner_ref = bf16[4,256,128]{2,1,0:T(8,128)(2,1)S(1)} collective-permute-done((bf16[4,256,128]{2,1,0:T(8,128)(2,1)S(1)}, bf16[4,256,128]{2,1,0:T(8,128)(2,1)S(1)}, u32[]{:S(2)}, u32[]{:S(2)}) %collective-permute-start.22) | collective-permute-done | bytes 262176 | tf_op jit(solution)/shard_map/ppermute | solution.py:25
  147.6 3.2 %collective-permute-start.10 = (bf16[4,256,128]{2,1,0:T(8,128)(2,1)S(1)}, bf16[4,256,128]{2,1,0:T(8,128)(2,1)S(1)}, u32[]{:S(2)}, u32[]{:S(2)}) collective-permute-start(bf16[4,256,128]{2,1,0:T(8,128)(2,1)S(1)} %shard_map.90), channel_id=1, source_target_pairs={{0,16},{2,18},{4,20},{6,22},{8,24},{10,26},{12,28},{14,30},{16,0},... | collective-permute-start | bytes 786440 | tf_op jit(solution)/shard_map/ppermute | solution.py:25
  152.7 13.0 %collective-permute-done.34.b_ref = bf16[4,256,128]{2,1,0:T(8,128)(2,1)S(1)} collective-permute-done((bf16[4,256,128]{2,1,0:T(8,128)(2,1)S(1)}, bf16[4,256,128]{2,1,0:T(8,128)(2,1)S(1)}, u32[]{:S(2)}, u32[]{:S(2)}) %collective-permute-start.34) | collective-permute-done | bytes 262176 | tf_op jit(solution)/shard_map/ppermute | solution.py:25
  165.6 1.1 shard_map.114.refs_0_
  166.7 4.5 %collective-permute-done.26.b_ref = bf16[4,256,128]{2,1,0:T(8,128)(2,1)S(1)} collective-permute-done((bf16[4,256,128]{2,1,0:T(8,128)(2,1)S(1)}, bf16[4,256,128]{2,1,0:T(8,128)(2,1)S(1)}, u32[]{:S(2)}, u32[]{:S(2)}) %collective-permute-start.26) | collective-permute-done | bytes 262176 | tf_op jit(solution)/shard_map/ppermute | solution.py:25
  171.3 1.1 shard_map.115.refs_0_
  172.4 4.5 %collective-permute-done.18.b_ref = bf16[4,256,128]{2,1,0:T(8,128)(2,1)S(1)} collective-permute-done((bf16[4,256,128]{2,1,0:T(8,128)(2,1)S(1)}, bf16[4,256,128]{2,1,0:T(8,128)(2,1)S(1)}, u32[]{:S(2)}, u32[]{:S(2)}) %collective-permute-start.18) | collective-permute-done | bytes 262176 | tf_op jit(solution)/shard_map/ppermute | solution.py:25
  176.9 1.1 shard_map.116.refs_0_
  178.0 3.2 %collective-permute-done.10.b_ref = bf16[4,256,128]{2,1,0:T(8,128)(2,1)S(1)} collective-permute-done((bf16[4,256,128]{2,1,0:T(8,128)(2,1)S(1)}, bf16[4,256,128]{2,1,0:T(8,128)(2,1)S(1)}, u32[]{:S(2)}, u32[]{:S(2)}) %collective-permute-start.10) | collective-permute-done | bytes 262176 | tf_op jit(solution)/shard_map/ppermute | solution.py:25
  181.2 1.1 shard_map.117
  (69 shorter events, 15.5 us)
Async XLA Ops:
  2.3 33.8 %collective-permute-start.1 = (bf16[4,256,128]{2,1,0:T(8,128)(2,1)S(1)}, bf16[4,256,128]{2,1,0:T(8,128)(2,1)S(1)}, u32[]{:S(2)}, u32[]{:S(2)}) collective-permute-start(bf16[4,256,128]{2,1,0:T(8,128)(2,1)S(1)} %shard_map.83.own_ref), channel_id=1, source_target_pairs={{0,16},{2,18},{4,20},{6,22},{8,24},{10,26},{12,28},{14,30},{16,0},... | collective-permute-start | bytes 786440 | tf_op jit(solution)/shard_map/ppermute | solution.py:25
  6.7 35.0 %collective-permute-start.11 = (bf16[4,256,128]{2,1,0:T(8,128)(2,1)S(1)}, bf16[4,256,128]{2,1,0:T(8,128)(2,1)S(1)}, u32[]{:S(2)}, u32[]{:S(2)}) collective-permute-start(bf16[4,256,128]{2,1,0:T(8,128)(2,1)S(1)} %shard_map.91.own_ref), channel_id=1, source_target_pairs={{0,16},{2,18},{4,20},{6,22},{8,24},{10,26},{12,28},{14,30},{16,0},... | collective-permute-start | bytes 786440 | tf_op jit(solution)/shard_map/ppermute | solution.py:25
  7.1 40.3 %collective-permute-start.19 = (bf16[4,256,128]{2,1,0:T(8,128)(2,1)S(1)}, bf16[4,256,128]{2,1,0:T(8,128)(2,1)S(1)}, u32[]{:S(2)}, u32[]{:S(2)}) collective-permute-start(bf16[4,256,128]{2,1,0:T(8,128)(2,1)S(1)} %shard_map.98.own_ref), channel_id=1, source_target_pairs={{0,16},{2,18},{4,20},{6,22},{8,24},{10,26},{12,28},{14,30},{16,0},... | collective-permute-start | bytes 786440 | tf_op jit(solution)/shard_map/ppermute | solution.py:25
  10.3 25.7 %copy-start.4 = (s32[2,3,1,1,4]{4,3,2,1,0:T(1,128)S(1)}, s32[2,3,1,1,4]{4,3,2,1,0:T(1,128)}, u32[]{:S(2)}) copy-start(s32[2,3,1,1,4]{4,3,2,1,0:T(1,128)} %table_ref.31) | copy-start | bytes 292
  10.3 27.5 %copy-start.1 = (bf16[1,1,3,4,256,512]{5,4,3,2,1,0:T(8,128)(2,1)S(1)}, bf16[1,1,3,4,256,512]{5,4,3,2,1,0:T(8,128)(2,1)}, u32[]{:S(2)}) copy-start(bf16[1,1,3,4,256,512]{5,4,3,2,1,0:T(8,128)(2,1)} %w_ref.28) | copy-start | bytes 9437188
  10.3 41.8 %collective-permute-start.27 = (bf16[4,256,128]{2,1,0:T(8,128)(2,1)S(1)}, bf16[4,256,128]{2,1,0:T(8,128)(2,1)S(1)}, u32[]{:S(2)}, u32[]{:S(2)}) collective-permute-start(bf16[4,256,128]{2,1,0:T(8,128)(2,1)S(1)} %shard_map.106.own_ref), channel_id=1, source_target_pairs={{0,16},{2,18},{4,20},{6,22},{8,24},{10,26},{12,28},{14,30},{16,0},... | collective-permute-start | bytes 786440 | tf_op jit(solution)/shard_map/ppermute | solution.py:25
  10.7 43.0 %collective-permute-start.7 = (bf16[4,256,128]{2,1,0:T(8,128)(2,1)S(1)}, bf16[4,256,128]{2,1,0:T(8,128)(2,1)S(1)}, u32[]{:S(2)}, u32[]{:S(2)}) collective-permute-start(bf16[4,256,128]{2,1,0:T(8,128)(2,1)S(1)} %shard_map.87.own_ref), channel_id=1, source_target_pairs={{0,8},{2,10},{4,12},{6,14},{8,0},{10,2},{12,4},{14,6},{16,24},{18,... | collective-permute-start | bytes 786440 | tf_op jit(solution)/shard_map/ppermute | solution.py:25
  36.0 6.1 %collective-permute-start = (s32[2,3,1,1,4]{4,3,2,1,0:T(1,128)S(1)}, s32[2,3,1,1,4]{4,3,2,1,0:T(1,128)S(1)}, u32[]{:S(2)}, u32[]{:S(2)}) collective-permute-start(s32[2,3,1,1,4]{4,3,2,1,0:T(1,128)S(1)} %copy-done.4), channel_id=1, source_target_pairs={{0,1},{1,0},{2,3},{3,2},{4,5},{5,4},{6,7},{7,6},{8,9},{9,8},{10,11... | collective-permute-start | bytes 296 | tf_op jit(solution)/shard_map/ppermute | solution.py:25
  41.6 16.1 %collective-permute-start.23 = (bf16[4,256,128]{2,1,0:T(8,128)(2,1)S(1)}, bf16[4,256,128]{2,1,0:T(8,128)(2,1)S(1)}, u32[]{:S(2)}, u32[]{:S(2)}) collective-permute-start(bf16[4,256,128]{2,1,0:T(8,128)(2,1)S(1)} %shard_map.102.own_ref), channel_id=1, source_target_pairs={{0,8},{2,10},{4,12},{6,14},{8,0},{10,2},{12,4},{14,6},{16,24},{18,... | collective-permute-start | bytes 786440 | tf_op jit(solution)/shard_map/ppermute | solution.py:25
  42.1 21.3 %collective-permute-start.31 = (bf16[4,256,128]{2,1,0:T(8,128)(2,1)S(1)}, bf16[4,256,128]{2,1,0:T(8,128)(2,1)S(1)}, u32[]{:S(2)}, u32[]{:S(2)}) collective-permute-start(bf16[4,256,128]{2,1,0:T(8,128)(2,1)S(1)} %shard_map.110.own_ref), channel_id=1, source_target_pairs={{0,8},{2,10},{4,12},{6,14},{8,0},{10,2},{12,4},{14,6},{16,24},{18,... | collective-permute-start | bytes 786440 | tf_op jit(solution)/shard_map/ppermute | solution.py:25
  47.4 21.5 %collective-permute-start.15 = (bf16[4,256,128]{2,1,0:T(8,128)(2,1)S(1)}, bf16[4,256,128]{2,1,0:T(8,128)(2,1)S(1)}, u32[]{:S(2)}, u32[]{:S(2)}) collective-permute-start(bf16[4,256,128]{2,1,0:T(8,128)(2,1)S(1)} %get-tuple-element.12.own_ref), channel_id=1, source_target_pairs={{0,8},{2,10},{4,12},{6,14},{8,0},{10,2},{12,4},{14,6},{16,24},{18,... | collective-permute-start | bytes 786440 | tf_op jit(solution)/shard_map/ppermute | solution.py:25
  52.1 18.8 %collective-permute-start.2 = (bf16[4,256,128]{2,1,0:T(8,128)(2,1)S(1)}, bf16[4,256,128]{2,1,0:T(8,128)(2,1)S(1)}, u32[]{:S(2)}, u32[]{:S(2)}) collective-permute-start(bf16[4,256,128]{2,1,0:T(8,128)(2,1)S(1)} %shard_map.84), channel_id=1, source_target_pairs={{0,1},{1,0},{2,3},{3,2},{4,5},{5,4},{6,7},{7,6},{8,9},{9,8},{10,11... | collective-permute-start | bytes 786440 | tf_op jit(solution)/shard_map/ppermute | solution.py:25
  53.7 19.3 %collective-permute-start.12 = (bf16[4,256,128]{2,1,0:T(8,128)(2,1)S(1)}, bf16[4,256,128]{2,1,0:T(8,128)(2,1)S(1)}, u32[]{:S(2)}, u32[]{:S(2)}) collective-permute-start(bf16[4,256,128]{2,1,0:T(8,128)(2,1)S(1)} %shard_map.92), channel_id=1, source_target_pairs={{0,1},{1,0},{2,3},{3,2},{4,5},{5,4},{6,7},{7,6},{8,9},{9,8},{10,11... | collective-permute-start | bytes 786440 | tf_op jit(solution)/shard_map/ppermute | solution.py:25
  57.7 12.7 %copy-start = (bf16[1,1,3,4,256,512]{5,4,3,2,1,0:T(8,128)(2,1)S(1)}, bf16[1,1,3,4,256,512]{5,4,3,2,1,0:T(8,128)(2,1)}, u32[]{:S(2)}) copy-start(bf16[1,1,3,4,256,512]{5,4,3,2,1,0:T(8,128)(2,1)} %w_ref.31) | copy-start | bytes 9437188
  57.7 68.3 %collective-permute-start.4 = (bf16[1,1,1,4,256,512]{5,4,3,2,1,0:T(8,128)(2,1)S(1)}, bf16[1,1,1,4,256,512]{5,4,3,2,1,0:T(8,128)(2,1)S(1)}, u32[]{:S(2)}, u32[]{:S(2)}) collective-permute-start(bf16[1,1,1,4,256,512]{5,4,3,2,1,0:T(8,128)(2,1)S(1)} %get-tuple-element.14), channel_id=1, source_target_pairs={{0,1},{1,0},{2,3},{3,2},{4,5},{5,4},{6,7},{7,6},{8,9},{9,8},{10,11... | collective-permute-start | bytes 3145736 | tf_op jit(solution)/shard_map/ppermute | solution.py:25
  63.4 31.7 %collective-permute-start.20 = (bf16[4,256,128]{2,1,0:T(8,128)(2,1)S(1)}, bf16[4,256,128]{2,1,0:T(8,128)(2,1)S(1)}, u32[]{:S(2)}, u32[]{:S(2)}) collective-permute-start(bf16[4,256,128]{2,1,0:T(8,128)(2,1)S(1)} %shard_map.99), channel_id=1, source_target_pairs={{0,1},{1,0},{2,3},{3,2},{4,5},{5,4},{6,7},{7,6},{8,9},{9,8},{10,11... | collective-permute-start | bytes 786440 | tf_op jit(solution)/shard_map/ppermute | solution.py:25
  68.9 31.7 %collective-permute-start.28 = (bf16[4,256,128]{2,1,0:T(8,128)(2,1)S(1)}, bf16[4,256,128]{2,1,0:T(8,128)(2,1)S(1)}, u32[]{:S(2)}, u32[]{:S(2)}) collective-permute-start(bf16[4,256,128]{2,1,0:T(8,128)(2,1)S(1)} %shard_map.107), channel_id=1, source_target_pairs={{0,1},{1,0},{2,3},{3,2},{4,5},{5,4},{6,7},{7,6},{8,9},{9,8},{10,11... | collective-permute-start | bytes 786440 | tf_op jit(solution)/shard_map/ppermute | solution.py:25
  70.9 31.8 %collective-permute-start.8 = (bf16[4,256,128]{2,1,0:T(8,128)(2,1)S(1)}, bf16[4,256,128]{2,1,0:T(8,128)(2,1)S(1)}, u32[]{:S(2)}, u32[]{:S(2)}) collective-permute-start(bf16[4,256,128]{2,1,0:T(8,128)(2,1)S(1)} %shard_map.88.own_ref), channel_id=1, source_target_pairs={{0,4},{2,6},{4,0},{6,2},{8,12},{10,14},{12,8},{14,10},{16,20},{18,... | collective-permute-start | bytes 786440 | tf_op jit(solution)/shard_map/ppermute | solution.py:25
  72.9 30.2 %collective-permute-start.24 = (bf16[4,256,128]{2,1,0:T(8,128)(2,1)S(1)}, bf16[4,256,128]{2,1,0:T(8,128)(2,1)S(1)}, u32[]{:S(2)}, u32[]{:S(2)}) collective-permute-start(bf16[4,256,128]{2,1,0:T(8,128)(2,1)S(1)} %shard_map.103.own_ref), channel_id=1, source_target_pairs={{0,4},{2,6},{4,0},{6,2},{8,12},{10,14},{12,8},{14,10},{16,20},{18,... | collective-permute-start | bytes 786440 | tf_op jit(solution)/shard_map/ppermute | solution.py:25
  95.0 38.2 %collective-permute-start.6 = (bf16[1,1,1,4,256,512]{5,4,3,2,1,0:T(8,128)(2,1)S(1)}, bf16[1,1,1,4,256,512]{5,4,3,2,1,0:T(8,128)(2,1)S(1)}, u32[]{:S(2)}, u32[]{:S(2)}) collective-permute-start(bf16[1,1,1,4,256,512]{5,4,3,2,1,0:T(8,128)(2,1)S(1)} %get-tuple-element.13), channel_id=1, source_target_pairs={{0,1},{1,0},{2,3},{3,2},{4,5},{5,4},{6,7},{7,6},{8,9},{9,8},{10,11... | collective-permute-start | bytes 3145736 | tf_op jit(solution)/shard_map/ppermute | solution.py:25
  100.6 7.6 %collective-permute-start.32 = (bf16[4,256,128]{2,1,0:T(8,128)(2,1)S(1)}, bf16[4,256,128]{2,1,0:T(8,128)(2,1)S(1)}, u32[]{:S(2)}, u32[]{:S(2)}) collective-permute-start(bf16[4,256,128]{2,1,0:T(8,128)(2,1)S(1)} %shard_map.111.own_ref), channel_id=1, source_target_pairs={{0,4},{2,6},{4,0},{6,2},{8,12},{10,14},{12,8},{14,10},{16,20},{18,... | collective-permute-start | bytes 786440 | tf_op jit(solution)/shard_map/ppermute | solution.py:25
  102.7 8.4 %collective-permute-start.16 = (bf16[4,256,128]{2,1,0:T(8,128)(2,1)S(1)}, bf16[4,256,128]{2,1,0:T(8,128)(2,1)S(1)}, u32[]{:S(2)}, u32[]{:S(2)}) collective-permute-start(bf16[4,256,128]{2,1,0:T(8,128)(2,1)S(1)} %shard_map.95.own_ref), channel_id=1, source_target_pairs={{0,4},{2,6},{4,0},{6,2},{8,12},{10,14},{12,8},{14,10},{16,20},{18,... | collective-permute-start | bytes 786440 | tf_op jit(solution)/shard_map/ppermute | solution.py:25
  103.2 10.2 %collective-permute-start.3 = (bf16[4,256,128]{2,1,0:T(8,128)(2,1)S(1)}, bf16[4,256,128]{2,1,0:T(8,128)(2,1)S(1)}, u32[]{:S(2)}, u32[]{:S(2)}) collective-permute-start(bf16[4,256,128]{2,1,0:T(8,128)(2,1)S(1)} %collective-permute-done.2.own_ref), channel_id=1, source_target_pairs={{0,8},{2,10},{4,12},{6,14},{8,0},{10,2},{12,4},{14,6},{16,24},{18,... | collective-permute-start | bytes 786440 | tf_op jit(solution)/shard_map/ppermute | solution.py:25
  108.2 9.4 %collective-permute-start.13 = (bf16[4,256,128]{2,1,0:T(8,128)(2,1)S(1)}, bf16[4,256,128]{2,1,0:T(8,128)(2,1)S(1)}, u32[]{:S(2)}, u32[]{:S(2)}) collective-permute-start(bf16[4,256,128]{2,1,0:T(8,128)(2,1)S(1)} %collective-permute-done.12.own_ref), channel_id=1, source_target_pairs={{0,8},{2,10},{4,12},{6,14},{8,0},{10,2},{12,4},{14,6},{16,24},{18,... | collective-permute-start | bytes 786440 | tf_op jit(solution)/shard_map/ppermute | solution.py:25
  111.0 11.7 %collective-permute-start.21 = (bf16[4,256,128]{2,1,0:T(8,128)(2,1)S(1)}, bf16[4,256,128]{2,1,0:T(8,128)(2,1)S(1)}, u32[]{:S(2)}, u32[]{:S(2)}) collective-permute-start(bf16[4,256,128]{2,1,0:T(8,128)(2,1)S(1)} %collective-permute-done.20.own_ref), channel_id=1, source_target_pairs={{0,8},{2,10},{4,12},{6,14},{8,0},{10,2},{12,4},{14,6},{16,24},{18,... | collective-permute-start | bytes 786440 | tf_op jit(solution)/shard_map/ppermute | solution.py:25
  113.3 12.2 %collective-permute-start.29 = (bf16[4,256,128]{2,1,0:T(8,128)(2,1)S(1)}, bf16[4,256,128]{2,1,0:T(8,128)(2,1)S(1)}, u32[]{:S(2)}, u32[]{:S(2)}) collective-permute-start(bf16[4,256,128]{2,1,0:T(8,128)(2,1)S(1)} %collective-permute-done.28.own_ref), channel_id=1, source_target_pairs={{0,8},{2,10},{4,12},{6,14},{8,0},{10,2},{12,4},{14,6},{16,24},{18,... | collective-permute-start | bytes 786440 | tf_op jit(solution)/shard_map/ppermute | solution.py:25
  117.6 9.5 %collective-permute-start.9 = (bf16[4,256,128]{2,1,0:T(8,128)(2,1)S(1)}, bf16[4,256,128]{2,1,0:T(8,128)(2,1)S(1)}, u32[]{:S(2)}, u32[]{:S(2)}) collective-permute-start(bf16[4,256,128]{2,1,0:T(8,128)(2,1)S(1)} %shard_map.89.own_ref), channel_id=1, source_target_pairs={{0,2},{2,0},{4,6},{6,4},{8,10},{10,8},{12,14},{14,12},{16,18},{18,... | collective-permute-start | bytes 786440 | tf_op jit(solution)/shard_map/ppermute | solution.py:25
  122.8 6.4 %collective-permute-start.25 = (bf16[4,256,128]{2,1,0:T(8,128)(2,1)S(1)}, bf16[4,256,128]{2,1,0:T(8,128)(2,1)S(1)}, u32[]{:S(2)}, u32[]{:S(2)}) collective-permute-start(bf16[4,256,128]{2,1,0:T(8,128)(2,1)S(1)} %shard_map.104.own_ref), channel_id=1, source_target_pairs={{0,2},{2,0},{4,6},{6,4},{8,10},{10,8},{12,14},{14,12},{16,18},{18,... | collective-permute-start | bytes 786440 | tf_op jit(solution)/shard_map/ppermute | solution.py:25
  125.6 4.6 %collective-permute-start.33 = (bf16[4,256,128]{2,1,0:T(8,128)(2,1)S(1)}, bf16[4,256,128]{2,1,0:T(8,128)(2,1)S(1)}, u32[]{:S(2)}, u32[]{:S(2)}) collective-permute-start(bf16[4,256,128]{2,1,0:T(8,128)(2,1)S(1)} %shard_map.112.own_ref), channel_id=1, source_target_pairs={{0,2},{2,0},{4,6},{6,4},{8,10},{10,8},{12,14},{14,12},{16,18},{18,... | collective-permute-start | bytes 786440 | tf_op jit(solution)/shard_map/ppermute | solution.py:25
  126.0 6.2 %collective-permute-start.17 = (bf16[4,256,128]{2,1,0:T(8,128)(2,1)S(1)}, bf16[4,256,128]{2,1,0:T(8,128)(2,1)S(1)}, u32[]{:S(2)}, u32[]{:S(2)}) collective-permute-start(bf16[4,256,128]{2,1,0:T(8,128)(2,1)S(1)} %shard_map.96.own_ref), channel_id=1, source_target_pairs={{0,2},{2,0},{4,6},{6,4},{8,10},{10,8},{12,14},{14,12},{16,18},{18,... | collective-permute-start | bytes 786440 | tf_op jit(solution)/shard_map/ppermute | solution.py:25
  127.1 10.1 %collective-permute-start.5 = (bf16[4,256,128]{2,1,0:T(8,128)(2,1)S(1)}, bf16[4,256,128]{2,1,0:T(8,128)(2,1)S(1)}, u32[]{:S(2)}, u32[]{:S(2)}) collective-permute-start(bf16[4,256,128]{2,1,0:T(8,128)(2,1)S(1)} %shard_map.85.own_ref), channel_id=1, source_target_pairs={{0,4},{2,6},{4,0},{6,2},{8,12},{10,14},{12,8},{14,10},{16,20},{18,... | collective-permute-start | bytes 786440 | tf_op jit(solution)/shard_map/ppermute | solution.py:25
  129.1 12.8 %collective-permute-start.14 = (bf16[4,256,128]{2,1,0:T(8,128)(2,1)S(1)}, bf16[4,256,128]{2,1,0:T(8,128)(2,1)S(1)}, u32[]{:S(2)}, u32[]{:S(2)}) collective-permute-start(bf16[4,256,128]{2,1,0:T(8,128)(2,1)S(1)} %shard_map.93.own_ref), channel_id=1, source_target_pairs={{0,4},{2,6},{4,0},{6,2},{8,12},{10,14},{12,8},{14,10},{16,20},{18,... | collective-permute-start | bytes 786440 | tf_op jit(solution)/shard_map/ppermute | solution.py:25
  130.2 17.4 %collective-permute-start.22 = (bf16[4,256,128]{2,1,0:T(8,128)(2,1)S(1)}, bf16[4,256,128]{2,1,0:T(8,128)(2,1)S(1)}, u32[]{:S(2)}, u32[]{:S(2)}) collective-permute-start(bf16[4,256,128]{2,1,0:T(8,128)(2,1)S(1)} %shard_map.100.own_ref), channel_id=1, source_target_pairs={{0,4},{2,6},{4,0},{6,2},{8,12},{10,14},{12,8},{14,10},{16,20},{18,... | collective-permute-start | bytes 786440 | tf_op jit(solution)/shard_map/ppermute | solution.py:25
  132.2 20.0 %collective-permute-start.30 = (bf16[4,256,128]{2,1,0:T(8,128)(2,1)S(1)}, bf16[4,256,128]{2,1,0:T(8,128)(2,1)S(1)}, u32[]{:S(2)}, u32[]{:S(2)}) collective-permute-start(bf16[4,256,128]{2,1,0:T(8,128)(2,1)S(1)} %shard_map.108.own_ref), channel_id=1, source_target_pairs={{0,4},{2,6},{4,0},{6,2},{8,12},{10,14},{12,8},{14,10},{16,20},{18,... | collective-permute-start | bytes 786440 | tf_op jit(solution)/shard_map/ppermute | solution.py:25
  133.3 32.4 %collective-permute-start.34 = (bf16[4,256,128]{2,1,0:T(8,128)(2,1)S(1)}, bf16[4,256,128]{2,1,0:T(8,128)(2,1)S(1)}, u32[]{:S(2)}, u32[]{:S(2)}) collective-permute-start(bf16[4,256,128]{2,1,0:T(8,128)(2,1)S(1)} %shard_map.113), channel_id=1, source_target_pairs={{0,16},{2,18},{4,20},{6,22},{8,24},{10,26},{12,28},{14,30},{16,0},... | collective-permute-start | bytes 786440 | tf_op jit(solution)/shard_map/ppermute | solution.py:25
  137.2 34.1 %collective-permute-start.26 = (bf16[4,256,128]{2,1,0:T(8,128)(2,1)S(1)}, bf16[4,256,128]{2,1,0:T(8,128)(2,1)S(1)}, u32[]{:S(2)}, u32[]{:S(2)}) collective-permute-start(bf16[4,256,128]{2,1,0:T(8,128)(2,1)S(1)} %shard_map.105), channel_id=1, source_target_pairs={{0,16},{2,18},{4,20},{6,22},{8,24},{10,26},{12,28},{14,30},{16,0},... | collective-permute-start | bytes 786440 | tf_op jit(solution)/shard_map/ppermute | solution.py:25
  141.9 34.9 %collective-permute-start.18 = (bf16[4,256,128]{2,1,0:T(8,128)(2,1)S(1)}, bf16[4,256,128]{2,1,0:T(8,128)(2,1)S(1)}, u32[]{:S(2)}, u32[]{:S(2)}) collective-permute-start(bf16[4,256,128]{2,1,0:T(8,128)(2,1)S(1)} %shard_map.97), channel_id=1, source_target_pairs={{0,16},{2,18},{4,20},{6,22},{8,24},{10,26},{12,28},{14,30},{16,0},... | collective-permute-start | bytes 786440 | tf_op jit(solution)/shard_map/ppermute | solution.py:25
  147.6 33.7 %collective-permute-start.10 = (bf16[4,256,128]{2,1,0:T(8,128)(2,1)S(1)}, bf16[4,256,128]{2,1,0:T(8,128)(2,1)S(1)}, u32[]{:S(2)}, u32[]{:S(2)}) collective-permute-start(bf16[4,256,128]{2,1,0:T(8,128)(2,1)S(1)} %shard_map.90), channel_id=1, source_target_pairs={{0,16},{2,18},{4,20},{6,22},{8,24},{10,26},{12,28},{14,30},{16,0},... | collective-permute-start | bytes 786440 | tf_op jit(solution)/shard_map/ppermute | solution.py:25
  151.2 14.4 %copy-start.2 = (bf16[1,1,4,256,256]{4,3,2,1,0:T(8,128)(2,1)S(1)}, bf16[1,1,4,256,256]{4,3,2,1,0:T(8,128)(2,1)}, u32[]{:S(2)}) copy-start(bf16[1,1,4,256,256]{4,3,2,1,0:T(8,128)(2,1)} %one_ref.9) | copy-start | bytes 1572868
  151.2 14.4 %copy-start.3 = (bf16[1,1,4,256,256]{4,3,2,1,0:T(8,128)(2,1)S(1)}, bf16[1,1,4,256,256]{4,3,2,1,0:T(8,128)(2,1)}, u32[]{:S(2)}) copy-start(bf16[1,1,4,256,256]{4,3,2,1,0:T(8,128)(2,1)} %two_ref.9) | copy-start | bytes 1572868

commit v3 on v2

--- a/solution.py
+++ b/solution.py
@@ -10,14 +10,14 @@
 VMEM = pl.BlockSpec(memory_space=pltpu.VMEM)
 HBM = pl.BlockSpec(memory_space=pltpu.HBM)
 ORDER = (
-    (2, 0, 0), (1, 0, 0), (2, 0, 2), (3, 0, 0), (1, 0, 2), (2, 0, 3),
-    (3, 2, 0), (1, 0, 3), (2, 0, 1), (2, 1, 0), (2, 2, 0), (1, 1, 2),
-    (1, 1, 0), (2, 1, 2), (1, 0, 1), (1, 2, 2), (2, 1, 3), (1, 1, 3),
-    (2, 2, 2), (1, 2, 0), (2, 1, 1), (2, 3, 0), (2, 3, 2), (1, 1, 1),
-    (3, 1, 0), (2, 2, 3), (1, 2, 3), (1, 3, 0), (1, 3, 2), (2, 3, 3),
-    (1, 2, 1), (2, 2, 1), (1, 3, 3), (2, 3, 1), (1, 4, 2), (1, 3, 1),
-    (1, 4, 3), (0, 0, 2), (1, 4, 0), (0, 0, 3), (0, 0, 0), (1, 4, 1),
-    (0, 0, 1),
+    (2, 0, 2), (1, 0, 0), (2, 0, 1), (1, 0, 1), (3, 0, 0), (2, 0, 3),
+    (1, 1, 0), (2, 0, 0), (2, 1, 1), (1, 0, 2), (1, 0, 3), (2, 2, 1),
+    (2, 1, 2), (1, 1, 1), (1, 2, 0), (3, 2, 0), (2, 2, 2), (1, 1, 2),
+    (2, 1, 0), (2, 1, 3), (2, 3, 2), (1, 2, 1), (1, 1, 3), (3, 1, 0),
+    (2, 3, 1), (1, 3, 0), (2, 2, 0), (1, 2, 2), (1, 3, 1), (2, 3, 0),
+    (1, 2, 3), (2, 2, 3), (1, 3, 2), (2, 3, 3), (1, 4, 0), (1, 3, 3),
+    (1, 4, 1), (0, 0, 0), (0, 0, 1), (1, 4, 2), (0, 0, 2), (1, 4, 3),
+    (0, 0, 3),
 )
 
 
@@ -108,34 +108,50 @@
     )(table, own, partner, weights)
 
 
-def target(sibling, distant, one, two, chunk, shape, held):
+def target(sibling, distant, one, two, chunk, shape, ready):
     nodes, leaf, width = sibling.shape
 
-    def kernel(a_ref, b_ref, one_ref, two_ref, *refs):
-        o_ref, z_ref, sem = refs[-3:]
+    def product(a_ref, b_ref, one_ref, two_ref, z_ref, n):
+        total = dot(one_ref[0, 0, n], a_ref[n]) + dot(two_ref[0, 0, n], b_ref[n])
+        z_ref[n] = total.astype(z_ref.dtype)
+
+    def early(*refs):
+        for n in range(nodes):
+            product(*refs, n)
+
+    def last(*refs):
+        o_ref, z_ref, sem, ready_sem = refs[-4:]
         copies = []
-        for n in range(nodes):
-            total = dot(one_ref[0, 0, n], a_ref[n]) + dot(two_ref[0, 0, n], b_ref[n])
-            z_ref[n] = total.astype(z_ref.dtype)
+        for i, (k, _) in enumerate(ready):
+            for n in range(nodes):
+                piece = o_ref.at[0, 0, pl.ds(n * leaf, leaf), pl.ds(k * width, width)]
+                copy = pltpu.make_async_copy(refs[4 + i].at[n], piece, ready_sem.at[i, n])
+                copies.append(copy)
+                copy.start()
+        for n in range(nodes):
+            product(*refs[:4], z_ref, n)
             piece = o_ref.at[0, 0, pl.ds(n * leaf, leaf), pl.ds(chunk * width, width)]
-            copies.append(pltpu.make_async_copy(z_ref.at[n], piece, sem.at[n]))
-            copies[n].start()
+            copy = pltpu.make_async_copy(z_ref.at[n], piece, sem.at[n])
+            copies.append(copy)
+            copy.start()
         for copy in copies:
             copy.wait()
 
     args = (sibling, distant, one, two)
-    specs = [VMEM] * 4
-    alias = {}
-    if held is not None:
-        args += (held,)
-        specs.append(HBM)
-        alias = {4: 0}
-    return pl.pallas_call(
-        kernel, out_shape=jax.ShapeDtypeStruct(shape, jnp.bfloat16),
-        in_specs=specs, out_specs=HBM, input_output_aliases=alias,
+    if len(ready) < CHUNKS - 1:
+        return pl.pallas_call(
+            early, out_shape=jax.ShapeDtypeStruct(sibling.shape, jnp.bfloat16),
+            in_specs=[VMEM] * 4, out_specs=VMEM,
+            cost_estimate=cost(2, sibling.shape), compiler_params=small(),
+        )(*args)
+    args += tuple(value for _, value in ready)
+    return pl.pallas_call(
+        last, out_shape=jax.ShapeDtypeStruct(shape, jnp.bfloat16),
+        in_specs=[VMEM] * len(args), out_specs=HBM,
         scratch_shapes=[
             pltpu.VMEM((nodes, leaf, width), jnp.bfloat16),
             pltpu.SemaphoreType.DMA((nodes,)),
+            pltpu.SemaphoreType.DMA((len(ready), nodes)),
         ],
         cost_estimate=cost(2, sibling.shape), compiler_params=small(),
     )(*args)
@@ -149,15 +165,16 @@
     top = lax.axis_size("grp").bit_length() - 1
     sources = {1: source_one, 2: source_two}
     value, moved = {}, {}
-    out = None
+    out, ready = None, []
     for step in ORDER:
         level, stage, k = step
         axis, bit = "half", 0
         sent = None
         if level == 0:
             out = target(
-                value[1, k], moved[2, k], target_one, target_two, k, shape, out
+                value[1, k], moved[2, k], target_one, target_two, k, shape, ready
             )
+            ready.append((k, out))
         elif level == 3:
             sent = pairing if stage == 2 else sections_one[:, :, stage + 1 : stage + 2]
         elif stage == 0:
@@ -175,9 +192,7 @@
             )
             axis, bit = "grp", top - 2 - stage if stage < 3 else top - 1
         elif stage == 1:
-            sent = value[1, k] = advance(
-                value[1, k], moved[1, k], sections_one, 0, pairing, 0, 0
-            )
+            sent = value[1, k] = advance(value[1, k], moved[1, k], sections_one, 0, pairing, 0, 0)
         elif stage == 2:
             sent = value[1, k] = moved[1, k]
             axis, bit = "grp", top - 2

time: 183 us -> 183 us (level)
  waiting for transfers between devices: 115 us -> 117 us
  Pallas kernels: 19.2 us -> 17.3 us
    ppermute x35, waiting for transfers between devices: 115 us -> 117 us  [swapped(): lax.ppermute(value, axis, [(i, i ^ 1 << bit) for i in range(lax.axis_size...]
    pallas_call x4, Pallas kernels: 4.35 us -> 2.47 us  [the longest x3 1.28 us: target(): pl.pallas_call(early, out_shape=jax.ShapeDtypeStruct(sibling.shape, jnp.b...]
  transfers between devices with their start and end apart: 35 -> 35, of which waited for: 21 -> 21; matrix products, arithmetic and copies ran while one was open for 0% -> 0% of each run, Pallas kernels for 9% -> 8%
where the time goes in v3:
time: 183 us
  waiting for transfers between devices  117 us (64%)
  starting transfers between devices  47.7 us (26%)
  Pallas kernels  17.3 us (9%)
    ppermute x35, waiting for transfers between devices, swapped(): lax.ppermute(value, axis, [(i, i ^ 1 << bit) for i in range(lax.axis_size...  117 us
    ppermute x35, starting transfers between devices, swapped(): lax.ppermute(value, axis, [(i, i ^ 1 << bit) for i in range(lax.axis_size...  47.7 us
    pallas_call x24, Pallas kernels, advance(): pl.pallas_call(kernel, out_shape=jax.ShapeDtypeStruct(own.shape, own.dtyp...  10.9 us
  transfers between devices with their start and end apart: 35, of which 21 were waited for; matrix products, arithmetic and copies ran while one was open for 0% of the time, Pallas kernels for 8%

profile of v3, /device:TPU:0, one launch (start us, length us, event | category | flops | bytes accessed | tf_op | source)
XLA Modules:
  0.0 182.6 jit_solution(605910704473167689)
XLA Ops:
  0.0 2.0 %shard_map.82 = (bf16[4,256,128]{2,1,0:T(8,128)(2,1)S(1)}, bf16[1,1,1024,512]{3,2,1,0:T(8,128)(2,1)S(1)}, bf16[1,1,4,256,256]{4,3,2,1,0:T(8,128)(2,1)S(1)}, bf16[1,1,4,256,256]{4,3,2,1,0:T(8,128)(2,1)S(1)}) custom-call(bf16[1,1,1024,512]{3,2,1,0:T(8,128)(2,1)} %x_ref.1, bf16[1,1,4,256,256]{4,3,2,1,0:T(8,128)(2,1)} %one_ref.1, ...), custom_call_target="tpu_custom_call" | custom-call | flops 67108864 | bytes 1048576 | tf_op jit(solution)/shard_map/pallas_call | solution.py:72
  2.3 4.1 %collective-permute-start.1 = (bf16[4,256,128]{2,1,0:T(8,128)(2,1)S(1)}, bf16[4,256,128]{2,1,0:T(8,128)(2,1)S(1)}, u32[]{:S(2)}, u32[]{:S(2)}) collective-permute-start(bf16[4,256,128]{2,1,0:T(8,128)(2,1)S(1)} %shard_map.83.own_ref), channel_id=1, source_target_pairs={{0,16},{2,18},{4,20},{6,22},{8,24},{10,26},{12,28},{14,30},{16,0},... | collective-permute-start | bytes 786440 | tf_op jit(solution)/shard_map/ppermute | solution.py:25
  7.1 3.0 %collective-permute-start.19 = (bf16[4,256,128]{2,1,0:T(8,128)(2,1)S(1)}, bf16[4,256,128]{2,1,0:T(8,128)(2,1)S(1)}, u32[]{:S(2)}, u32[]{:S(2)}) collective-permute-start(bf16[4,256,128]{2,1,0:T(8,128)(2,1)S(1)} %shard_map.100.own_ref), channel_id=1, source_target_pairs={{0,16},{2,18},{4,20},{6,22},{8,24},{10,26},{12,28},{14,30},{16,0},... | collective-permute-start | bytes 786440 | tf_op jit(solution)/shard_map/ppermute | solution.py:25
  10.7 2.0 %collective-permute-start.7 = (bf16[4,256,128]{2,1,0:T(8,128)(2,1)S(1)}, bf16[4,256,128]{2,1,0:T(8,128)(2,1)S(1)}, u32[]{:S(2)}, u32[]{:S(2)}) collective-permute-start(bf16[4,256,128]{2,1,0:T(8,128)(2,1)S(1)} %shard_map.87.own_ref), channel_id=1, source_target_pairs={{0,8},{2,10},{4,12},{6,14},{8,0},{10,2},{12,4},{14,6},{16,24},{18,... | collective-permute-start | bytes 786440 | tf_op jit(solution)/shard_map/ppermute | solution.py:25
  13.3 22.8 %collective-permute-done.1.partner_ref = bf16[4,256,128]{2,1,0:T(8,128)(2,1)S(1)} collective-permute-done((bf16[4,256,128]{2,1,0:T(8,128)(2,1)S(1)}, bf16[4,256,128]{2,1,0:T(8,128)(2,1)S(1)}, u32[]{:S(2)}, u32[]{:S(2)}) %collective-permute-start.1) | collective-permute-done | bytes 262176 | tf_op jit(solution)/shard_map/ppermute | solution.py:25
  36.0 1.8 collective-permute-start
  38.3 3.4 %collective-permute-done.11.partner_ref = bf16[4,256,128]{2,1,0:T(8,128)(2,1)S(1)} collective-permute-done((bf16[4,256,128]{2,1,0:T(8,128)(2,1)S(1)}, bf16[4,256,128]{2,1,0:T(8,128)(2,1)S(1)}, u32[]{:S(2)}, u32[]{:S(2)}) %collective-permute-start.11) | collective-permute-done | bytes 262176 | tf_op jit(solution)/shard_map/ppermute | solution.py:25
  42.1 2.1 %collective-permute-start.23 = (bf16[4,256,128]{2,1,0:T(8,128)(2,1)S(1)}, bf16[4,256,128]{2,1,0:T(8,128)(2,1)S(1)}, u32[]{:S(2)}, u32[]{:S(2)}) collective-permute-start(bf16[4,256,128]{2,1,0:T(8,128)(2,1)S(1)} %shard_map.104.own_ref), channel_id=1, source_target_pairs={{0,8},{2,10},{4,12},{6,14},{8,0},{10,2},{12,4},{14,6},{16,24},{18,... | collective-permute-start | bytes 786440 | tf_op jit(solution)/shard_map/ppermute | solution.py:25
  44.2 3.2 %collective-permute-done.19.partner_ref = bf16[4,256,128]{2,1,0:T(8,128)(2,1)S(1)} collective-permute-done((bf16[4,256,128]{2,1,0:T(8,128)(2,1)S(1)}, bf16[4,256,128]{2,1,0:T(8,128)(2,1)S(1)}, u32[]{:S(2)}, u32[]{:S(2)}) %collective-permute-start.19) | collective-permute-done | bytes 262176 | tf_op jit(solution)/shard_map/ppermute | solution.py:25
  47.4 4.8 %collective-permute-done.27.partner_ref = bf16[4,256,128]{2,1,0:T(8,128)(2,1)S(1)} collective-permute-done((bf16[4,256,128]{2,1,0:T(8,128)(2,1)S(1)}, bf16[4,256,128]{2,1,0:T(8,128)(2,1)S(1)}, u32[]{:S(2)}, u32[]{:S(2)}) %collective-permute-start.27) | collective-permute-done | bytes 262176 | tf_op jit(solution)/shard_map/ppermute | solution.py:25
  52.1 1.5 collective-permute-start.2
  54.4 3.4 %collective-permute-done.15.partner_ref = bf16[4,256,128]{2,1,0:T(8,128)(2,1)S(1)} collective-permute-done((bf16[4,256,128]{2,1,0:T(8,128)(2,1)S(1)}, bf16[4,256,128]{2,1,0:T(8,128)(2,1)S(1)}, u32[]{:S(2)}, u32[]{:S(2)}) %collective-permute-start.15) | collective-permute-done | bytes 262176 | tf_op jit(solution)/shard_map/ppermute | solution.py:25
  57.7 1.5 collective-permute-start.4
  59.7 3.6 %collective-permute-done.23.partner_ref = bf16[4,256,128]{2,1,0:T(8,128)(2,1)S(1)} collective-permute-done((bf16[4,256,128]{2,1,0:T(8,128)(2,1)S(1)}, bf16[4,256,128]{2,1,0:T(8,128)(2,1)S(1)}, u32[]{:S(2)}, u32[]{:S(2)}) %collective-permute-start.23) | collective-permute-done | bytes 262176 | tf_op jit(solution)/shard_map/ppermute | solution.py:25
  63.4 1.5 collective-permute-start.20
  65.3 3.5 %collective-permute-done.31.partner_ref = bf16[4,256,128]{2,1,0:T(8,128)(2,1)S(1)} collective-permute-done((bf16[4,256,128]{2,1,0:T(8,128)(2,1)S(1)}, bf16[4,256,128]{2,1,0:T(8,128)(2,1)S(1)}, u32[]{:S(2)}, u32[]{:S(2)}) %collective-permute-start.31) | collective-permute-done | bytes 262176 | tf_op jit(solution)/shard_map/ppermute | solution.py:25
  68.9 1.5 collective-permute-start.28
  70.9 1.6 collective-permute-start.8
  72.9 0.6 collective-permute-start.16
  73.5 21.5 %collective-permute-done.20.own_ref = bf16[4,256,128]{2,1,0:T(8,128)(2,1)S(1)} collective-permute-done((bf16[4,256,128]{2,1,0:T(8,128)(2,1)S(1)}, bf16[4,256,128]{2,1,0:T(8,128)(2,1)S(1)}, u32[]{:S(2)}, u32[]{:S(2)}) %collective-permute-start.20) | collective-permute-done | bytes 262176 | tf_op jit(solution)/shard_map/ppermute | solution.py:25
  95.0 1.5 collective-permute-start.6
  97.0 3.6 %collective-permute-done.28.own_ref = bf16[4,256,128]{2,1,0:T(8,128)(2,1)S(1)} collective-permute-done((bf16[4,256,128]{2,1,0:T(8,128)(2,1)S(1)}, bf16[4,256,128]{2,1,0:T(8,128)(2,1)S(1)}, u32[]{:S(2)}, u32[]{:S(2)}) %collective-permute-start.28) | collective-permute-done | bytes 262176 | tf_op jit(solution)/shard_map/ppermute | solution.py:25
  100.6 1.6 collective-permute-start.24
  103.2 0.7 collective-permute-start.3
  103.8 4.4 %collective-permute-done.24.partner_ref = bf16[4,256,128]{2,1,0:T(8,128)(2,1)S(1)} collective-permute-done((bf16[4,256,128]{2,1,0:T(8,128)(2,1)S(1)}, bf16[4,256,128]{2,1,0:T(8,128)(2,1)S(1)}, u32[]{:S(2)}, u32[]{:S(2)}) %collective-permute-start.24) | collective-permute-done | bytes 262176 | tf_op jit(solution)/shard_map/ppermute | solution.py:25
  108.2 2.2 %collective-permute-start.13 = (bf16[4,256,128]{2,1,0:T(8,128)(2,1)S(1)}, bf16[4,256,128]{2,1,0:T(8,128)(2,1)S(1)}, u32[]{:S(2)}, u32[]{:S(2)}) collective-permute-start(bf16[4,256,128]{2,1,0:T(8,128)(2,1)S(1)} %collective-permute-done.12.own_ref), channel_id=1, source_target_pairs={{0,8},{2,10},{4,12},{6,14},{8,0},{10,2},{12,4},{14,6},{16,24},{18,... | collective-permute-start | bytes 786440 | tf_op jit(solution)/shard_map/ppermute | solution.py:25
  110.5 0.6 collective-permute-done.32.partner_ref
  111.0 2.3 %collective-permute-start.21 = (bf16[4,256,128]{2,1,0:T(8,128)(2,1)S(1)}, bf16[4,256,128]{2,1,0:T(8,128)(2,1)S(1)}, u32[]{:S(2)}, u32[]{:S(2)}) collective-permute-start(bf16[4,256,128]{2,1,0:T(8,128)(2,1)S(1)} %collective-permute-done.20.own_ref), channel_id=1, source_target_pairs={{0,8},{2,10},{4,12},{6,14},{8,0},{10,2},{12,4},{14,6},{16,24},{18,... | collective-permute-start | bytes 786440 | tf_op jit(solution)/shard_map/ppermute | solution.py:25
  113.8 3.8 %collective-permute-done.13.partner_ref = bf16[4,256,128]{2,1,0:T(8,128)(2,1)S(1)} collective-permute-done((bf16[4,256,128]{2,1,0:T(8,128)(2,1)S(1)}, bf16[4,256,128]{2,1,0:T(8,128)(2,1)S(1)}, u32[]{:S(2)}, u32[]{:S(2)}) %collective-permute-start.13) | collective-permute-done | bytes 262176 | tf_op jit(solution)/shard_map/ppermute | solution.py:25
  118.1 4.7 %collective-permute-done.21.partner_ref = bf16[4,256,128]{2,1,0:T(8,128)(2,1)S(1)} collective-permute-done((bf16[4,256,128]{2,1,0:T(8,128)(2,1)S(1)}, bf16[4,256,128]{2,1,0:T(8,128)(2,1)S(1)}, u32[]{:S(2)}, u32[]{:S(2)}) %collective-permute-start.21) | collective-permute-done | bytes 262176 | tf_op jit(solution)/shard_map/ppermute | solution.py:25
  123.2 2.4 %collective-permute-done.29.partner_ref = bf16[4,256,128]{2,1,0:T(8,128)(2,1)S(1)} collective-permute-done((bf16[4,256,128]{2,1,0:T(8,128)(2,1)S(1)}, bf16[4,256,128]{2,1,0:T(8,128)(2,1)S(1)}, u32[]{:S(2)}, u32[]{:S(2)}) %collective-permute-start.29) | collective-permute-done | bytes 262176 | tf_op jit(solution)/shard_map/ppermute | solution.py:25
  126.0 0.6 collective-permute-start.33
  127.1 1.6 collective-permute-start.5
  129.1 0.6 collective-permute-start.14
  130.2 1.6 collective-permute-start.22
  132.2 0.6 collective-permute-start.30
  133.3 3.3 %collective-permute-start.18 = (bf16[4,256,128]{2,1,0:T(8,128)(2,1)S(1)}, bf16[4,256,128]{2,1,0:T(8,128)(2,1)S(1)}, u32[]{:S(2)}, u32[]{:S(2)}) collective-permute-start(bf16[4,256,128]{2,1,0:T(8,128)(2,1)S(1)} %shard_map.98), channel_id=1, source_target_pairs={{0,16},{2,18},{4,20},{6,22},{8,24},{10,26},{12,28},{14,30},{16,0},... | collective-permute-start | bytes 786440 | tf_op jit(solution)/shard_map/ppermute | solution.py:25
  136.5 0.6 shard_map.107
  137.2 2.4 %collective-permute-start.26 = (bf16[4,256,128]{2,1,0:T(8,128)(2,1)S(1)}, bf16[4,256,128]{2,1,0:T(8,128)(2,1)S(1)}, u32[]{:S(2)}, u32[]{:S(2)}) collective-permute-start(bf16[4,256,128]{2,1,0:T(8,128)(2,1)S(1)} %shard_map.107), channel_id=1, source_target_pairs={{0,16},{2,18},{4,20},{6,22},{8,24},{10,26},{12,28},{14,30},{16,0},... | collective-permute-start | bytes 786440 | tf_op jit(solution)/shard_map/ppermute | solution.py:25
  140.0 1.9 %collective-permute-done.14.partner_ref = bf16[4,256,128]{2,1,0:T(8,128)(2,1)S(1)} collective-permute-done((bf16[4,256,128]{2,1,0:T(8,128)(2,1)S(1)}, bf16[4,256,128]{2,1,0:T(8,128)(2,1)S(1)}, u32[]{:S(2)}, u32[]{:S(2)}) %collective-permute-start.14) | collective-permute-done | bytes 262176 | tf_op jit(solution)/shard_map/ppermute | solution.py:25
  141.9 3.2 %collective-permute-start.34 = (bf16[4,256,128]{2,1,0:T(8,128)(2,1)S(1)}, bf16[4,256,128]{2,1,0:T(8,128)(2,1)S(1)}, u32[]{:S(2)}, u32[]{:S(2)}) collective-permute-start(bf16[4,256,128]{2,1,0:T(8,128)(2,1)S(1)} %shard_map.115), channel_id=1, source_target_pairs={{0,16},{2,18},{4,20},{6,22},{8,24},{10,26},{12,28},{14,30},{16,0},... | collective-permute-start | bytes 786440 | tf_op jit(solution)/shard_map/ppermute | solution.py:25
  145.6 2.0 %collective-permute-done.22.partner_ref = bf16[4,256,128]{2,1,0:T(8,128)(2,1)S(1)} collective-permute-done((bf16[4,256,128]{2,1,0:T(8,128)(2,1)S(1)}, bf16[4,256,128]{2,1,0:T(8,128)(2,1)S(1)}, u32[]{:S(2)}, u32[]{:S(2)}) %collective-permute-start.22) | collective-permute-done | bytes 262176 | tf_op jit(solution)/shard_map/ppermute | solution.py:25
  147.6 3.2 %collective-permute-start.10 = (bf16[4,256,128]{2,1,0:T(8,128)(2,1)S(1)}, bf16[4,256,128]{2,1,0:T(8,128)(2,1)S(1)}, u32[]{:S(2)}, u32[]{:S(2)}) collective-permute-start(bf16[4,256,128]{2,1,0:T(8,128)(2,1)S(1)} %shard_map.90), channel_id=1, source_target_pairs={{0,16},{2,18},{4,20},{6,22},{8,24},{10,26},{12,28},{14,30},{16,0},... | collective-permute-start | bytes 786440 | tf_op jit(solution)/shard_map/ppermute | solution.py:25
  152.7 13.0 %collective-permute-done.18.refs_1_ = bf16[4,256,128]{2,1,0:T(8,128)(2,1)S(1)} collective-permute-done((bf16[4,256,128]{2,1,0:T(8,128)(2,1)S(1)}, bf16[4,256,128]{2,1,0:T(8,128)(2,1)S(1)}, u32[]{:S(2)}, u32[]{:S(2)}) %collective-permute-start.18) | collective-permute-done | bytes 262176 | tf_op jit(solution)/shard_map/ppermute | solution.py:25
  166.1 5.2 %collective-permute-done.26.refs_1_ = bf16[4,256,128]{2,1,0:T(8,128)(2,1)S(1)} collective-permute-done((bf16[4,256,128]{2,1,0:T(8,128)(2,1)S(1)}, bf16[4,256,128]{2,1,0:T(8,128)(2,1)S(1)}, u32[]{:S(2)}, u32[]{:S(2)}) %collective-permute-start.26) | collective-permute-done | bytes 262176 | tf_op jit(solution)/shard_map/ppermute | solution.py:25
  171.7 5.2 %collective-permute-done.34.refs_1_ = bf16[4,256,128]{2,1,0:T(8,128)(2,1)S(1)} collective-permute-done((bf16[4,256,128]{2,1,0:T(8,128)(2,1)S(1)}, bf16[4,256,128]{2,1,0:T(8,128)(2,1)S(1)}, u32[]{:S(2)}, u32[]{:S(2)}) %collective-permute-start.34) | collective-permute-done | bytes 262176 | tf_op jit(solution)/shard_map/ppermute | solution.py:25
  177.3 3.9 %collective-permute-done.10.refs_1_ = bf16[4,256,128]{2,1,0:T(8,128)(2,1)S(1)} collective-permute-done((bf16[4,256,128]{2,1,0:T(8,128)(2,1)S(1)}, bf16[4,256,128]{2,1,0:T(8,128)(2,1)S(1)}, u32[]{:S(2)}, u32[]{:S(2)}) %collective-permute-start.10) | collective-permute-done | bytes 262176 | tf_op jit(solution)/shard_map/ppermute | solution.py:25
  181.2 1.2 shard_map.117
  (69 shorter events, 15.1 us)
Async XLA Ops:
  2.3 33.8 %collective-permute-start.1 = (bf16[4,256,128]{2,1,0:T(8,128)(2,1)S(1)}, bf16[4,256,128]{2,1,0:T(8,128)(2,1)S(1)}, u32[]{:S(2)}, u32[]{:S(2)}) collective-permute-start(bf16[4,256,128]{2,1,0:T(8,128)(2,1)S(1)} %shard_map.83.own_ref), channel_id=1, source_target_pairs={{0,16},{2,18},{4,20},{6,22},{8,24},{10,26},{12,28},{14,30},{16,0},... | collective-permute-start | bytes 786440 | tf_op jit(solution)/shard_map/ppermute | solution.py:25
  6.7 35.0 %collective-permute-start.11 = (bf16[4,256,128]{2,1,0:T(8,128)(2,1)S(1)}, bf16[4,256,128]{2,1,0:T(8,128)(2,1)S(1)}, u32[]{:S(2)}, u32[]{:S(2)}) collective-permute-start(bf16[4,256,128]{2,1,0:T(8,128)(2,1)S(1)} %shard_map.91.own_ref), channel_id=1, source_target_pairs={{0,16},{2,18},{4,20},{6,22},{8,24},{10,26},{12,28},{14,30},{16,0},... | collective-permute-start | bytes 786440 | tf_op jit(solution)/shard_map/ppermute | solution.py:25
  7.1 40.3 %collective-permute-start.19 = (bf16[4,256,128]{2,1,0:T(8,128)(2,1)S(1)}, bf16[4,256,128]{2,1,0:T(8,128)(2,1)S(1)}, u32[]{:S(2)}, u32[]{:S(2)}) collective-permute-start(bf16[4,256,128]{2,1,0:T(8,128)(2,1)S(1)} %shard_map.100.own_ref), channel_id=1, source_target_pairs={{0,16},{2,18},{4,20},{6,22},{8,24},{10,26},{12,28},{14,30},{16,0},... | collective-permute-start | bytes 786440 | tf_op jit(solution)/shard_map/ppermute | solution.py:25
  10.3 25.7 %copy-start.4 = (s32[2,3,1,1,4]{4,3,2,1,0:T(1,128)S(1)}, s32[2,3,1,1,4]{4,3,2,1,0:T(1,128)}, u32[]{:S(2)}) copy-start(s32[2,3,1,1,4]{4,3,2,1,0:T(1,128)} %table_ref.31) | copy-start | bytes 292
  10.3 27.5 %copy-start.1 = (bf16[1,1,3,4,256,512]{5,4,3,2,1,0:T(8,128)(2,1)S(1)}, bf16[1,1,3,4,256,512]{5,4,3,2,1,0:T(8,128)(2,1)}, u32[]{:S(2)}) copy-start(bf16[1,1,3,4,256,512]{5,4,3,2,1,0:T(8,128)(2,1)} %w_ref.28) | copy-start | bytes 9437188
  10.3 41.8 %collective-permute-start.27 = (bf16[4,256,128]{2,1,0:T(8,128)(2,1)S(1)}, bf16[4,256,128]{2,1,0:T(8,128)(2,1)S(1)}, u32[]{:S(2)}, u32[]{:S(2)}) collective-permute-start(bf16[4,256,128]{2,1,0:T(8,128)(2,1)S(1)} %shard_map.109.own_ref), channel_id=1, source_target_pairs={{0,16},{2,18},{4,20},{6,22},{8,24},{10,26},{12,28},{14,30},{16,0},... | collective-permute-start | bytes 786440 | tf_op jit(solution)/shard_map/ppermute | solution.py:25
  10.7 43.0 %collective-permute-start.7 = (bf16[4,256,128]{2,1,0:T(8,128)(2,1)S(1)}, bf16[4,256,128]{2,1,0:T(8,128)(2,1)S(1)}, u32[]{:S(2)}, u32[]{:S(2)}) collective-permute-start(bf16[4,256,128]{2,1,0:T(8,128)(2,1)S(1)} %shard_map.87.own_ref), channel_id=1, source_target_pairs={{0,8},{2,10},{4,12},{6,14},{8,0},{10,2},{12,4},{14,6},{16,24},{18,... | collective-permute-start | bytes 786440 | tf_op jit(solution)/shard_map/ppermute | solution.py:25
  36.0 6.1 %collective-permute-start = (s32[2,3,1,1,4]{4,3,2,1,0:T(1,128)S(1)}, s32[2,3,1,1,4]{4,3,2,1,0:T(1,128)S(1)}, u32[]{:S(2)}, u32[]{:S(2)}) collective-permute-start(s32[2,3,1,1,4]{4,3,2,1,0:T(1,128)S(1)} %copy-done.4), channel_id=1, source_target_pairs={{0,1},{1,0},{2,3},{3,2},{4,5},{5,4},{6,7},{7,6},{8,9},{9,8},{10,11... | collective-permute-start | bytes 296 | tf_op jit(solution)/shard_map/ppermute | solution.py:25
  41.6 16.1 %collective-permute-start.15 = (bf16[4,256,128]{2,1,0:T(8,128)(2,1)S(1)}, bf16[4,256,128]{2,1,0:T(8,128)(2,1)S(1)}, u32[]{:S(2)}, u32[]{:S(2)}) collective-permute-start(bf16[4,256,128]{2,1,0:T(8,128)(2,1)S(1)} %shard_map.95.own_ref), channel_id=1, source_target_pairs={{0,8},{2,10},{4,12},{6,14},{8,0},{10,2},{12,4},{14,6},{16,24},{18,... | collective-permute-start | bytes 786440 | tf_op jit(solution)/shard_map/ppermute | solution.py:25
  42.1 21.3 %collective-permute-start.23 = (bf16[4,256,128]{2,1,0:T(8,128)(2,1)S(1)}, bf16[4,256,128]{2,1,0:T(8,128)(2,1)S(1)}, u32[]{:S(2)}, u32[]{:S(2)}) collective-permute-start(bf16[4,256,128]{2,1,0:T(8,128)(2,1)S(1)} %shard_map.104.own_ref), channel_id=1, source_target_pairs={{0,8},{2,10},{4,12},{6,14},{8,0},{10,2},{12,4},{14,6},{16,24},{18,... | collective-permute-start | bytes 786440 | tf_op jit(solution)/shard_map/ppermute | solution.py:25
  47.4 21.5 %collective-permute-start.31 = (bf16[4,256,128]{2,1,0:T(8,128)(2,1)S(1)}, bf16[4,256,128]{2,1,0:T(8,128)(2,1)S(1)}, u32[]{:S(2)}, u32[]{:S(2)}) collective-permute-start(bf16[4,256,128]{2,1,0:T(8,128)(2,1)S(1)} %get-tuple-element.12.own_ref), channel_id=1, source_target_pairs={{0,8},{2,10},{4,12},{6,14},{8,0},{10,2},{12,4},{14,6},{16,24},{18,... | collective-permute-start | bytes 786440 | tf_op jit(solution)/shard_map/ppermute | solution.py:25
  52.1 18.8 %collective-permute-start.2 = (bf16[4,256,128]{2,1,0:T(8,128)(2,1)S(1)}, bf16[4,256,128]{2,1,0:T(8,128)(2,1)S(1)}, u32[]{:S(2)}, u32[]{:S(2)}) collective-permute-start(bf16[4,256,128]{2,1,0:T(8,128)(2,1)S(1)} %shard_map.84), channel_id=1, source_target_pairs={{0,1},{1,0},{2,3},{3,2},{4,5},{5,4},{6,7},{7,6},{8,9},{9,8},{10,11... | collective-permute-start | bytes 786440 | tf_op jit(solution)/shard_map/ppermute | solution.py:25
  53.7 19.3 %collective-permute-start.12 = (bf16[4,256,128]{2,1,0:T(8,128)(2,1)S(1)}, bf16[4,256,128]{2,1,0:T(8,128)(2,1)S(1)}, u32[]{:S(2)}, u32[]{:S(2)}) collective-permute-start(bf16[4,256,128]{2,1,0:T(8,128)(2,1)S(1)} %shard_map.92), channel_id=1, source_target_pairs={{0,1},{1,0},{2,3},{3,2},{4,5},{5,4},{6,7},{7,6},{8,9},{9,8},{10,11... | collective-permute-start | bytes 786440 | tf_op jit(solution)/shard_map/ppermute | solution.py:25
  57.7 12.7 %copy-start = (bf16[1,1,3,4,256,512]{5,4,3,2,1,0:T(8,128)(2,1)S(1)}, bf16[1,1,3,4,256,512]{5,4,3,2,1,0:T(8,128)(2,1)}, u32[]{:S(2)}) copy-start(bf16[1,1,3,4,256,512]{5,4,3,2,1,0:T(8,128)(2,1)} %w_ref.31) | copy-start | bytes 9437188
  57.7 68.3 %collective-permute-start.4 = (bf16[1,1,1,4,256,512]{5,4,3,2,1,0:T(8,128)(2,1)S(1)}, bf16[1,1,1,4,256,512]{5,4,3,2,1,0:T(8,128)(2,1)S(1)}, u32[]{:S(2)}, u32[]{:S(2)}) collective-permute-start(bf16[1,1,1,4,256,512]{5,4,3,2,1,0:T(8,128)(2,1)S(1)} %get-tuple-element.14), channel_id=1, source_target_pairs={{0,1},{1,0},{2,3},{3,2},{4,5},{5,4},{6,7},{7,6},{8,9},{9,8},{10,11... | collective-permute-start | bytes 3145736 | tf_op jit(solution)/shard_map/ppermute | solution.py:25
  63.4 31.7 %collective-permute-start.20 = (bf16[4,256,128]{2,1,0:T(8,128)(2,1)S(1)}, bf16[4,256,128]{2,1,0:T(8,128)(2,1)S(1)}, u32[]{:S(2)}, u32[]{:S(2)}) collective-permute-start(bf16[4,256,128]{2,1,0:T(8,128)(2,1)S(1)} %shard_map.101), channel_id=1, source_target_pairs={{0,1},{1,0},{2,3},{3,2},{4,5},{5,4},{6,7},{7,6},{8,9},{9,8},{10,11... | collective-permute-start | bytes 786440 | tf_op jit(solution)/shard_map/ppermute | solution.py:25
  68.9 31.7 %collective-permute-start.28 = (bf16[4,256,128]{2,1,0:T(8,128)(2,1)S(1)}, bf16[4,256,128]{2,1,0:T(8,128)(2,1)S(1)}, u32[]{:S(2)}, u32[]{:S(2)}) collective-permute-start(bf16[4,256,128]{2,1,0:T(8,128)(2,1)S(1)} %shard_map.110), channel_id=1, source_target_pairs={{0,1},{1,0},{2,3},{3,2},{4,5},{5,4},{6,7},{7,6},{8,9},{9,8},{10,11... | collective-permute-start | bytes 786440 | tf_op jit(solution)/shard_map/ppermute | solution.py:25
  70.9 31.8 %collective-permute-start.8 = (bf16[4,256,128]{2,1,0:T(8,128)(2,1)S(1)}, bf16[4,256,128]{2,1,0:T(8,128)(2,1)S(1)}, u32[]{:S(2)}, u32[]{:S(2)}) collective-permute-start(bf16[4,256,128]{2,1,0:T(8,128)(2,1)S(1)} %shard_map.88.own_ref), channel_id=1, source_target_pairs={{0,4},{2,6},{4,0},{6,2},{8,12},{10,14},{12,8},{14,10},{16,20},{18,... | collective-permute-start | bytes 786440 | tf_op jit(solution)/shard_map/ppermute | solution.py:25
  72.9 30.2 %collective-permute-start.16 = (bf16[4,256,128]{2,1,0:T(8,128)(2,1)S(1)}, bf16[4,256,128]{2,1,0:T(8,128)(2,1)S(1)}, u32[]{:S(2)}, u32[]{:S(2)}) collective-permute-start(bf16[4,256,128]{2,1,0:T(8,128)(2,1)S(1)} %shard_map.96.own_ref), channel_id=1, source_target_pairs={{0,4},{2,6},{4,0},{6,2},{8,12},{10,14},{12,8},{14,10},{16,20},{18,... | collective-permute-start | bytes 786440 | tf_op jit(solution)/shard_map/ppermute | solution.py:25
  95.0 38.2 %collective-permute-start.6 = (bf16[1,1,1,4,256,512]{5,4,3,2,1,0:T(8,128)(2,1)S(1)}, bf16[1,1,1,4,256,512]{5,4,3,2,1,0:T(8,128)(2,1)S(1)}, u32[]{:S(2)}, u32[]{:S(2)}) collective-permute-start(bf16[1,1,1,4,256,512]{5,4,3,2,1,0:T(8,128)(2,1)S(1)} %get-tuple-element.13), channel_id=1, source_target_pairs={{0,1},{1,0},{2,3},{3,2},{4,5},{5,4},{6,7},{7,6},{8,9},{9,8},{10,11... | collective-permute-start | bytes 3145736 | tf_op jit(solution)/shard_map/ppermute | solution.py:25
  100.6 7.6 %collective-permute-start.24 = (bf16[4,256,128]{2,1,0:T(8,128)(2,1)S(1)}, bf16[4,256,128]{2,1,0:T(8,128)(2,1)S(1)}, u32[]{:S(2)}, u32[]{:S(2)}) collective-permute-start(bf16[4,256,128]{2,1,0:T(8,128)(2,1)S(1)} %shard_map.105.own_ref), channel_id=1, source_target_pairs={{0,4},{2,6},{4,0},{6,2},{8,12},{10,14},{12,8},{14,10},{16,20},{18,... | collective-permute-start | bytes 786440 | tf_op jit(solution)/shard_map/ppermute | solution.py:25
  102.7 8.4 %collective-permute-start.32 = (bf16[4,256,128]{2,1,0:T(8,128)(2,1)S(1)}, bf16[4,256,128]{2,1,0:T(8,128)(2,1)S(1)}, u32[]{:S(2)}, u32[]{:S(2)}) collective-permute-start(bf16[4,256,128]{2,1,0:T(8,128)(2,1)S(1)} %shard_map.113.own_ref), channel_id=1, source_target_pairs={{0,4},{2,6},{4,0},{6,2},{8,12},{10,14},{12,8},{14,10},{16,20},{18,... | collective-permute-start | bytes 786440 | tf_op jit(solution)/shard_map/ppermute | solution.py:25
  103.2 10.2 %collective-permute-start.3 = (bf16[4,256,128]{2,1,0:T(8,128)(2,1)S(1)}, bf16[4,256,128]{2,1,0:T(8,128)(2,1)S(1)}, u32[]{:S(2)}, u32[]{:S(2)}) collective-permute-start(bf16[4,256,128]{2,1,0:T(8,128)(2,1)S(1)} %collective-permute-done.2.own_ref), channel_id=1, source_target_pairs={{0,8},{2,10},{4,12},{6,14},{8,0},{10,2},{12,4},{14,6},{16,24},{18,... | collective-permute-start | bytes 786440 | tf_op jit(solution)/shard_map/ppermute | solution.py:25
  108.2 9.4 %collective-permute-start.13 = (bf16[4,256,128]{2,1,0:T(8,128)(2,1)S(1)}, bf16[4,256,128]{2,1,0:T(8,128)(2,1)S(1)}, u32[]{:S(2)}, u32[]{:S(2)}) collective-permute-start(bf16[4,256,128]{2,1,0:T(8,128)(2,1)S(1)} %collective-permute-done.12.own_ref), channel_id=1, source_target_pairs={{0,8},{2,10},{4,12},{6,14},{8,0},{10,2},{12,4},{14,6},{16,24},{18,... | collective-permute-start | bytes 786440 | tf_op jit(solution)/shard_map/ppermute | solution.py:25
  111.0 11.7 %collective-permute-start.21 = (bf16[4,256,128]{2,1,0:T(8,128)(2,1)S(1)}, bf16[4,256,128]{2,1,0:T(8,128)(2,1)S(1)}, u32[]{:S(2)}, u32[]{:S(2)}) collective-permute-start(bf16[4,256,128]{2,1,0:T(8,128)(2,1)S(1)} %collective-permute-done.20.own_ref), channel_id=1, source_target_pairs={{0,8},{2,10},{4,12},{6,14},{8,0},{10,2},{12,4},{14,6},{16,24},{18,... | collective-permute-start | bytes 786440 | tf_op jit(solution)/shard_map/ppermute | solution.py:25
  113.3 12.2 %collective-permute-start.29 = (bf16[4,256,128]{2,1,0:T(8,128)(2,1)S(1)}, bf16[4,256,128]{2,1,0:T(8,128)(2,1)S(1)}, u32[]{:S(2)}, u32[]{:S(2)}) collective-permute-start(bf16[4,256,128]{2,1,0:T(8,128)(2,1)S(1)} %collective-permute-done.28.own_ref), channel_id=1, source_target_pairs={{0,8},{2,10},{4,12},{6,14},{8,0},{10,2},{12,4},{14,6},{16,24},{18,... | collective-permute-start | bytes 786440 | tf_op jit(solution)/shard_map/ppermute | solution.py:25
  117.6 9.5 %collective-permute-start.9 = (bf16[4,256,128]{2,1,0:T(8,128)(2,1)S(1)}, bf16[4,256,128]{2,1,0:T(8,128)(2,1)S(1)}, u32[]{:S(2)}, u32[]{:S(2)}) collective-permute-start(bf16[4,256,128]{2,1,0:T(8,128)(2,1)S(1)} %shard_map.89.own_ref), channel_id=1, source_target_pairs={{0,2},{2,0},{4,6},{6,4},{8,10},{10,8},{12,14},{14,12},{16,18},{18,... | collective-permute-start | bytes 786440 | tf_op jit(solution)/shard_map/ppermute | solution.py:25
  122.8 6.4 %collective-permute-start.17 = (bf16[4,256,128]{2,1,0:T(8,128)(2,1)S(1)}, bf16[4,256,128]{2,1,0:T(8,128)(2,1)S(1)}, u32[]{:S(2)}, u32[]{:S(2)}) collective-permute-start(bf16[4,256,128]{2,1,0:T(8,128)(2,1)S(1)} %shard_map.97.own_ref), channel_id=1, source_target_pairs={{0,2},{2,0},{4,6},{6,4},{8,10},{10,8},{12,14},{14,12},{16,18},{18,... | collective-permute-start | bytes 786440 | tf_op jit(solution)/shard_map/ppermute | solution.py:25
  125.6 4.6 %collective-permute-start.25 = (bf16[4,256,128]{2,1,0:T(8,128)(2,1)S(1)}, bf16[4,256,128]{2,1,0:T(8,128)(2,1)S(1)}, u32[]{:S(2)}, u32[]{:S(2)}) collective-permute-start(bf16[4,256,128]{2,1,0:T(8,128)(2,1)S(1)} %shard_map.106.own_ref), channel_id=1, source_target_pairs={{0,2},{2,0},{4,6},{6,4},{8,10},{10,8},{12,14},{14,12},{16,18},{18,... | collective-permute-start | bytes 786440 | tf_op jit(solution)/shard_map/ppermute | solution.py:25
  126.0 6.2 %collective-permute-start.33 = (bf16[4,256,128]{2,1,0:T(8,128)(2,1)S(1)}, bf16[4,256,128]{2,1,0:T(8,128)(2,1)S(1)}, u32[]{:S(2)}, u32[]{:S(2)}) collective-permute-start(bf16[4,256,128]{2,1,0:T(8,128)(2,1)S(1)} %shard_map.114.own_ref), channel_id=1, source_target_pairs={{0,2},{2,0},{4,6},{6,4},{8,10},{10,8},{12,14},{14,12},{16,18},{18,... | collective-permute-start | bytes 786440 | tf_op jit(solution)/shard_map/ppermute | solution.py:25
  127.1 10.1 %collective-permute-start.5 = (bf16[4,256,128]{2,1,0:T(8,128)(2,1)S(1)}, bf16[4,256,128]{2,1,0:T(8,128)(2,1)S(1)}, u32[]{:S(2)}, u32[]{:S(2)}) collective-permute-start(bf16[4,256,128]{2,1,0:T(8,128)(2,1)S(1)} %shard_map.85.own_ref), channel_id=1, source_target_pairs={{0,4},{2,6},{4,0},{6,2},{8,12},{10,14},{12,8},{14,10},{16,20},{18,... | collective-permute-start | bytes 786440 | tf_op jit(solution)/shard_map/ppermute | solution.py:25
  129.1 12.8 %collective-permute-start.14 = (bf16[4,256,128]{2,1,0:T(8,128)(2,1)S(1)}, bf16[4,256,128]{2,1,0:T(8,128)(2,1)S(1)}, u32[]{:S(2)}, u32[]{:S(2)}) collective-permute-start(bf16[4,256,128]{2,1,0:T(8,128)(2,1)S(1)} %shard_map.93.own_ref), channel_id=1, source_target_pairs={{0,4},{2,6},{4,0},{6,2},{8,12},{10,14},{12,8},{14,10},{16,20},{18,... | collective-permute-start | bytes 786440 | tf_op jit(solution)/shard_map/ppermute | solution.py:25
  130.2 17.4 %collective-permute-start.22 = (bf16[4,256,128]{2,1,0:T(8,128)(2,1)S(1)}, bf16[4,256,128]{2,1,0:T(8,128)(2,1)S(1)}, u32[]{:S(2)}, u32[]{:S(2)}) collective-permute-start(bf16[4,256,128]{2,1,0:T(8,128)(2,1)S(1)} %shard_map.102.own_ref), channel_id=1, source_target_pairs={{0,4},{2,6},{4,0},{6,2},{8,12},{10,14},{12,8},{14,10},{16,20},{18,... | collective-permute-start | bytes 786440 | tf_op jit(solution)/shard_map/ppermute | solution.py:25
  132.2 20.0 %collective-permute-start.30 = (bf16[4,256,128]{2,1,0:T(8,128)(2,1)S(1)}, bf16[4,256,128]{2,1,0:T(8,128)(2,1)S(1)}, u32[]{:S(2)}, u32[]{:S(2)}) collective-permute-start(bf16[4,256,128]{2,1,0:T(8,128)(2,1)S(1)} %shard_map.111.own_ref), channel_id=1, source_target_pairs={{0,4},{2,6},{4,0},{6,2},{8,12},{10,14},{12,8},{14,10},{16,20},{18,... | collective-permute-start | bytes 786440 | tf_op jit(solution)/shard_map/ppermute | solution.py:25
  133.3 32.4 %collective-permute-start.18 = (bf16[4,256,128]{2,1,0:T(8,128)(2,1)S(1)}, bf16[4,256,128]{2,1,0:T(8,128)(2,1)S(1)}, u32[]{:S(2)}, u32[]{:S(2)}) collective-permute-start(bf16[4,256,128]{2,1,0:T(8,128)(2,1)S(1)} %shard_map.98), channel_id=1, source_target_pairs={{0,16},{2,18},{4,20},{6,22},{8,24},{10,26},{12,28},{14,30},{16,0},... | collective-permute-start | bytes 786440 | tf_op jit(solution)/shard_map/ppermute | solution.py:25
  137.2 34.1 %collective-permute-start.26 = (bf16[4,256,128]{2,1,0:T(8,128)(2,1)S(1)}, bf16[4,256,128]{2,1,0:T(8,128)(2,1)S(1)}, u32[]{:S(2)}, u32[]{:S(2)}) collective-permute-start(bf16[4,256,128]{2,1,0:T(8,128)(2,1)S(1)} %shard_map.107), channel_id=1, source_target_pairs={{0,16},{2,18},{4,20},{6,22},{8,24},{10,26},{12,28},{14,30},{16,0},... | collective-permute-start | bytes 786440 | tf_op jit(solution)/shard_map/ppermute | solution.py:25
  141.9 34.9 %collective-permute-start.34 = (bf16[4,256,128]{2,1,0:T(8,128)(2,1)S(1)}, bf16[4,256,128]{2,1,0:T(8,128)(2,1)S(1)}, u32[]{:S(2)}, u32[]{:S(2)}) collective-permute-start(bf16[4,256,128]{2,1,0:T(8,128)(2,1)S(1)} %shard_map.115), channel_id=1, source_target_pairs={{0,16},{2,18},{4,20},{6,22},{8,24},{10,26},{12,28},{14,30},{16,0},... | collective-permute-start | bytes 786440 | tf_op jit(solution)/shard_map/ppermute | solution.py:25
  147.6 33.7 %collective-permute-start.10 = (bf16[4,256,128]{2,1,0:T(8,128)(2,1)S(1)}, bf16[4,256,128]{2,1,0:T(8,128)(2,1)S(1)}, u32[]{:S(2)}, u32[]{:S(2)}) collective-permute-start(bf16[4,256,128]{2,1,0:T(8,128)(2,1)S(1)} %shard_map.90), channel_id=1, source_target_pairs={{0,16},{2,18},{4,20},{6,22},{8,24},{10,26},{12,28},{14,30},{16,0},... | collective-permute-start | bytes 786440 | tf_op jit(solution)/shard_map/ppermute | solution.py:25
  151.2 14.4 %copy-start.2 = (bf16[1,1,4,256,256]{4,3,2,1,0:T(8,128)(2,1)S(1)}, bf16[1,1,4,256,256]{4,3,2,1,0:T(8,128)(2,1)}, u32[]{:S(2)}) copy-start(bf16[1,1,4,256,256]{4,3,2,1,0:T(8,128)(2,1)} %refs_2_.7) | copy-start | bytes 1572868
  151.2 14.4 %copy-start.3 = (bf16[1,1,4,256,256]{4,3,2,1,0:T(8,128)(2,1)S(1)}, bf16[1,1,4,256,256]{4,3,2,1,0:T(8,128)(2,1)}, u32[]{:S(2)}) copy-start(bf16[1,1,4,256,256]{4,3,2,1,0:T(8,128)(2,1)} %refs_3_.7) | copy-start | bytes 1572868

commit v4 on v3

--- a/solution.py
+++ b/solution.py
@@ -14,7 +14,7 @@
     (1, 1, 0), (2, 0, 0), (2, 1, 1), (1, 0, 2), (1, 0, 3), (2, 2, 1),
     (2, 1, 2), (1, 1, 1), (1, 2, 0), (3, 2, 0), (2, 2, 2), (1, 1, 2),
     (2, 1, 0), (2, 1, 3), (2, 3, 2), (1, 2, 1), (1, 1, 3), (3, 1, 0),
-    (2, 3, 1), (1, 3, 0), (2, 2, 0), (1, 2, 2), (1, 3, 1), (2, 3, 0),
+    (2, 3, 1), (2, 2, 0), (1, 2, 2), (1, 3, 1), (1, 3, 0), (2, 3, 0),
     (1, 2, 3), (2, 2, 3), (1, 3, 2), (2, 3, 3), (1, 4, 0), (1, 3, 3),
     (1, 4, 1), (0, 0, 0), (0, 0, 1), (1, 4, 2), (0, 0, 2), (1, 4, 3),
     (0, 0, 3),
@@ -138,20 +138,27 @@
             copy.wait()
 
     args = (sibling, distant, one, two)
-    if len(ready) < CHUNKS - 1:
+    final = len(ready) == CHUNKS - 1
+    if len(ready) < CHUNKS - 2:
         return pl.pallas_call(
             early, out_shape=jax.ShapeDtypeStruct(sibling.shape, jnp.bfloat16),
             in_specs=[VMEM] * 4, out_specs=VMEM,
             cost_estimate=cost(2, sibling.shape), compiler_params=small(),
         )(*args)
-    args += tuple(value for _, value in ready)
+    alias = {}
+    specs = [VMEM] * (4 + len(ready))
+    if final:
+        args += (ready[-1][1],)
+        specs, alias, ready = [VMEM] * 4 + [HBM], {4: 0}, []
+    else:
+        args += tuple(value for _, value in ready)
     return pl.pallas_call(
         last, out_shape=jax.ShapeDtypeStruct(shape, jnp.bfloat16),
-        in_specs=[VMEM] * len(args), out_specs=HBM,
+        in_specs=specs, out_specs=HBM, input_output_aliases=alias,
         scratch_shapes=[
             pltpu.VMEM((nodes, leaf, width), jnp.bfloat16),
             pltpu.SemaphoreType.DMA((nodes,)),
-            pltpu.SemaphoreType.DMA((len(ready), nodes)),
+            pltpu.SemaphoreType.DMA((max(len(ready), 1), nodes)),
         ],
         cost_estimate=cost(2, sibling.shape), compiler_params=small(),
     )(*args)
@@ -192,7 +199,9 @@
             )
             axis, bit = "grp", top - 2 - stage if stage < 3 else top - 1
         elif stage == 1:
-            sent = value[1, k] = advance(value[1, k], moved[1, k], sections_one, 0, pairing, 0, 0)
+            sent = value[1, k] = advance(
+                value[1, k], moved[1, k], sections_one, 0, pairing, 0, 0
+            )
         elif stage == 2:
             sent = value[1, k] = moved[1, k]
             axis, bit = "grp", top - 2

time: 183 us -> 183 us (level)
  no operation moved by 1% of the time
where the time goes in v4:
time: 183 us
  waiting for transfers between devices  116 us (63%)
  starting transfers between devices  47.7 us (26%)
  Pallas kernels  18 us (10%)
    ppermute x35, waiting for transfers between devices, swapped(): lax.ppermute(value, axis, [(i, i ^ 1 << bit) for i in range(lax.axis_size...  116 us
    ppermute x35, starting transfers between devices, swapped(): lax.ppermute(value, axis, [(i, i ^ 1 << bit) for i in range(lax.axis_size...  47.7 us
    pallas_call x24, Pallas kernels, advance(): pl.pallas_call(kernel, out_shape=jax.ShapeDtypeStruct(own.shape, own.dtyp...  10.9 us
  transfers between devices with their start and end apart: 35, of which 21 were waited for; matrix products, arithmetic and copies ran while one was open for 0% of the time, Pallas kernels for 8%

profile of v4, /device:TPU:0, one launch (start us, length us, event | category | flops | bytes accessed | tf_op | source)
XLA Modules:
  0.0 182.5 jit_solution(353323328579803662)
XLA Ops:
  0.0 2.0 %shard_map.82 = (bf16[4,256,128]{2,1,0:T(8,128)(2,1)S(1)}, bf16[1,1,1024,512]{3,2,1,0:T(8,128)(2,1)S(1)}, bf16[1,1,4,256,256]{4,3,2,1,0:T(8,128)(2,1)S(1)}, bf16[1,1,4,256,256]{4,3,2,1,0:T(8,128)(2,1)S(1)}) custom-call(bf16[1,1,1024,512]{3,2,1,0:T(8,128)(2,1)} %x_ref.1, bf16[1,1,4,256,256]{4,3,2,1,0:T(8,128)(2,1)} %one_ref.1, ...), custom_call_target="tpu_custom_call" | custom-call | flops 67108864 | bytes 1048576 | tf_op jit(solution)/shard_map/pallas_call | solution.py:72
  2.3 4.1 %collective-permute-start.1 = (bf16[4,256,128]{2,1,0:T(8,128)(2,1)S(1)}, bf16[4,256,128]{2,1,0:T(8,128)(2,1)S(1)}, u32[]{:S(2)}, u32[]{:S(2)}) collective-permute-start(bf16[4,256,128]{2,1,0:T(8,128)(2,1)S(1)} %shard_map.83.own_ref), channel_id=1, source_target_pairs={{0,16},{2,18},{4,20},{6,22},{8,24},{10,26},{12,28},{14,30},{16,0},... | collective-permute-start | bytes 786440 | tf_op jit(solution)/shard_map/ppermute | solution.py:25
  7.1 3.0 %collective-permute-start.19 = (bf16[4,256,128]{2,1,0:T(8,128)(2,1)S(1)}, bf16[4,256,128]{2,1,0:T(8,128)(2,1)S(1)}, u32[]{:S(2)}, u32[]{:S(2)}) collective-permute-start(bf16[4,256,128]{2,1,0:T(8,128)(2,1)S(1)} %shard_map.98.own_ref), channel_id=1, source_target_pairs={{0,16},{2,18},{4,20},{6,22},{8,24},{10,26},{12,28},{14,30},{16,0},... | collective-permute-start | bytes 786440 | tf_op jit(solution)/shard_map/ppermute | solution.py:25
  10.7 2.0 %collective-permute-start.7 = (bf16[4,256,128]{2,1,0:T(8,128)(2,1)S(1)}, bf16[4,256,128]{2,1,0:T(8,128)(2,1)S(1)}, u32[]{:S(2)}, u32[]{:S(2)}) collective-permute-start(bf16[4,256,128]{2,1,0:T(8,128)(2,1)S(1)} %shard_map.87.own_ref), channel_id=1, source_target_pairs={{0,8},{2,10},{4,12},{6,14},{8,0},{10,2},{12,4},{14,6},{16,24},{18,... | collective-permute-start | bytes 786440 | tf_op jit(solution)/shard_map/ppermute | solution.py:25
  13.2 22.8 %collective-permute-done.1.partner_ref = bf16[4,256,128]{2,1,0:T(8,128)(2,1)S(1)} collective-permute-done((bf16[4,256,128]{2,1,0:T(8,128)(2,1)S(1)}, bf16[4,256,128]{2,1,0:T(8,128)(2,1)S(1)}, u32[]{:S(2)}, u32[]{:S(2)}) %collective-permute-start.1) | collective-permute-done | bytes 262176 | tf_op jit(solution)/shard_map/ppermute | solution.py:25
  36.0 1.8 collective-permute-start
  38.3 3.4 %collective-permute-done.11.partner_ref = bf16[4,256,128]{2,1,0:T(8,128)(2,1)S(1)} collective-permute-done((bf16[4,256,128]{2,1,0:T(8,128)(2,1)S(1)}, bf16[4,256,128]{2,1,0:T(8,128)(2,1)S(1)}, u32[]{:S(2)}, u32[]{:S(2)}) %collective-permute-start.11) | collective-permute-done | bytes 262176 | tf_op jit(solution)/shard_map/ppermute | solution.py:25
  42.1 2.1 %collective-permute-start.31 = (bf16[4,256,128]{2,1,0:T(8,128)(2,1)S(1)}, bf16[4,256,128]{2,1,0:T(8,128)(2,1)S(1)}, u32[]{:S(2)}, u32[]{:S(2)}) collective-permute-start(bf16[4,256,128]{2,1,0:T(8,128)(2,1)S(1)} %shard_map.111.own_ref), channel_id=1, source_target_pairs={{0,8},{2,10},{4,12},{6,14},{8,0},{10,2},{12,4},{14,6},{16,24},{18,... | collective-permute-start | bytes 786440 | tf_op jit(solution)/shard_map/ppermute | solution.py:25
  44.2 3.2 %collective-permute-done.19.partner_ref = bf16[4,256,128]{2,1,0:T(8,128)(2,1)S(1)} collective-permute-done((bf16[4,256,128]{2,1,0:T(8,128)(2,1)S(1)}, bf16[4,256,128]{2,1,0:T(8,128)(2,1)S(1)}, u32[]{:S(2)}, u32[]{:S(2)}) %collective-permute-start.19) | collective-permute-done | bytes 262176 | tf_op jit(solution)/shard_map/ppermute | solution.py:25
  47.4 4.8 %collective-permute-done.27.partner_ref = bf16[4,256,128]{2,1,0:T(8,128)(2,1)S(1)} collective-permute-done((bf16[4,256,128]{2,1,0:T(8,128)(2,1)S(1)}, bf16[4,256,128]{2,1,0:T(8,128)(2,1)S(1)}, u32[]{:S(2)}, u32[]{:S(2)}) %collective-permute-start.27) | collective-permute-done | bytes 262176 | tf_op jit(solution)/shard_map/ppermute | solution.py:25
  52.1 1.5 collective-permute-start.2
  54.4 3.4 %collective-permute-done.23.partner_ref = bf16[4,256,128]{2,1,0:T(8,128)(2,1)S(1)} collective-permute-done((bf16[4,256,128]{2,1,0:T(8,128)(2,1)S(1)}, bf16[4,256,128]{2,1,0:T(8,128)(2,1)S(1)}, u32[]{:S(2)}, u32[]{:S(2)}) %collective-permute-start.23) | collective-permute-done | bytes 262176 | tf_op jit(solution)/shard_map/ppermute | solution.py:25
  57.7 1.5 collective-permute-start.4
  59.7 3.6 %collective-permute-done.31.partner_ref = bf16[4,256,128]{2,1,0:T(8,128)(2,1)S(1)} collective-permute-done((bf16[4,256,128]{2,1,0:T(8,128)(2,1)S(1)}, bf16[4,256,128]{2,1,0:T(8,128)(2,1)S(1)}, u32[]{:S(2)}, u32[]{:S(2)}) %collective-permute-start.31) | collective-permute-done | bytes 262176 | tf_op jit(solution)/shard_map/ppermute | solution.py:25
  63.4 1.5 collective-permute-start.20
  65.3 3.5 %collective-permute-done.15.partner_ref = bf16[4,256,128]{2,1,0:T(8,128)(2,1)S(1)} collective-permute-done((bf16[4,256,128]{2,1,0:T(8,128)(2,1)S(1)}, bf16[4,256,128]{2,1,0:T(8,128)(2,1)S(1)}, u32[]{:S(2)}, u32[]{:S(2)}) %collective-permute-start.15) | collective-permute-done | bytes 262176 | tf_op jit(solution)/shard_map/ppermute | solution.py:25
  68.9 1.5 collective-permute-start.28
  70.9 1.6 collective-permute-start.8
  72.9 0.6 collective-permute-start.24
  73.5 21.5 %collective-permute-done.20.own_ref = bf16[4,256,128]{2,1,0:T(8,128)(2,1)S(1)} collective-permute-done((bf16[4,256,128]{2,1,0:T(8,128)(2,1)S(1)}, bf16[4,256,128]{2,1,0:T(8,128)(2,1)S(1)}, u32[]{:S(2)}, u32[]{:S(2)}) %collective-permute-start.20) | collective-permute-done | bytes 262176 | tf_op jit(solution)/shard_map/ppermute | solution.py:25
  95.0 1.5 collective-permute-start.6
  97.0 3.6 %collective-permute-done.28.own_ref = bf16[4,256,128]{2,1,0:T(8,128)(2,1)S(1)} collective-permute-done((bf16[4,256,128]{2,1,0:T(8,128)(2,1)S(1)}, bf16[4,256,128]{2,1,0:T(8,128)(2,1)S(1)}, u32[]{:S(2)}, u32[]{:S(2)}) %collective-permute-start.28) | collective-permute-done | bytes 262176 | tf_op jit(solution)/shard_map/ppermute | solution.py:25
  100.6 1.6 collective-permute-start.32
  103.2 0.7 collective-permute-start.3
  103.8 4.4 %collective-permute-done.32.partner_ref = bf16[4,256,128]{2,1,0:T(8,128)(2,1)S(1)} collective-permute-done((bf16[4,256,128]{2,1,0:T(8,128)(2,1)S(1)}, bf16[4,256,128]{2,1,0:T(8,128)(2,1)S(1)}, u32[]{:S(2)}, u32[]{:S(2)}) %collective-permute-start.32) | collective-permute-done | bytes 262176 | tf_op jit(solution)/shard_map/ppermute | solution.py:25
  108.2 2.2 %collective-permute-start.13 = (bf16[4,256,128]{2,1,0:T(8,128)(2,1)S(1)}, bf16[4,256,128]{2,1,0:T(8,128)(2,1)S(1)}, u32[]{:S(2)}, u32[]{:S(2)}) collective-permute-start(bf16[4,256,128]{2,1,0:T(8,128)(2,1)S(1)} %collective-permute-done.12.own_ref), channel_id=1, source_target_pairs={{0,8},{2,10},{4,12},{6,14},{8,0},{10,2},{12,4},{14,6},{16,24},{18,... | collective-permute-start | bytes 786440 | tf_op jit(solution)/shard_map/ppermute | solution.py:25
  111.0 2.3 %collective-permute-start.21 = (bf16[4,256,128]{2,1,0:T(8,128)(2,1)S(1)}, bf16[4,256,128]{2,1,0:T(8,128)(2,1)S(1)}, u32[]{:S(2)}, u32[]{:S(2)}) collective-permute-start(bf16[4,256,128]{2,1,0:T(8,128)(2,1)S(1)} %collective-permute-done.20.own_ref), channel_id=1, source_target_pairs={{0,8},{2,10},{4,12},{6,14},{8,0},{10,2},{12,4},{14,6},{16,24},{18,... | collective-permute-start | bytes 786440 | tf_op jit(solution)/shard_map/ppermute | solution.py:25
  113.8 3.8 %collective-permute-done.13.partner_ref = bf16[4,256,128]{2,1,0:T(8,128)(2,1)S(1)} collective-permute-done((bf16[4,256,128]{2,1,0:T(8,128)(2,1)S(1)}, bf16[4,256,128]{2,1,0:T(8,128)(2,1)S(1)}, u32[]{:S(2)}, u32[]{:S(2)}) %collective-permute-start.13) | collective-permute-done | bytes 262176 | tf_op jit(solution)/shard_map/ppermute | solution.py:25
  118.1 4.7 %collective-permute-done.21.partner_ref = bf16[4,256,128]{2,1,0:T(8,128)(2,1)S(1)} collective-permute-done((bf16[4,256,128]{2,1,0:T(8,128)(2,1)S(1)}, bf16[4,256,128]{2,1,0:T(8,128)(2,1)S(1)}, u32[]{:S(2)}, u32[]{:S(2)}) %collective-permute-start.21) | collective-permute-done | bytes 262176 | tf_op jit(solution)/shard_map/ppermute | solution.py:25
  123.2 2.4 %collective-permute-done.29.partner_ref = bf16[4,256,128]{2,1,0:T(8,128)(2,1)S(1)} collective-permute-done((bf16[4,256,128]{2,1,0:T(8,128)(2,1)S(1)}, bf16[4,256,128]{2,1,0:T(8,128)(2,1)S(1)}, u32[]{:S(2)}, u32[]{:S(2)}) %collective-permute-start.29) | collective-permute-done | bytes 262176 | tf_op jit(solution)/shard_map/ppermute | solution.py:25
  126.0 0.6 collective-permute-start.17
  127.1 1.6 collective-permute-start.5
  129.1 0.6 collective-permute-start.14
  130.2 1.6 collective-permute-start.22
  132.2 0.6 collective-permute-start.30
  133.3 3.3 %collective-permute-start.26 = (bf16[4,256,128]{2,1,0:T(8,128)(2,1)S(1)}, bf16[4,256,128]{2,1,0:T(8,128)(2,1)S(1)}, u32[]{:S(2)}, u32[]{:S(2)}) collective-permute-start(bf16[4,256,128]{2,1,0:T(8,128)(2,1)S(1)} %shard_map.105), channel_id=1, source_target_pairs={{0,16},{2,18},{4,20},{6,22},{8,24},{10,26},{12,28},{14,30},{16,0},... | collective-permute-start | bytes 786440 | tf_op jit(solution)/shard_map/ppermute | solution.py:25
  136.5 0.6 shard_map.114
  137.2 2.4 %collective-permute-start.34 = (bf16[4,256,128]{2,1,0:T(8,128)(2,1)S(1)}, bf16[4,256,128]{2,1,0:T(8,128)(2,1)S(1)}, u32[]{:S(2)}, u32[]{:S(2)}) collective-permute-start(bf16[4,256,128]{2,1,0:T(8,128)(2,1)S(1)} %shard_map.114), channel_id=1, source_target_pairs={{0,16},{2,18},{4,20},{6,22},{8,24},{10,26},{12,28},{14,30},{16,0},... | collective-permute-start | bytes 786440 | tf_op jit(solution)/shard_map/ppermute | solution.py:25
  140.0 1.9 %collective-permute-done.14.partner_ref = bf16[4,256,128]{2,1,0:T(8,128)(2,1)S(1)} collective-permute-done((bf16[4,256,128]{2,1,0:T(8,128)(2,1)S(1)}, bf16[4,256,128]{2,1,0:T(8,128)(2,1)S(1)}, u32[]{:S(2)}, u32[]{:S(2)}) %collective-permute-start.14) | collective-permute-done | bytes 262176 | tf_op jit(solution)/shard_map/ppermute | solution.py:25
  141.9 3.2 %collective-permute-start.18 = (bf16[4,256,128]{2,1,0:T(8,128)(2,1)S(1)}, bf16[4,256,128]{2,1,0:T(8,128)(2,1)S(1)}, u32[]{:S(2)}, u32[]{:S(2)}) collective-permute-start(bf16[4,256,128]{2,1,0:T(8,128)(2,1)S(1)} %shard_map.97), channel_id=1, source_target_pairs={{0,16},{2,18},{4,20},{6,22},{8,24},{10,26},{12,28},{14,30},{16,0},... | collective-permute-start | bytes 786440 | tf_op jit(solution)/shard_map/ppermute | solution.py:25
  145.6 2.0 %collective-permute-done.22.partner_ref = bf16[4,256,128]{2,1,0:T(8,128)(2,1)S(1)} collective-permute-done((bf16[4,256,128]{2,1,0:T(8,128)(2,1)S(1)}, bf16[4,256,128]{2,1,0:T(8,128)(2,1)S(1)}, u32[]{:S(2)}, u32[]{:S(2)}) %collective-permute-start.22) | collective-permute-done | bytes 262176 | tf_op jit(solution)/shard_map/ppermute | solution.py:25
  147.6 3.2 %collective-permute-start.10 = (bf16[4,256,128]{2,1,0:T(8,128)(2,1)S(1)}, bf16[4,256,128]{2,1,0:T(8,128)(2,1)S(1)}, u32[]{:S(2)}, u32[]{:S(2)}) collective-permute-start(bf16[4,256,128]{2,1,0:T(8,128)(2,1)S(1)} %shard_map.90), channel_id=1, source_target_pairs={{0,16},{2,18},{4,20},{6,22},{8,24},{10,26},{12,28},{14,30},{16,0},... | collective-permute-start | bytes 786440 | tf_op jit(solution)/shard_map/ppermute | solution.py:25
  152.7 13.0 %collective-permute-done.26.refs_1_ = bf16[4,256,128]{2,1,0:T(8,128)(2,1)S(1)} collective-permute-done((bf16[4,256,128]{2,1,0:T(8,128)(2,1)S(1)}, bf16[4,256,128]{2,1,0:T(8,128)(2,1)S(1)}, u32[]{:S(2)}, u32[]{:S(2)}) %collective-permute-start.26) | collective-permute-done | bytes 262176 | tf_op jit(solution)/shard_map/ppermute | solution.py:25
  166.1 5.2 %collective-permute-done.34.refs_1_ = bf16[4,256,128]{2,1,0:T(8,128)(2,1)S(1)} collective-permute-done((bf16[4,256,128]{2,1,0:T(8,128)(2,1)S(1)}, bf16[4,256,128]{2,1,0:T(8,128)(2,1)S(1)}, u32[]{:S(2)}, u32[]{:S(2)}) %collective-permute-start.34) | collective-permute-done | bytes 262176 | tf_op jit(solution)/shard_map/ppermute | solution.py:25
  171.7 5.2 %collective-permute-done.18.refs_1_ = bf16[4,256,128]{2,1,0:T(8,128)(2,1)S(1)} collective-permute-done((bf16[4,256,128]{2,1,0:T(8,128)(2,1)S(1)}, bf16[4,256,128]{2,1,0:T(8,128)(2,1)S(1)}, u32[]{:S(2)}, u32[]{:S(2)}) %collective-permute-start.18) | collective-permute-done | bytes 262176 | tf_op jit(solution)/shard_map/ppermute | solution.py:25
  176.9 1.2 shard_map.116.refs_4_
  178.0 3.2 %collective-permute-done.10.refs_1_ = bf16[4,256,128]{2,1,0:T(8,128)(2,1)S(1)} collective-permute-done((bf16[4,256,128]{2,1,0:T(8,128)(2,1)S(1)}, bf16[4,256,128]{2,1,0:T(8,128)(2,1)S(1)}, u32[]{:S(2)}, u32[]{:S(2)}) %collective-permute-start.10) | collective-permute-done | bytes 262176 | tf_op jit(solution)/shard_map/ppermute | solution.py:25
  181.2 1.1 shard_map.117
  (69 shorter events, 15.2 us)
Async XLA Ops:
  2.3 33.8 %collective-permute-start.1 = (bf16[4,256,128]{2,1,0:T(8,128)(2,1)S(1)}, bf16[4,256,128]{2,1,0:T(8,128)(2,1)S(1)}, u32[]{:S(2)}, u32[]{:S(2)}) collective-permute-start(bf16[4,256,128]{2,1,0:T(8,128)(2,1)S(1)} %shard_map.83.own_ref), channel_id=1, source_target_pairs={{0,16},{2,18},{4,20},{6,22},{8,24},{10,26},{12,28},{14,30},{16,0},... | collective-permute-start | bytes 786440 | tf_op jit(solution)/shard_map/ppermute | solution.py:25
  6.7 35.0 %collective-permute-start.11 = (bf16[4,256,128]{2,1,0:T(8,128)(2,1)S(1)}, bf16[4,256,128]{2,1,0:T(8,128)(2,1)S(1)}, u32[]{:S(2)}, u32[]{:S(2)}) collective-permute-start(bf16[4,256,128]{2,1,0:T(8,128)(2,1)S(1)} %shard_map.91.own_ref), channel_id=1, source_target_pairs={{0,16},{2,18},{4,20},{6,22},{8,24},{10,26},{12,28},{14,30},{16,0},... | collective-permute-start | bytes 786440 | tf_op jit(solution)/shard_map/ppermute | solution.py:25
  7.1 40.3 %collective-permute-start.19 = (bf16[4,256,128]{2,1,0:T(8,128)(2,1)S(1)}, bf16[4,256,128]{2,1,0:T(8,128)(2,1)S(1)}, u32[]{:S(2)}, u32[]{:S(2)}) collective-permute-start(bf16[4,256,128]{2,1,0:T(8,128)(2,1)S(1)} %shard_map.98.own_ref), channel_id=1, source_target_pairs={{0,16},{2,18},{4,20},{6,22},{8,24},{10,26},{12,28},{14,30},{16,0},... | collective-permute-start | bytes 786440 | tf_op jit(solution)/shard_map/ppermute | solution.py:25
  10.3 25.7 %copy-start.4 = (s32[2,3,1,1,4]{4,3,2,1,0:T(1,128)S(1)}, s32[2,3,1,1,4]{4,3,2,1,0:T(1,128)}, u32[]{:S(2)}) copy-start(s32[2,3,1,1,4]{4,3,2,1,0:T(1,128)} %table_ref.31) | copy-start | bytes 292
  10.3 27.5 %copy-start.1 = (bf16[1,1,3,4,256,512]{5,4,3,2,1,0:T(8,128)(2,1)S(1)}, bf16[1,1,3,4,256,512]{5,4,3,2,1,0:T(8,128)(2,1)}, u32[]{:S(2)}) copy-start(bf16[1,1,3,4,256,512]{5,4,3,2,1,0:T(8,128)(2,1)} %w_ref.28) | copy-start | bytes 9437188
  10.3 41.8 %collective-permute-start.27 = (bf16[4,256,128]{2,1,0:T(8,128)(2,1)S(1)}, bf16[4,256,128]{2,1,0:T(8,128)(2,1)S(1)}, u32[]{:S(2)}, u32[]{:S(2)}) collective-permute-start(bf16[4,256,128]{2,1,0:T(8,128)(2,1)S(1)} %shard_map.107.own_ref), channel_id=1, source_target_pairs={{0,16},{2,18},{4,20},{6,22},{8,24},{10,26},{12,28},{14,30},{16,0},... | collective-permute-start | bytes 786440 | tf_op jit(solution)/shard_map/ppermute | solution.py:25
  10.7 43.0 %collective-permute-start.7 = (bf16[4,256,128]{2,1,0:T(8,128)(2,1)S(1)}, bf16[4,256,128]{2,1,0:T(8,128)(2,1)S(1)}, u32[]{:S(2)}, u32[]{:S(2)}) collective-permute-start(bf16[4,256,128]{2,1,0:T(8,128)(2,1)S(1)} %shard_map.87.own_ref), channel_id=1, source_target_pairs={{0,8},{2,10},{4,12},{6,14},{8,0},{10,2},{12,4},{14,6},{16,24},{18,... | collective-permute-start | bytes 786440 | tf_op jit(solution)/shard_map/ppermute | solution.py:25
  36.0 6.1 %collective-permute-start = (s32[2,3,1,1,4]{4,3,2,1,0:T(1,128)S(1)}, s32[2,3,1,1,4]{4,3,2,1,0:T(1,128)S(1)}, u32[]{:S(2)}, u32[]{:S(2)}) collective-permute-start(s32[2,3,1,1,4]{4,3,2,1,0:T(1,128)S(1)} %copy-done.4), channel_id=1, source_target_pairs={{0,1},{1,0},{2,3},{3,2},{4,5},{5,4},{6,7},{7,6},{8,9},{9,8},{10,11... | collective-permute-start | bytes 296 | tf_op jit(solution)/shard_map/ppermute | solution.py:25
  41.6 16.1 %collective-permute-start.23 = (bf16[4,256,128]{2,1,0:T(8,128)(2,1)S(1)}, bf16[4,256,128]{2,1,0:T(8,128)(2,1)S(1)}, u32[]{:S(2)}, u32[]{:S(2)}) collective-permute-start(bf16[4,256,128]{2,1,0:T(8,128)(2,1)S(1)} %shard_map.102.own_ref), channel_id=1, source_target_pairs={{0,8},{2,10},{4,12},{6,14},{8,0},{10,2},{12,4},{14,6},{16,24},{18,... | collective-permute-start | bytes 786440 | tf_op jit(solution)/shard_map/ppermute | solution.py:25
  42.1 21.3 %collective-permute-start.31 = (bf16[4,256,128]{2,1,0:T(8,128)(2,1)S(1)}, bf16[4,256,128]{2,1,0:T(8,128)(2,1)S(1)}, u32[]{:S(2)}, u32[]{:S(2)}) collective-permute-start(bf16[4,256,128]{2,1,0:T(8,128)(2,1)S(1)} %shard_map.111.own_ref), channel_id=1, source_target_pairs={{0,8},{2,10},{4,12},{6,14},{8,0},{10,2},{12,4},{14,6},{16,24},{18,... | collective-permute-start | bytes 786440 | tf_op jit(solution)/shard_map/ppermute | solution.py:25
  47.4 21.5 %collective-permute-start.15 = (bf16[4,256,128]{2,1,0:T(8,128)(2,1)S(1)}, bf16[4,256,128]{2,1,0:T(8,128)(2,1)S(1)}, u32[]{:S(2)}, u32[]{:S(2)}) collective-permute-start(bf16[4,256,128]{2,1,0:T(8,128)(2,1)S(1)} %get-tuple-element.12.own_ref), channel_id=1, source_target_pairs={{0,8},{2,10},{4,12},{6,14},{8,0},{10,2},{12,4},{14,6},{16,24},{18,... | collective-permute-start | bytes 786440 | tf_op jit(solution)/shard_map/ppermute | solution.py:25
  52.1 18.8 %collective-permute-start.2 = (bf16[4,256,128]{2,1,0:T(8,128)(2,1)S(1)}, bf16[4,256,128]{2,1,0:T(8,128)(2,1)S(1)}, u32[]{:S(2)}, u32[]{:S(2)}) collective-permute-start(bf16[4,256,128]{2,1,0:T(8,128)(2,1)S(1)} %shard_map.84), channel_id=1, source_target_pairs={{0,1},{1,0},{2,3},{3,2},{4,5},{5,4},{6,7},{7,6},{8,9},{9,8},{10,11... | collective-permute-start | bytes 786440 | tf_op jit(solution)/shard_map/ppermute | solution.py:25
  53.7 19.3 %collective-permute-start.12 = (bf16[4,256,128]{2,1,0:T(8,128)(2,1)S(1)}, bf16[4,256,128]{2,1,0:T(8,128)(2,1)S(1)}, u32[]{:S(2)}, u32[]{:S(2)}) collective-permute-start(bf16[4,256,128]{2,1,0:T(8,128)(2,1)S(1)} %shard_map.92), channel_id=1, source_target_pairs={{0,1},{1,0},{2,3},{3,2},{4,5},{5,4},{6,7},{7,6},{8,9},{9,8},{10,11... | collective-permute-start | bytes 786440 | tf_op jit(solution)/shard_map/ppermute | solution.py:25
  57.7 12.7 %copy-start = (bf16[1,1,3,4,256,512]{5,4,3,2,1,0:T(8,128)(2,1)S(1)}, bf16[1,1,3,4,256,512]{5,4,3,2,1,0:T(8,128)(2,1)}, u32[]{:S(2)}) copy-start(bf16[1,1,3,4,256,512]{5,4,3,2,1,0:T(8,128)(2,1)} %w_ref.31) | copy-start | bytes 9437188
  57.7 68.3 %collective-permute-start.4 = (bf16[1,1,1,4,256,512]{5,4,3,2,1,0:T(8,128)(2,1)S(1)}, bf16[1,1,1,4,256,512]{5,4,3,2,1,0:T(8,128)(2,1)S(1)}, u32[]{:S(2)}, u32[]{:S(2)}) collective-permute-start(bf16[1,1,1,4,256,512]{5,4,3,2,1,0:T(8,128)(2,1)S(1)} %get-tuple-element.14), channel_id=1, source_target_pairs={{0,1},{1,0},{2,3},{3,2},{4,5},{5,4},{6,7},{7,6},{8,9},{9,8},{10,11... | collective-permute-start | bytes 3145736 | tf_op jit(solution)/shard_map/ppermute | solution.py:25
  63.4 31.7 %collective-permute-start.20 = (bf16[4,256,128]{2,1,0:T(8,128)(2,1)S(1)}, bf16[4,256,128]{2,1,0:T(8,128)(2,1)S(1)}, u32[]{:S(2)}, u32[]{:S(2)}) collective-permute-start(bf16[4,256,128]{2,1,0:T(8,128)(2,1)S(1)} %shard_map.99), channel_id=1, source_target_pairs={{0,1},{1,0},{2,3},{3,2},{4,5},{5,4},{6,7},{7,6},{8,9},{9,8},{10,11... | collective-permute-start | bytes 786440 | tf_op jit(solution)/shard_map/ppermute | solution.py:25
  68.9 31.7 %collective-permute-start.28 = (bf16[4,256,128]{2,1,0:T(8,128)(2,1)S(1)}, bf16[4,256,128]{2,1,0:T(8,128)(2,1)S(1)}, u32[]{:S(2)}, u32[]{:S(2)}) collective-permute-start(bf16[4,256,128]{2,1,0:T(8,128)(2,1)S(1)} %shard_map.108), channel_id=1, source_target_pairs={{0,1},{1,0},{2,3},{3,2},{4,5},{5,4},{6,7},{7,6},{8,9},{9,8},{10,11... | collective-permute-start | bytes 786440 | tf_op jit(solution)/shard_map/ppermute | solution.py:25
  70.9 31.8 %collective-permute-start.8 = (bf16[4,256,128]{2,1,0:T(8,128)(2,1)S(1)}, bf16[4,256,128]{2,1,0:T(8,128)(2,1)S(1)}, u32[]{:S(2)}, u32[]{:S(2)}) collective-permute-start(bf16[4,256,128]{2,1,0:T(8,128)(2,1)S(1)} %shard_map.88.own_ref), channel_id=1, source_target_pairs={{0,4},{2,6},{4,0},{6,2},{8,12},{10,14},{12,8},{14,10},{16,20},{18,... | collective-permute-start | bytes 786440 | tf_op jit(solution)/shard_map/ppermute | solution.py:25
  72.9 30.2 %collective-permute-start.24 = (bf16[4,256,128]{2,1,0:T(8,128)(2,1)S(1)}, bf16[4,256,128]{2,1,0:T(8,128)(2,1)S(1)}, u32[]{:S(2)}, u32[]{:S(2)}) collective-permute-start(bf16[4,256,128]{2,1,0:T(8,128)(2,1)S(1)} %shard_map.103.own_ref), channel_id=1, source_target_pairs={{0,4},{2,6},{4,0},{6,2},{8,12},{10,14},{12,8},{14,10},{16,20},{18,... | collective-permute-start | bytes 786440 | tf_op jit(solution)/shard_map/ppermute | solution.py:25
  95.0 38.2 %collective-permute-start.6 = (bf16[1,1,1,4,256,512]{5,4,3,2,1,0:T(8,128)(2,1)S(1)}, bf16[1,1,1,4,256,512]{5,4,3,2,1,0:T(8,128)(2,1)S(1)}, u32[]{:S(2)}, u32[]{:S(2)}) collective-permute-start(bf16[1,1,1,4,256,512]{5,4,3,2,1,0:T(8,128)(2,1)S(1)} %get-tuple-element.13), channel_id=1, source_target_pairs={{0,1},{1,0},{2,3},{3,2},{4,5},{5,4},{6,7},{7,6},{8,9},{9,8},{10,11... | collective-permute-start | bytes 3145736 | tf_op jit(solution)/shard_map/ppermute | solution.py:25
  100.6 7.6 %collective-permute-start.32 = (bf16[4,256,128]{2,1,0:T(8,128)(2,1)S(1)}, bf16[4,256,128]{2,1,0:T(8,128)(2,1)S(1)}, u32[]{:S(2)}, u32[]{:S(2)}) collective-permute-start(bf16[4,256,128]{2,1,0:T(8,128)(2,1)S(1)} %shard_map.112.own_ref), channel_id=1, source_target_pairs={{0,4},{2,6},{4,0},{6,2},{8,12},{10,14},{12,8},{14,10},{16,20},{18,... | collective-permute-start | bytes 786440 | tf_op jit(solution)/shard_map/ppermute | solution.py:25
  102.7 8.4 %collective-permute-start.16 = (bf16[4,256,128]{2,1,0:T(8,128)(2,1)S(1)}, bf16[4,256,128]{2,1,0:T(8,128)(2,1)S(1)}, u32[]{:S(2)}, u32[]{:S(2)}) collective-permute-start(bf16[4,256,128]{2,1,0:T(8,128)(2,1)S(1)} %shard_map.95.own_ref), channel_id=1, source_target_pairs={{0,4},{2,6},{4,0},{6,2},{8,12},{10,14},{12,8},{14,10},{16,20},{18,... | collective-permute-start | bytes 786440 | tf_op jit(solution)/shard_map/ppermute | solution.py:25
  103.2 10.2 %collective-permute-start.3 = (bf16[4,256,128]{2,1,0:T(8,128)(2,1)S(1)}, bf16[4,256,128]{2,1,0:T(8,128)(2,1)S(1)}, u32[]{:S(2)}, u32[]{:S(2)}) collective-permute-start(bf16[4,256,128]{2,1,0:T(8,128)(2,1)S(1)} %collective-permute-done.2.own_ref), channel_id=1, source_target_pairs={{0,8},{2,10},{4,12},{6,14},{8,0},{10,2},{12,4},{14,6},{16,24},{18,... | collective-permute-start | bytes 786440 | tf_op jit(solution)/shard_map/ppermute | solution.py:25
  108.2 9.4 %collective-permute-start.13 = (bf16[4,256,128]{2,1,0:T(8,128)(2,1)S(1)}, bf16[4,256,128]{2,1,0:T(8,128)(2,1)S(1)}, u32[]{:S(2)}, u32[]{:S(2)}) collective-permute-start(bf16[4,256,128]{2,1,0:T(8,128)(2,1)S(1)} %collective-permute-done.12.own_ref), channel_id=1, source_target_pairs={{0,8},{2,10},{4,12},{6,14},{8,0},{10,2},{12,4},{14,6},{16,24},{18,... | collective-permute-start | bytes 786440 | tf_op jit(solution)/shard_map/ppermute | solution.py:25
  111.0 11.7 %collective-permute-start.21 = (bf16[4,256,128]{2,1,0:T(8,128)(2,1)S(1)}, bf16[4,256,128]{2,1,0:T(8,128)(2,1)S(1)}, u32[]{:S(2)}, u32[]{:S(2)}) collective-permute-start(bf16[4,256,128]{2,1,0:T(8,128)(2,1)S(1)} %collective-permute-done.20.own_ref), channel_id=1, source_target_pairs={{0,8},{2,10},{4,12},{6,14},{8,0},{10,2},{12,4},{14,6},{16,24},{18,... | collective-permute-start | bytes 786440 | tf_op jit(solution)/shard_map/ppermute | solution.py:25
  113.3 12.2 %collective-permute-start.29 = (bf16[4,256,128]{2,1,0:T(8,128)(2,1)S(1)}, bf16[4,256,128]{2,1,0:T(8,128)(2,1)S(1)}, u32[]{:S(2)}, u32[]{:S(2)}) collective-permute-start(bf16[4,256,128]{2,1,0:T(8,128)(2,1)S(1)} %collective-permute-done.28.own_ref), channel_id=1, source_target_pairs={{0,8},{2,10},{4,12},{6,14},{8,0},{10,2},{12,4},{14,6},{16,24},{18,... | collective-permute-start | bytes 786440 | tf_op jit(solution)/shard_map/ppermute | solution.py:25
  117.6 9.5 %collective-permute-start.9 = (bf16[4,256,128]{2,1,0:T(8,128)(2,1)S(1)}, bf16[4,256,128]{2,1,0:T(8,128)(2,1)S(1)}, u32[]{:S(2)}, u32[]{:S(2)}) collective-permute-start(bf16[4,256,128]{2,1,0:T(8,128)(2,1)S(1)} %shard_map.89.own_ref), channel_id=1, source_target_pairs={{0,2},{2,0},{4,6},{6,4},{8,10},{10,8},{12,14},{14,12},{16,18},{18,... | collective-permute-start | bytes 786440 | tf_op jit(solution)/shard_map/ppermute | solution.py:25
  122.8 6.4 %collective-permute-start.25 = (bf16[4,256,128]{2,1,0:T(8,128)(2,1)S(1)}, bf16[4,256,128]{2,1,0:T(8,128)(2,1)S(1)}, u32[]{:S(2)}, u32[]{:S(2)}) collective-permute-start(bf16[4,256,128]{2,1,0:T(8,128)(2,1)S(1)} %shard_map.104.own_ref), channel_id=1, source_target_pairs={{0,2},{2,0},{4,6},{6,4},{8,10},{10,8},{12,14},{14,12},{16,18},{18,... | collective-permute-start | bytes 786440 | tf_op jit(solution)/shard_map/ppermute | solution.py:25
  125.6 4.6 %collective-permute-start.33 = (bf16[4,256,128]{2,1,0:T(8,128)(2,1)S(1)}, bf16[4,256,128]{2,1,0:T(8,128)(2,1)S(1)}, u32[]{:S(2)}, u32[]{:S(2)}) collective-permute-start(bf16[4,256,128]{2,1,0:T(8,128)(2,1)S(1)} %shard_map.113.own_ref), channel_id=1, source_target_pairs={{0,2},{2,0},{4,6},{6,4},{8,10},{10,8},{12,14},{14,12},{16,18},{18,... | collective-permute-start | bytes 786440 | tf_op jit(solution)/shard_map/ppermute | solution.py:25
  126.0 6.2 %collective-permute-start.17 = (bf16[4,256,128]{2,1,0:T(8,128)(2,1)S(1)}, bf16[4,256,128]{2,1,0:T(8,128)(2,1)S(1)}, u32[]{:S(2)}, u32[]{:S(2)}) collective-permute-start(bf16[4,256,128]{2,1,0:T(8,128)(2,1)S(1)} %shard_map.96.own_ref), channel_id=1, source_target_pairs={{0,2},{2,0},{4,6},{6,4},{8,10},{10,8},{12,14},{14,12},{16,18},{18,... | collective-permute-start | bytes 786440 | tf_op jit(solution)/shard_map/ppermute | solution.py:25
  127.1 10.1 %collective-permute-start.5 = (bf16[4,256,128]{2,1,0:T(8,128)(2,1)S(1)}, bf16[4,256,128]{2,1,0:T(8,128)(2,1)S(1)}, u32[]{:S(2)}, u32[]{:S(2)}) collective-permute-start(bf16[4,256,128]{2,1,0:T(8,128)(2,1)S(1)} %shard_map.85.own_ref), channel_id=1, source_target_pairs={{0,4},{2,6},{4,0},{6,2},{8,12},{10,14},{12,8},{14,10},{16,20},{18,... | collective-permute-start | bytes 786440 | tf_op jit(solution)/shard_map/ppermute | solution.py:25
  129.1 12.8 %collective-permute-start.14 = (bf16[4,256,128]{2,1,0:T(8,128)(2,1)S(1)}, bf16[4,256,128]{2,1,0:T(8,128)(2,1)S(1)}, u32[]{:S(2)}, u32[]{:S(2)}) collective-permute-start(bf16[4,256,128]{2,1,0:T(8,128)(2,1)S(1)} %shard_map.93.own_ref), channel_id=1, source_target_pairs={{0,4},{2,6},{4,0},{6,2},{8,12},{10,14},{12,8},{14,10},{16,20},{18,... | collective-permute-start | bytes 786440 | tf_op jit(solution)/shard_map/ppermute | solution.py:25
  130.2 17.4 %collective-permute-start.22 = (bf16[4,256,128]{2,1,0:T(8,128)(2,1)S(1)}, bf16[4,256,128]{2,1,0:T(8,128)(2,1)S(1)}, u32[]{:S(2)}, u32[]{:S(2)}) collective-permute-start(bf16[4,256,128]{2,1,0:T(8,128)(2,1)S(1)} %shard_map.100.own_ref), channel_id=1, source_target_pairs={{0,4},{2,6},{4,0},{6,2},{8,12},{10,14},{12,8},{14,10},{16,20},{18,... | collective-permute-start | bytes 786440 | tf_op jit(solution)/shard_map/ppermute | solution.py:25
  132.2 20.0 %collective-permute-start.30 = (bf16[4,256,128]{2,1,0:T(8,128)(2,1)S(1)}, bf16[4,256,128]{2,1,0:T(8,128)(2,1)S(1)}, u32[]{:S(2)}, u32[]{:S(2)}) collective-permute-start(bf16[4,256,128]{2,1,0:T(8,128)(2,1)S(1)} %shard_map.109.own_ref), channel_id=1, source_target_pairs={{0,4},{2,6},{4,0},{6,2},{8,12},{10,14},{12,8},{14,10},{16,20},{18,... | collective-permute-start | bytes 786440 | tf_op jit(solution)/shard_map/ppermute | solution.py:25
  133.3 32.4 %collective-permute-start.26 = (bf16[4,256,128]{2,1,0:T(8,128)(2,1)S(1)}, bf16[4,256,128]{2,1,0:T(8,128)(2,1)S(1)}, u32[]{:S(2)}, u32[]{:S(2)}) collective-permute-start(bf16[4,256,128]{2,1,0:T(8,128)(2,1)S(1)} %shard_map.105), channel_id=1, source_target_pairs={{0,16},{2,18},{4,20},{6,22},{8,24},{10,26},{12,28},{14,30},{16,0},... | collective-permute-start | bytes 786440 | tf_op jit(solution)/shard_map/ppermute | solution.py:25
  137.2 34.1 %collective-permute-start.34 = (bf16[4,256,128]{2,1,0:T(8,128)(2,1)S(1)}, bf16[4,256,128]{2,1,0:T(8,128)(2,1)S(1)}, u32[]{:S(2)}, u32[]{:S(2)}) collective-permute-start(bf16[4,256,128]{2,1,0:T(8,128)(2,1)S(1)} %shard_map.114), channel_id=1, source_target_pairs={{0,16},{2,18},{4,20},{6,22},{8,24},{10,26},{12,28},{14,30},{16,0},... | collective-permute-start | bytes 786440 | tf_op jit(solution)/shard_map/ppermute | solution.py:25
  141.9 34.9 %collective-permute-start.18 = (bf16[4,256,128]{2,1,0:T(8,128)(2,1)S(1)}, bf16[4,256,128]{2,1,0:T(8,128)(2,1)S(1)}, u32[]{:S(2)}, u32[]{:S(2)}) collective-permute-start(bf16[4,256,128]{2,1,0:T(8,128)(2,1)S(1)} %shard_map.97), channel_id=1, source_target_pairs={{0,16},{2,18},{4,20},{6,22},{8,24},{10,26},{12,28},{14,30},{16,0},... | collective-permute-start | bytes 786440 | tf_op jit(solution)/shard_map/ppermute | solution.py:25
  147.6 33.7 %collective-permute-start.10 = (bf16[4,256,128]{2,1,0:T(8,128)(2,1)S(1)}, bf16[4,256,128]{2,1,0:T(8,128)(2,1)S(1)}, u32[]{:S(2)}, u32[]{:S(2)}) collective-permute-start(bf16[4,256,128]{2,1,0:T(8,128)(2,1)S(1)} %shard_map.90), channel_id=1, source_target_pairs={{0,16},{2,18},{4,20},{6,22},{8,24},{10,26},{12,28},{14,30},{16,0},... | collective-permute-start | bytes 786440 | tf_op jit(solution)/shard_map/ppermute | solution.py:25
  151.2 14.4 %copy-start.2 = (bf16[1,1,4,256,256]{4,3,2,1,0:T(8,128)(2,1)S(1)}, bf16[1,1,4,256,256]{4,3,2,1,0:T(8,128)(2,1)}, u32[]{:S(2)}) copy-start(bf16[1,1,4,256,256]{4,3,2,1,0:T(8,128)(2,1)} %refs_2_.7) | copy-start | bytes 1572868
  151.2 14.4 %copy-start.3 = (bf16[1,1,4,256,256]{4,3,2,1,0:T(8,128)(2,1)S(1)}, bf16[1,1,4,256,256]{4,3,2,1,0:T(8,128)(2,1)}, u32[]{:S(2)}) copy-start(bf16[1,1,4,256,256]{4,3,2,1,0:T(8,128)(2,1)} %refs_3_.7) | copy-start | bytes 1572868
